TPU v7x, 512 devices: a whole 4x8x8 slice. The times are simulated.
512 devices in a mesh: chan: 128 (over z, y, core), orb: 4 (over x).
Axes of the slice: x: 4, y: 8, z: 8, core: 2. Of those that a mesh axis runs over, the one named last changes fastest.
Arguments:
- amplitudes: bfloat16 [327680, 1024], P(('chan', 'orb')), may hold values from -6 to 6
- recoupling: float32 [327680], P(('chan', 'orb')), may hold values from -1.5 to 1.5
- denominators: float32 [327680], P(('chan', 'orb')), may hold values from 1 to 8
- interaction: bfloat16 [512, 1024, 1024], P('chan', 'orb'), may hold values from -0.25 to 0.25
- pair_source: int32 [512, 1024], P('chan', 'orb'), may hold values from -1 to 639, as said below
- return_slot: int32 [327680], P(('chan', 'orb')), may hold values from 0 to 1023, as said below
- channel_sizes: int32 [512], P('chan'), may hold values from 256 to 1024, as said below
Outputs:
- updated: bfloat16 [327680, 1024], P(('chan', 'orb'))
Inputs may be any that keep to these rules, and one draw needn't show every extreme that they name: `channel_sizes`: every channel size is a multiple of 4; the 4 sizes of blocks c with the same c div 4 sum to 2560. pair_source[c, p] = -1 exactly where live[c, p] = 0. For each e and o, over the blocks c with c div 4 = e and the positions p with p div 256 = o, the other values name each number 0 to 639 once. return_slot[(e * 4 + o) * 640 + i] is the k with pair_source[e * 4 + k div 256, o * 256 + k mod 256] = i.
All inputs are finite; a program needn't handle non-finite values.
Results may differ from a plain program's by a relative error of at most 0.002.
Values may be sent and summed in bfloat16 or wider, within the bound.
No kernel may reach another device: no remote copies, remote signals or barrier semaphores. Data moves between devices by JAX's collectives and lax.ppermute only.
A program may use at most 64 MiB of HBM per device.

v0:
```python
import jax
import jax.numpy as jnp
from jax import lax
from jax.sharding import PartitionSpec as P


def shards(
    amplitudes, recoupling, denominators, interaction, pair_source, return_slot, channel_sizes
):
    chan_count = lax.axis_size("chan")
    orb_count = lax.axis_size("orb")
    row_count = amplitudes.shape[0]
    width = amplitudes.shape[1]
    per_peer = row_count // chan_count
    blocks_here = pair_source.shape[0]
    rows_block = pair_source.shape[1]
    relayed = (amplitudes.astype(jnp.float32) * recoupling[:, None]).astype(jnp.bfloat16)
    received = lax.all_to_all(
        relayed.reshape(chan_count, per_peer, width),
        "chan",
        split_axis=0,
        concat_axis=0,
        tiled=True,
    )
    received = received.reshape(row_count, width)
    flat_source = pair_source.reshape(-1)
    amp_rows = jnp.take(received, jnp.maximum(flat_source, 0), axis=0)
    position = jnp.arange(width, dtype=jnp.int32)
    pair_rank = orb_count * (position % rows_block) + position // rows_block
    live_mask = pair_rank[None, :] < channel_sizes[:, None]
    keep = (pair_source >= 0)[:, :, None] & live_mask[:, None, :]
    amp_block = jnp.where(
        keep, amp_rows.reshape(blocks_here, rows_block, width), jnp.zeros((), jnp.bfloat16)
    )
    cycle_local = jnp.einsum(
        "bik,bkj->bij",
        interaction,
        lax.all_gather(amp_block, "orb", axis=1, tiled=True),
        preferred_element_type=jnp.float32,
    ).astype(jnp.bfloat16)
    outgoing = jnp.take(cycle_local.reshape(blocks_here * rows_block, width), return_slot, axis=0)
    returned = lax.all_to_all(
        outgoing.reshape(chan_count, per_peer, width),
        "chan",
        split_axis=0,
        concat_axis=0,
        tiled=True,
    )
    returned = returned.reshape(row_count, width)
    updated = (
        amplitudes.astype(jnp.float32)
        + recoupling[:, None] * returned.astype(jnp.float32) / denominators[:, None]
    )
    return updated.astype(jnp.bfloat16)


def solution(mesh):
    in_specs = (
        P(("chan", "orb"), None),
        P(("chan", "orb")),
        P(("chan", "orb")),
        P("chan", "orb", None),
        P("chan", "orb"),
        P(("chan", "orb")),
        P("chan"),
    )
    out_specs = P(("chan", "orb"), None)
    return jax.shard_map(shards, mesh=mesh, in_specs=in_specs, out_specs=out_specs, check_vma=False)
```

profile of v0, /device:TPU:1, one launch (start us, length us, event | category | flops | bytes accessed | tf_op | source)
XLA Modules:
  0.0 271.4 jit_solution(17211001511739684204)
XLA Ops:
  6.5 0.0 copy-start
  6.5 1.7 fusion
  8.3 1.6 reshape.97
  9.9 0.0 copy-start.4
  9.9 0.0 copy-start.6
  9.9 19.0 %all-to-all-start = ((bf16[128,5,1024]{2,1,0:T(8,128)(2,1)}), bf16[128,5,1024]{2,1,0:T(8,128)(2,1)}, u32[]{:S(2)}, u32[]{:S(2)}) async-start(bf16[128,5,1024]{2,1,0:T(8,128)(2,1)} %reshape.97), calls=%async_computation | async-start | bytes 4194304 | tf_op jit(solution)/shard_map/all_to_all | solution.py:18
  28.9 0.0 all-gather.2.cloned.1.call-start
  28.9 0.0 copy-done.4
  29.0 0.0 copy-done.6
  29.0 0.1 broadcast_compare_fusion
  29.1 50.7 %all-to-all-done = bf16[128,5,1024]{2,1,0:T(8,128)(2,1)} async-done(((bf16[128,5,1024]{2,1,0:T(8,128)(2,1)}), bf16[128,5,1024]{2,1,0:T(8,128)(2,1)}, u32[]{:S(2)}, u32[]{:S(2)}) %all-to-all-start) | async-done | bytes 1310752 | tf_op jit(solution)/shard_map/all_to_all | solution.py:18
  79.8 2.6 reshape.98
  82.4 5.4 %gather_fusion = bf16[1024,1024]{1,0:T(8,128)(2,1)} fusion(bf16[640,1024]{1,0:T(8,128)(2,1)S(1)} %reshape.98, s32[1024]{0:T(1024)S(1)} %broadcast_clamp_fusion), kind=kCustom, calls=%fused_computation | custom fusion | bytes 4198400 | tf_op jit(solution)/shard_map/jit(_take)/gather | solution.py:27
  87.8 3.1 %and_select_fusion = bf16[4,256,1024]{2,1,0:T(8,128)(2,1)} fusion(bf16[4,256,1024]{2,1,0:T(8,128)(2,1)} %bitcast.10, pred[4,256]{1,0:T(4,128)(4,1)S(1)} %get-tuple-element.6, pred[4,1024]{1,0:T(4,128)(4,1)S(1)} %broadcast_compare_fusion, pred[4,256]{1,0:T(4,128)(4,1)S(1)} %get-tuple-element.5), kind=kLoop, calls=%fused_computation.2 | loop fusion | flops 3145728 | bytes 4200448 | tf_op jit(solution)/shard_map/jit(_where)/select_n | solution.py:32
  90.9 0.0 copy-start.3
  90.9 0.0 all-gather.2.cloned.1.call-update
  91.0 0.7 copy-done.3
  91.6 0.2 broadcast_in_dim.35
  91.9 83.3 %all-gather.2.cloned.1.call-done = bf16[4,1024,1024]{2,1,0:T(8,128)(2,1)} async-done(((bf16[4,256,1024]{2,1,0:T(8,128)(2,1)}), bf16[4,1024,1024]{2,1,0:T(8,128)(2,1)}) %all-gather.2.cloned.1.call-update) | async-done | bytes 8388624 | tf_op jit(solution)/shard_map/all_gather | solution.py:38
  175.2 0.0 copy-done
  175.2 7.1 %convolution_convert_fusion = bf16[4,1024,256]{1,2,0:T(8,128)(2,1)} fusion(bf16[4,256,1024]{2,1,0:T(8,128)(2,1)S(1)} %copy-done, bf16[4,1024,1024]{2,1,0:T(8,128)(2,1)} %all-gather.2.cloned.1.call-done), kind=kOutput, calls=%fused_computation.8 | convolution fusion | flops 2148532224 | bytes 12582912 | tf_op jit(solution)/shard_map/bik,bkj->bij/dot_general | solution.py:35
  182.3 5.7 %gather_fusion.1 = bf16[640,1024]{1,0:T(8,128)(2,1)S(1)} fusion(bf16[1024,1024]{1,0:T(8,128)(2,1)} %bitcast.9, s32[1024]{0:T(1024)S(1)} %pad_clamp_fusion), kind=kCustom, calls=%fused_computation.1 | custom fusion | bytes 2624000 | tf_op jit(solution)/shard_map/jit(_take)/gather | solution.py:41
  188.0 1.6 gather.15
  189.6 1.9 broadcast_select_fusion
  191.5 65.6 %all_to_all.10 = bf16[128,5,1024]{2,1,0:T(8,128)(2,1)} all-to-all(bf16[128,5,1024]{2,1,0:T(8,128)(2,1)S(1)} %broadcast_select_fusion), channel_id=1, replica_groups=mesh['chan'=128,'orb'=4] {'chan'}, dimensions={0} | all-to-all | bytes 2621440 | tf_op jit(solution)/shard_map/all_to_all | solution.py:42
  257.2 0.0 copy-start.1
  257.2 0.0 copy-start.2
  257.2 0.0 copy-start.5
  257.2 4.1 %reshape.100 = f32[640,1024]{1,0:T(8,128)} reshape(bf16[128,5,1024]{2,1,0:T(8,128)(2,1)} %all_to_all.10) | data formatting | bytes 3932160 | tf_op jit(solution)/shard_map/convert_element_type | solution.py:52
  261.2 0.0 copy-done.1
  261.3 0.0 copy-done.2
  261.3 0.0 copy-done.5
  261.3 3.3 %fusion.1 = bf16[640,1024]{1,0:T(8,128)(2,1)} fusion(bf16[640,1024]{1,0:T(8,128)(2,1)S(1)} %copy-done.1, f32[640,1024]{1,0:T(8,128)} %reshape.100, f32[640]{0:T(1024)S(1)} %copy-done.5, f32[640]{0:T(1024)S(1)} %copy-done.2), kind=kLoop, calls=%fused_computation.6 | loop fusion | flops 3276800 | bytes 5248000 | tf_op jit(solution)/shard_map/convert_element_type | solution.py:54
  (8 shorter events, 0.0 us)
Async XLA Ops:
  6.5 168.7 %copy-start = (bf16[4,256,1024]{2,1,0:T(8,128)(2,1)S(1)}, bf16[4,256,1024]{2,1,0:T(8,128)(2,1)}, u32[]{:S(2)}) copy-start(bf16[4,256,1024]{2,1,0:T(8,128)(2,1)} %param.10) | copy-start | bytes 6291460
  9.9 19.1 %copy-start.4 = (s32[4,256]{1,0:T(4,128)S(1)}, s32[4,256]{1,0:T(4,128)}, u32[]{:S(2)}) copy-start(s32[4,256]{1,0:T(4,128)} %param.11) | copy-start | bytes 12292
  9.9 19.1 %copy-start.6 = (s32[4]{0:T(128)S(1)}, s32[4]{0:T(128)}, u32[]{:S(2)}) copy-start(s32[4]{0:T(128)} %param.13) | copy-start | bytes 52
  9.9 69.9 %all-to-all-start = ((bf16[128,5,1024]{2,1,0:T(8,128)(2,1)}), bf16[128,5,1024]{2,1,0:T(8,128)(2,1)}, u32[]{:S(2)}, u32[]{:S(2)}) async-start(bf16[128,5,1024]{2,1,0:T(8,128)(2,1)} %reshape.97), calls=%async_computation | async-start | bytes 4194304 | tf_op jit(solution)/shard_map/all_to_all | solution.py:18
  28.9 146.3 %all-gather.2.cloned.1.call-start = ((), (), s32[]{:S(2)}) async-start(), calls=%async_computation.2 | async-start | bytes 10485760 | tf_op jit(solution)/shard_map/all_gather | solution.py:38
  90.9 0.7 copy-start.3
  257.2 4.1 %copy-start.1 = (bf16[640,1024]{1,0:T(8,128)(2,1)S(1)}, bf16[640,1024]{1,0:T(8,128)(2,1)}, u32[]{:S(2)}) copy-start(bf16[640,1024]{1,0:T(8,128)(2,1)} %param.7) | copy-start | bytes 3932164
  257.2 4.1 %copy-start.2 = (f32[640]{0:T(1024)S(1)}, f32[640]{0:T(1024)}, u32[]{:S(2)}) copy-start(f32[640]{0:T(1024)} %param.8) | copy-start | bytes 7684
  257.2 4.1 %copy-start.5 = (f32[640]{0:T(1024)S(1)}, f32[640]{0:T(1024)}, u32[]{:S(2)}) copy-start(f32[640]{0:T(1024)} %param.9) | copy-start | bytes 7684
Sparse Core Ops, SparseCore 0:
  91.1 84.0 all-gather.1
where the time goes:
time: 274 us; the launch traced here: 271 us
  waiting for transfers between devices  134 us (49%)
  blocking collectives  65.6 us (24%)
  local copies, waits for them, and re-layouts  21.9 us (8%)
  starting transfers between devices  19 us (7%)
  between operations  13.5 us (5%)
  other arithmetic  10.1 us (4%)
  matrix products  7.09 us (3%)
    all_gather x1, waiting for transfers between devices, shards(): lax.all_gather(amp_block, 'orb', axis=1, tiled=True)  83.3 us
    all_to_all x1, blocking collectives, shards(): lax.all_to_all(outgoing.reshape(chan_count, per_peer, width), 'chan', spl...  65.6 us
    all_to_all x1, waiting for transfers between devices, shards(): lax.all_to_all(relayed.reshape(chan_count, per_peer, width), 'chan', spli...  50.7 us
    all_to_all x1, starting transfers between devices, shards(): lax.all_to_all(relayed.reshape(chan_count, per_peer, width), 'chan', spli...  19 us
    gather x2, local copies, waits for them, and re-layouts, shards(): jnp.take(cycle_local.reshape(blocks_here * rows_block, width), return_slo...  7.34 us
    dot_general x1, matrix products, shards(): jnp.einsum('bik,bkj->bij', interaction, lax.all_gather(amp_block, 'orb',...  7.09 us
  transfers between devices with their start and end apart: 2, of which 2 were waited for; matrix products, arithmetic and copies ran while one was open for 0% of the time, Pallas kernels for 0%

commit v1 on v0

v1 whole, which is shorter than its diff:
```python
import jax
import jax.numpy as jnp
from jax import lax
from jax.sharding import PartitionSpec as P

BOTH = ("chan", "orb")


def shards(
    amplitudes, recoupling, denominators, interaction, pair_source, return_slot, channel_sizes
):
    chan_count = lax.axis_size("chan")
    orb_count = lax.axis_size("orb")
    row_count, width = amplitudes.shape
    quota = row_count // chan_count
    blocks_here, rows_block = pair_source.shape
    halves = rows_block // 128
    peers = chan_count * orb_count
    bf = jnp.bfloat16

    def shift(x, by):
        return lax.ppermute(x, "orb", [(i, (i + by) % orb_count) for i in range(orb_count)])

    rows = jnp.take(interaction.reshape(blocks_here * rows_block, width), return_slot, axis=0)
    block_of = (return_slot // rows_block).astype(bf)
    slot_of = (return_slot % rows_block).astype(bf)
    tags = jnp.zeros((16, width), bf).at[0, :row_count].set(block_of).at[1, :row_count].set(slot_of)
    packed = jnp.concatenate([rows, tags], axis=0)
    half = packed.shape[0] // 2
    after = shift(packed, -1)
    before = shift(packed, 1)
    across = jnp.concatenate([shift(after[:half], -1), shift(before[half:], 1)], axis=0)

    relayed = (amplitudes.astype(jnp.float32) * recoupling[:, None]).astype(bf)
    outgoing = relayed.reshape(chan_count, quota, orb_count, halves, 128).transpose(0, 2, 1, 3, 4)
    received = lax.all_to_all(
        outgoing.reshape(peers, quota, halves, 128), BOTH, split_axis=0, concat_axis=0, tiled=True
    )

    stack = jnp.stack([packed, after, across, before])
    block_at = stack[:, row_count, :row_count]
    slot_at = stack[:, row_count + 1, :row_count]
    weights = stack[:, :row_count]
    here = lax.axis_index("orb")
    order = (jnp.arange(orb_count) - here) % orb_count
    block_at = block_at[order]
    slot_at = slot_at[order]
    weights = weights[order]
    pick = (jnp.arange(rows_block, dtype=jnp.int32).astype(bf)[None, :, None] == slot_at[:, None, :]).astype(bf)
    spread = jnp.einsum(
        "arok,oki->aroi",
        weights.reshape(orb_count, row_count, orb_count, rows_block),
        pick,
        preferred_element_type=jnp.float32,
    ).astype(bf)
    mixing = jnp.where(
        block_at[:, :, None, None] == block_at[None, None, :, :], spread, jnp.zeros((), bf)
    )
    sizes = channel_sizes // orb_count
    size_at = jnp.sum(
        jnp.where(
            block_at[:, :, None].astype(jnp.int32) == jnp.arange(blocks_here, dtype=jnp.int32),
            sizes,
            0,
        ),
        axis=2,
    )
    live = jnp.arange(rows_block, dtype=jnp.int32)[None, None, :] < size_at[:, :, None]

    block = received.reshape(chan_count, orb_count, quota, rows_block).transpose(1, 0, 2, 3)
    block = block.reshape(orb_count, row_count, rows_block)
    block = jnp.where(live, block, jnp.zeros((), bf))
    cycle = jnp.einsum("aroi,oik->ark", mixing, block, preferred_element_type=jnp.float32).astype(bf)
    back = cycle.reshape(orb_count, chan_count, quota, halves, 128).transpose(1, 0, 2, 3, 4)
    returned = lax.all_to_all(
        back.reshape(peers, quota, halves, 128), BOTH, split_axis=0, concat_axis=0, tiled=True
    )
    returned = returned.reshape(chan_count, orb_count, quota, halves, 128).transpose(0, 2, 1, 3, 4)
    returned = returned.reshape(row_count, width)
    updated = (
        amplitudes.astype(jnp.float32)
        + recoupling[:, None] * returned.astype(jnp.float32) / denominators[:, None]
    )
    return updated.astype(bf)


def solution(mesh):
    in_specs = (
        P(("chan", "orb"), None),
        P(("chan", "orb")),
        P(("chan", "orb")),
        P("chan", "orb", None),
        P("chan", "orb"),
        P(("chan", "orb")),
        P("chan"),
    )
    out_specs = P(("chan", "orb"), None)
    return jax.shard_map(shards, mesh=mesh, in_specs=in_specs, out_specs=out_specs, check_vma=False)
```

time: 274 us -> 191 us (0.70)
  waiting for transfers between devices: 134 us -> 23.4 us
  local copies, waits for them, and re-layouts: 21.9 us -> 43.2 us
  starting transfers between devices: 19 us -> 36.3 us
  between operations: 13.5 us -> 0.28 us
  blocking collectives: 65.6 us -> 55.1 us
  other arithmetic: 10.1 us -> 20.5 us
  matrix products: 7.09 us -> 11.6 us
    all_gather x1 -> x0, waiting for transfers between devices: 83.3 us -> none  [shards(): lax.all_gather(amp_block, 'orb', axis=1, tiled=True)]
    all_to_all x1, waiting for transfers between devices: 50.7 us -> 0.01 us  [shards(): lax.all_to_all(outgoing.reshape(peers, quota, halves, 128), BOTH, split_a...]
    ppermute x0 -> x4, waiting for transfers between devices: none -> 23.4 us  [shift(): lax.ppermute(x, 'orb', [(i, (i + by) % orb_count) for i in range(orb_coun...]
    ppermute x0 -> x4, starting transfers between devices: none -> 13.6 us  [shift(): lax.ppermute(x, 'orb', [(i, (i + by) % orb_count) for i in range(orb_coun...]
    reshape x2 -> x7, local copies, waits for them, and re-layouts: 4.21 us -> 15.5 us  [the longest x2 6.08 us: shards(): relayed.reshape(chan_count, quota, orb_count, halves, 128)]
    another operation x0 -> x3, other arithmetic: none -> 10.8 us  [shards(): stack = jnp.stack([packed, after, across, before])]
    all_to_all x1, blocking collectives: 65.6 us -> 55.1 us  [shards(): lax.all_to_all(back.reshape(peers, quota, halves, 128), BOTH, split_axis=...]
    dot_general x1, matrix products: 7.09 us -> 11.6 us  [shards(): jnp.einsum('aroi,oik->ark', mixing, block, preferred_element_type=jnp.flo...]
  transfers between devices with their start and end apart: 2 -> 5, of which waited for: 2 -> 2; matrix products, arithmetic and copies ran while one was open for 0% -> 16% of each run, Pallas kernels for 0% -> 0%
where the time goes in v1:
time: 191 us; the launch traced here: 190 us
  blocking collectives  55.1 us (29%)
  local copies, waits for them, and re-layouts  43.2 us (23%)
  starting transfers between devices  36.3 us (19%)
  waiting for transfers between devices  23.4 us (12%)
  other arithmetic  20.5 us (11%)
  matrix products  11.6 us (6%)
    all_to_all x1, blocking collectives, shards(): lax.all_to_all(back.reshape(peers, quota, halves, 128), BOTH, split_axis=...  55.1 us
    ppermute x4, waiting for transfers between devices, shift(): lax.ppermute(x, 'orb', [(i, (i + by) % orb_count) for i in range(orb_coun...  23.4 us
    all_to_all x1, starting transfers between devices, shards(): lax.all_to_all(outgoing.reshape(peers, quota, halves, 128), BOTH, split_a...  22.7 us
    ppermute x4, starting transfers between devices, shift(): lax.ppermute(x, 'orb', [(i, (i + by) % orb_count) for i in range(orb_coun...  13.6 us
    dot_general x1, matrix products, shards(): jnp.einsum('aroi,oik->ark', mixing, block, preferred_element_type=jnp.flo...  11.6 us
    another operation x3, other arithmetic, shards(): stack = jnp.stack([packed, after, across, before])  10.8 us
    convert_element_type x2, local copies, waits for them, and re-layouts, shards(): returned.astype(jnp.float32)  8.36 us
    reshape x2, local copies, waits for them, and re-layouts, shards(): relayed.reshape(chan_count, quota, orb_count, halves, 128)  6.08 us
  transfers between devices with their start and end apart: 5, of which 2 were waited for; matrix products, arithmetic and copies ran while one was open for 16% of the time, Pallas kernels for 0%

profile of v1, /device:TPU:1, one launch (start us, length us, event | category | flops | bytes accessed | tf_op | source)
XLA Modules:
  0.0 190.4 jit_solution(2705073392497884068)
XLA Ops:
  0.0 0.8 add_select_fusion.2
  0.9 0.7 compare_and_fusion
  1.6 0.0 copy-done
  1.6 2.8 %gather_fusion = bf16[640,1024]{1,0:T(8,128)(2,1)S(1)} fusion(bf16[1024,1024]{1,0:T(8,128)(2,1)S(1)} %bitcast.54, s32[1024]{0:T(1024)S(1)} %pad_clamp_fusion.1), kind=kCustom, calls=%fused_computation | custom fusion | bytes 2624000 | tf_op jit(solution)/shard_map/jit(_take)/gather | solution.py:24
  4.4 1.2 broadcast_select_fusion
  5.7 0.1 scatter.9
  5.8 0.0 copy-start.2
  5.9 0.0 copy-start.5
  5.9 2.8 %fusion.36 = (bf16[1,656,1024]{2,1,0:T(8,128)(2,1)S(1)}, bf16[656,1024]{1,0:T(8,128)(2,1)}) fusion(bf16[16,1024]{1,0:T(8,128)(2,1)S(1)} %scatter.9, bf16[640,1024]{1,0:T(8,128)(2,1)} %broadcast_select_fusion), kind=kLoop, calls=%fused_computation.66 | loop fusion | flops 2686976 | bytes 4030464 | tf_op jit(solution)/shard_map/stack | solution.py:40
  8.7 3.9 %collective-permute-start.2 = (bf16[656,1024]{1,0:T(8,128)(2,1)}, bf16[656,1024]{1,0:T(8,128)(2,1)}, u32[]{:S(2)}, u32[]{:S(2)}) collective-permute-start(bf16[656,1024]{1,0:T(8,128)(2,1)} %get-tuple-element.32), channel_id=1, source_target_pairs={{0,1},{1,2},{2,3},{3,0},{4,5},{5,6},{6,7},{7,4},{8,9},{9,10},{10,1... | collective-permute-start | bytes 4030472 | tf_op jit(solution)/shard_map/ppermute | solution.py:22
  12.7 3.2 %collective-permute-start = (bf16[656,1024]{1,0:T(8,128)(2,1)}, bf16[656,1024]{1,0:T(8,128)(2,1)}, u32[]{:S(2)}, u32[]{:S(2)}) collective-permute-start(bf16[656,1024]{1,0:T(8,128)(2,1)} %get-tuple-element.32), channel_id=1, source_target_pairs={{0,3},{1,0},{2,1},{3,2},{4,7},{5,4},{6,5},{7,6},{8,11},{9,8},{10,9... | collective-permute-start | bytes 4030472 | tf_op jit(solution)/shard_map/ppermute | solution.py:22
  15.9 1.3 fusion.12
  17.2 4.4 %reshape.161 = bf16[128,5,4,2,128]{4,3,2,1,0:T(2,128)(2,1)} reshape(bf16[640,1024]{1,0:T(8,128)(2,1)} %fusion.12) | data formatting | bytes 2621440 | tf_op jit(solution)/shard_map/reshape | solution.py:35
  21.6 1.7 copy.33
  23.3 2.4 %copy.34 = bf16[512,5,2,128]{3,2,1,0:T(2,128)(2,1)} copy(bf16[512,5,2,128]{3,0,2,1:T(8,128)(2,1)S(1)} %bitcast.55) | data formatting | bytes 2621440 | tf_op jit(solution)/shard_map/reshape | solution.py:37
  25.7 22.7 %all-to-all-start = ((bf16[512,5,2,128]{3,2,1,0:T(2,128)(2,1)}), bf16[512,5,2,128]{3,2,1,0:T(2,128)(2,1)}, u32[]{:S(2)}, u32[]{:S(2)}) async-start(bf16[512,5,2,128]{3,2,1,0:T(2,128)(2,1)} %copy.34), calls=%async_computation | async-start | bytes 2621440 | tf_op jit(solution)/shard_map/all_to_all | solution.py:36
  48.4 0.0 copy-start.7
  48.4 2.1 %slice.64 = bf16[328,1024]{1,0:T(8,128)(2,1)} slice(bf16[656,1024]{1,0:T(8,128)(2,1)} %collective-permute-done.2), slice={[328:656], [0:1024]} | slice | bytes 1343488 | tf_op jit(solution)/shard_map/slice | solution.py:32
  50.5 3.2 %collective-permute-start.3 = (bf16[328,1024]{1,0:T(8,128)(2,1)}, bf16[328,1024]{1,0:T(8,128)(2,1)}, u32[]{:S(2)}, u32[]{:S(2)}) collective-permute-start(bf16[328,1024]{1,0:T(8,128)(2,1)} %slice.64), channel_id=1, source_target_pairs={{0,1},{1,2},{2,3},{3,0},{4,5},{5,6},{6,7},{7,4},{8,9},{9,10},{10,1... | collective-permute-start | bytes 2015240 | tf_op jit(solution)/shard_map/ppermute | solution.py:22
  53.7 0.0 collective-permute-done
  53.7 2.0 %slice.63 = bf16[328,1024]{1,0:T(8,128)(2,1)} slice(bf16[656,1024]{1,0:T(8,128)(2,1)} %collective-permute-done), slice={[0:328], [0:1024]} | slice | bytes 1343488 | tf_op jit(solution)/shard_map/slice | solution.py:32
  55.7 3.2 %collective-permute-start.1 = (bf16[328,1024]{1,0:T(8,128)(2,1)}, bf16[328,1024]{1,0:T(8,128)(2,1)}, u32[]{:S(2)}, u32[]{:S(2)}) collective-permute-start(bf16[328,1024]{1,0:T(8,128)(2,1)} %slice.63), channel_id=1, source_target_pairs={{0,3},{1,0},{2,1},{3,2},{4,7},{5,4},{6,5},{7,6},{8,11},{9,8},{10,9... | collective-permute-start | bytes 2015240 | tf_op jit(solution)/shard_map/ppermute | solution.py:22
  59.0 20.3 %collective-permute-done.3 = bf16[328,1024]{1,0:T(8,128)(2,1)} collective-permute-done((bf16[328,1024]{1,0:T(8,128)(2,1)}, bf16[328,1024]{1,0:T(8,128)(2,1)}, u32[]{:S(2)}, u32[]{:S(2)}) %collective-permute-start.3) | collective-permute-done | bytes 671776 | tf_op jit(solution)/shard_map/ppermute | solution.py:22
  79.3 3.2 %collective-permute-done.1 = bf16[328,1024]{1,0:T(8,128)(2,1)} collective-permute-done((bf16[328,1024]{1,0:T(8,128)(2,1)}, bf16[328,1024]{1,0:T(8,128)(2,1)}, u32[]{:S(2)}, u32[]{:S(2)}) %collective-permute-start.1) | collective-permute-done | bytes 671776 | tf_op jit(solution)/shard_map/ppermute | solution.py:22
  82.5 1.4 maximum_bitcast_fusion
  83.9 0.9 pad_maximum_fusion.4
  84.8 0.2 copy-done.1
  85.0 0.6 gather_fusion.1
  85.6 6.5 %pad_maximum_fusion = bf16[4,640,1024]{2,1,0:T(8,128)(2,1)} fusion(bf16[1,656,1024]{2,1,0:T(8,128)(2,1)} %bitcast.4, bf16[1,656,1024]{2,1,0:T(8,128)(2,1)} %copy-done.1, bf16[1,656,1024]{2,1,0:T(8,128)(2,1)} %bitcast.2, bf16[1,656,1024]{2,1,0:T(8,128)(2,1)S(1)} %get-tuple-element.31), kind=kLoop, calls=%fused_computation.14 | loop fusion | flops 20971520 | bytes 10616832 | tf_op jit(solution)/shard_map/stack | solution.py:40
  92.1 5.7 %gather_fusion.3 = bf16[4,640,1024]{2,1,0:T(8,128)(2,1)} fusion(bf16[4,640,1024]{2,1,0:T(8,128)(2,1)} %pad_maximum_fusion, s32[1024]{0:T(1024)S(1)} %pad_clamp_fusion), kind=kCustom, calls=%fused_computation.3 | custom fusion | bytes 10485776 | tf_op jit(solution)/shard_map/gather | solution.py:48
  97.8 0.1 select_reduce_fusion
  97.9 0.9 copy.32
  98.9 0.6 gather_fusion.2
  99.4 0.0 all-to-all-done
  99.4 2.2 %copy.35 = bf16[512,5,2,128]{3,2,0,1:T(2,128)(2,1)S(1)} copy(bf16[512,5,2,128]{3,2,1,0:T(2,128)(2,1)} %all-to-all-done) | data formatting | bytes 2621440 | tf_op jit(solution)/shard_map/all_to_all | solution.py:36
  101.6 1.7 reshape.163
  103.3 1.8 copy.36
  105.2 1.0 fusion.14
  106.2 11.6 %bitcast_convert_fusion = bf16[4,640,256]{2,1,0:T(8,128)(2,1)} fusion(bf16[4,640]{1,0:T(4,128)(2,1)S(1)} %gather_fusion.1, bf16[4,80,4,8,256]{4,3,2,1,0:T(8,128)(2,1)} %bitcast.58, bf16[4,640,256]{2,0,1:T(4,128)(2,1)S(1)} %fusion.14, bf16[4,640]{1,0:T(4,128)(2,1)S(1)} %gather_fusion.2, bf16[256]{0:T(256)(128)(2,1)S(1)} %iota_convert_fusion), kind=kOutput, calls=%fused_computation.22 | convolution fusion | flops 6733168640 | bytes 7875072 | tf_op jit(solution)/shard_map/aroi,oik->ark/dot_general | solution.py:73
  117.9 2.9 %reshape.165 = bf16[4,128,5,2,128]{4,3,2,1,0:T(2,128)(2,1)S(1)} reshape(bf16[4,640,256]{2,1,0:T(8,128)(2,1)} %bitcast_convert_fusion) | data formatting | bytes 2621440 | tf_op jit(solution)/shard_map/reshape | solution.py:74
  120.8 1.0 copy.39
  121.8 1.3 copy.40
  123.2 55.1 %all_to_all.10 = bf16[512,5,2,128]{3,2,1,0:T(2,128)(2,1)S(1)} all-to-all(bf16[512,5,2,128]{3,2,1,0:T(2,128)(2,1)S(1)} %copy.40), channel_id=1, replica_groups=mesh['chan'=128,'orb'=4] {'chan','orb'}, dimensions={0} | all-to-all | bytes 2621440 | tf_op jit(solution)/shard_map/all_to_all | solution.py:75
  178.3 0.2 copy.41
  178.5 0.2 convert_bitcast_fusion
  178.7 3.5 %copy.42 = f32[128,5,4,2,128]{4,3,2,1,0:T(2,128)} copy(f32[128,5,4,2,128]{4,2,0,3,1:T(4,128)S(1)} %convert_bitcast_fusion) | data formatting | bytes 5242880 | tf_op jit(solution)/shard_map/convert_element_type | solution.py:82
  182.3 4.8 %reshape.167 = f32[640,1024]{1,0:T(8,128)} reshape(f32[128,5,4,2,128]{4,3,2,1,0:T(2,128)} %copy.42) | data formatting | bytes 5242880 | tf_op jit(solution)/shard_map/convert_element_type | solution.py:82
  187.1 3.3 %fusion.13 = bf16[640,1024]{1,0:T(8,128)(2,1)} fusion(bf16[640,1024]{1,0:T(8,128)(2,1)S(1)} %copy-done.3, f32[640,1024]{1,0:T(8,128)} %reshape.167, f32[640]{0:T(1024)S(1)} %copy-done.6, f32[640]{0:T(1024)S(1)} %copy-done.5), kind=kLoop, calls=%fused_computation.20 | loop fusion | flops 3276800 | bytes 5248000 | tf_op jit(solution)/shard_map/convert_element_type | solution.py:84
  (22 shorter events, 0.1 us)
Async XLA Ops:
  0.0 1.6 copy-start
  5.8 10.0 %copy-start.2 = (bf16[640,1024]{1,0:T(8,128)(2,1)S(1)}, bf16[640,1024]{1,0:T(8,128)(2,1)}, u32[]{:S(2)}) copy-start(bf16[640,1024]{1,0:T(8,128)(2,1)} %param.11) | copy-start | bytes 3932164
  5.9 10.0 %copy-start.5 = (f32[640]{0:T(1024)S(1)}, f32[640]{0:T(1024)}, u32[]{:S(2)}) copy-start(f32[640]{0:T(1024)} %param.12) | copy-start | bytes 7684
  8.7 39.7 %collective-permute-start.2 = (bf16[656,1024]{1,0:T(8,128)(2,1)}, bf16[656,1024]{1,0:T(8,128)(2,1)}, u32[]{:S(2)}, u32[]{:S(2)}) collective-permute-start(bf16[656,1024]{1,0:T(8,128)(2,1)} %get-tuple-element.32), channel_id=1, source_target_pairs={{0,1},{1,2},{2,3},{3,0},{4,5},{5,6},{6,7},{7,4},{8,9},{9,10},{10,1... | collective-permute-start | bytes 4030472 | tf_op jit(solution)/shard_map/ppermute | solution.py:22
  12.7 41.1 %collective-permute-start = (bf16[656,1024]{1,0:T(8,128)(2,1)}, bf16[656,1024]{1,0:T(8,128)(2,1)}, u32[]{:S(2)}, u32[]{:S(2)}) collective-permute-start(bf16[656,1024]{1,0:T(8,128)(2,1)} %get-tuple-element.32), channel_id=1, source_target_pairs={{0,3},{1,0},{2,1},{3,2},{4,7},{5,4},{6,5},{7,6},{8,11},{9,8},{10,9... | collective-permute-start | bytes 4030472 | tf_op jit(solution)/shard_map/ppermute | solution.py:22
  25.7 73.7 %all-to-all-start = ((bf16[512,5,2,128]{3,2,1,0:T(2,128)(2,1)}), bf16[512,5,2,128]{3,2,1,0:T(2,128)(2,1)}, u32[]{:S(2)}, u32[]{:S(2)}) async-start(bf16[512,5,2,128]{3,2,1,0:T(2,128)(2,1)} %copy.34), calls=%async_computation | async-start | bytes 2621440 | tf_op jit(solution)/shard_map/all_to_all | solution.py:36
  48.4 10.6 %copy-start.7 = (s32[4]{0:T(128)S(1)}, s32[4]{0:T(128)}, u32[]{:S(2)}) copy-start(s32[4]{0:T(128)} %param.16) | copy-start | bytes 52
  50.5 28.8 %collective-permute-start.3 = (bf16[328,1024]{1,0:T(8,128)(2,1)}, bf16[328,1024]{1,0:T(8,128)(2,1)}, u32[]{:S(2)}, u32[]{:S(2)}) collective-permute-start(bf16[328,1024]{1,0:T(8,128)(2,1)} %slice.64), channel_id=1, source_target_pairs={{0,1},{1,2},{2,3},{3,0},{4,5},{5,6},{6,7},{7,4},{8,9},{9,10},{10,1... | collective-permute-start | bytes 2015240 | tf_op jit(solution)/shard_map/ppermute | solution.py:22
  55.7 26.7 %collective-permute-start.1 = (bf16[328,1024]{1,0:T(8,128)(2,1)}, bf16[328,1024]{1,0:T(8,128)(2,1)}, u32[]{:S(2)}, u32[]{:S(2)}) collective-permute-start(bf16[328,1024]{1,0:T(8,128)(2,1)} %slice.63), channel_id=1, source_target_pairs={{0,3},{1,0},{2,1},{3,2},{4,7},{5,4},{6,5},{7,6},{8,11},{9,8},{10,9... | collective-permute-start | bytes 2015240 | tf_op jit(solution)/shard_map/ppermute | solution.py:22
  83.9 1.2 copy-start.1
  103.3 1.8 copy-start.4
  182.3 4.8 %copy-start.3 = (bf16[640,1024]{1,0:T(8,128)(2,1)S(1)}, bf16[640,1024]{1,0:T(8,128)(2,1)}, u32[]{:S(2)}) copy-start(bf16[640,1024]{1,0:T(8,128)(2,1)} %param.11) | copy-start | bytes 3932164
  182.3 4.8 %copy-start.6 = (f32[640]{0:T(1024)S(1)}, f32[640]{0:T(1024)}, u32[]{:S(2)}) copy-start(f32[640]{0:T(1024)} %param.13) | copy-start | bytes 7684

commit v2 on v0

v2 whole, which is shorter than its diff:
```python
import functools

import jax
import jax.numpy as jnp
from jax import lax
from jax.experimental import pallas as pl
from jax.experimental.pallas import tpu as pltpu
from jax.sharding import PartitionSpec as P


BOTH = ("chan", "orb")
LANES = 128
TAGS = 16
BF = jnp.bfloat16
F32 = jnp.float32
VMEM_BYTES = 56 * 1024 * 1024


def call(body, out_shape, in_specs, scratch=(), **kw):
    return pl.pallas_call(
        body,
        out_shape=out_shape,
        in_specs=in_specs,
        out_specs=jax.tree.map(lambda _: pl.BlockSpec(memory_space=pltpu.VMEM), out_shape),
        scratch_shapes=list(scratch),
        compiler_params=pltpu.CompilerParams(vmem_limit_bytes=VMEM_BYTES),
        **kw,
    )


VM = pl.BlockSpec(memory_space=pltpu.VMEM)
SM = pl.BlockSpec(memory_space=pltpu.SMEM)
ANY = pl.BlockSpec(memory_space=pl.ANY)


def one_hot(hit):
    return jnp.where(hit, 1.0, 0.0).astype(BF)


def column(rows):
    r, n = rows.shape
    tall = jnp.concatenate([rows, jnp.zeros((LANES - r, n), F32)], axis=0)
    return jnp.transpose(tall)


def pick_body(quota, src_ref, w_ref, out_ref):
    blocks, rows_block = src_ref.shape
    width = w_ref.shape[1]
    states = blocks * rows_block
    src = jnp.concatenate([src_ref[c : c + 1, :] for c in range(blocks)], axis=1)
    sender = (src * 205) >> 10
    place = jnp.where(src >= 0, (src - sender * quota) * LANES + sender, -1)
    lane = lax.broadcasted_iota(jnp.int32, (TAGS, states), 1)
    which = lax.broadcasted_iota(jnp.int32, (TAGS, states), 0)
    labels = jnp.where(which == 0, lane // rows_block, jnp.where(which == 1, lane % rows_block, 0))
    labels = labels.astype(F32).astype(BF)
    count = quota * LANES
    out_ref[count:, count:] = jnp.zeros((TAGS, width - count), BF)
    for q in range(quota):
        at = lax.broadcasted_iota(jnp.int32, (LANES, states), 0) + q * LANES
        hit = one_hot(at == place)
        here = slice(q * LANES, (q + 1) * LANES)
        out_ref[here, :] = jnp.dot(hit, w_ref[...], preferred_element_type=F32).astype(BF)
        out_ref[count:, here] = lax.dot_general(
            labels, hit, (((1,), (1,)), ((), ())), preferred_element_type=F32
        ).astype(BF)


def pack_body(orbs, quota, amp_ref, rec_ref, out_ref, tile_ref, flat_ref):
    tiles = amp_ref.shape[1] // LANES
    halves = tiles // orbs
    scale = column(rec_ref[...])
    for a in range(quota):
        rows = slice(a * LANES, (a + 1) * LANES)
        by = scale[:, a : a + 1]
        for t in range(tiles):
            tile_ref[t, rows, :] = amp_ref[rows, t * LANES : (t + 1) * LANES].astype(F32) * by
    for o in range(orbs):
        for q in range(quota):
            for h in range(halves):
                piece = tile_ref[o * halves + h, pl.ds(q, LANES, stride=quota), :]
                at = (o * quota + q) * halves + h
                flat_ref[pl.ds(at, LANES, stride=orbs * quota * halves), :] = piece
    out_ref[...] = flat_ref[...].astype(BF)


def mix_rows(w, owner, tags_ref, here, put):
    orbs = tags_ref.shape[0]
    for o in range(orbs):
        tag = tags_ref[(o + orbs - here) % orbs]
        part = w(o)
        slot = lax.broadcasted_iota(jnp.int32, (part.shape[1], tag.shape[1]), 0).astype(F32)
        spread = jnp.dot(part, one_hot(slot == tag[1:2, :]), preferred_element_type=F32)
        put(o, jnp.where(owner == tag[0:1, :], spread, 0.0).astype(BF))


def build_body(quota, here_ref, own_ref, after_ref, before_ref, far_ref, m0, m1, m3, tags_out, tags_ref):
    count = quota * LANES
    rows_block = own_ref.shape[1] // 4
    refs = (own_ref, after_ref, None, before_ref)
    for s, ref in enumerate(refs):
        tag = far_ref[:, :count] if ref is None else ref[count:, :count]
        tags_ref[s] = tag.astype(F32)
        tags_out[s] = tag.astype(F32)
    here = here_ref[0]
    for s, out in ((0, m0), (1, m1), (3, m3)):
        owner = column(tags_ref[s])[:, 0:1]
        ref = refs[s]

        def put(o, value, out=out):
            out[:, o * count : (o + 1) * count] = value

        mix_rows(
            lambda o, ref=ref: ref[:count, o * rows_block : (o + 1) * rows_block],
            owner, tags_ref, here, put,
        )


def cycle_body(
    quota, here_ref, size_ref, raw_ref, lo_ref, hi_ref, tags_ref, m0, m1, m3, out_ref,
    flat_ref, block_ref, mix_ref, far_ref, sem,
):
    orbs = tags_ref.shape[0]
    count = quota * LANES
    halves = 2
    rows_block = halves * LANES
    copies = []
    for i, (s, src) in enumerate(((0, m0), (1, m1), (3, m3))):
        cp = pltpu.make_async_copy(src, mix_ref.at[s], sem.at[i])
        cp.start()
        copies.append((s, cp))
    here = here_ref[0]
    half = count // 2
    far_ref[:half] = lo_ref[...]
    far_ref[half:] = hi_ref[...]

    def put(o, value):
        mix_ref[2, :, o * count : (o + 1) * count] = value

    mix_rows(
        lambda o: far_ref[:, o * rows_block : (o + 1) * rows_block],
        column(tags_ref[2])[:, 0:1], tags_ref, here, put,
    )
    flat_ref[...] = raw_ref[...].astype(F32)
    step = orbs * quota * halves
    lane = lax.broadcasted_iota(jnp.int32, (LANES, LANES), 1).astype(F32)
    for o in range(orbs):
        tag = tags_ref[(o + orbs - here) % orbs]
        size = jnp.zeros((8, count), F32)
        for c in range(size_ref.shape[0]):
            live = (size_ref[c] // orbs).astype(F32)
            size = size + jnp.where(tag[0:8, :] == float(c), live, 0.0)
        size = column(size)[:, 0:1]
        for q in range(quota):
            for h in range(halves):
                piece = flat_ref[pl.ds((o * quota + q) * halves + h, LANES, stride=step), :]
                keep = lane + float(h * LANES) < size[q * LANES : (q + 1) * LANES]
                row = o * count + q * LANES
                block_ref[row : row + LANES, h * LANES : (h + 1) * LANES] = jnp.where(
                    keep, piece, 0.0
                ).astype(BF)

    def multiply(s):
        done = jnp.dot(mix_ref[s], block_ref[...], preferred_element_type=F32)
        to = (here + s) % orbs
        for q in range(quota):
            for h in range(halves):
                flat_ref[pl.ds((to * quota + q) * halves + h, LANES, stride=step), :] = done[
                    q * LANES : (q + 1) * LANES, h * LANES : (h + 1) * LANES
                ]

    multiply(2)
    for s, cp in copies:
        cp.wait()
        multiply(s)
    out_ref[...] = flat_ref[...].astype(BF)


def finish_body(orbs, quota, raw_ref, amp_ref, rec_ref, den_ref, out_ref, flat_ref, tile_ref):
    tiles = amp_ref.shape[1] // LANES
    halves = tiles // orbs
    flat_ref[...] = raw_ref[...].astype(F32)
    for o in range(orbs):
        for q in range(quota):
            for h in range(halves):
                at = (o * quota + q) * halves + h
                piece = flat_ref[pl.ds(at, LANES, stride=orbs * quota * halves), :]
                tile_ref[o * halves + h, pl.ds(q, LANES, stride=quota), :] = piece
    rec = column(rec_ref[...])
    den = column(den_ref[...])
    for a in range(quota):
        rows = slice(a * LANES, (a + 1) * LANES)
        for t in range(tiles):
            cols = slice(t * LANES, (t + 1) * LANES)
            move = rec[:, a : a + 1] * tile_ref[t, rows, :] / den[:, a : a + 1]
            out_ref[rows, cols] = (amp_ref[rows, cols].astype(F32) + move).astype(BF)


def pick(pair_source, interaction, quota):
    blocks, rows_block, width = interaction.shape
    return call(
        functools.partial(pick_body, quota),
        jax.ShapeDtypeStruct((quota * LANES + TAGS, width), BF),
        [VM, VM],
        name="pick",
    )(pair_source, interaction.reshape(blocks * rows_block, width))


def pack(amplitudes, recoupling, orbs, quota):
    rows, width = amplitudes.shape
    flat = rows * width // LANES
    return call(
        functools.partial(pack_body, orbs, quota),
        jax.ShapeDtypeStruct((flat, LANES), BF),
        [VM, VM],
        [pltpu.VMEM((width // LANES, rows, LANES), F32), pltpu.VMEM((flat, LANES), F32)],
        name="pack",
    )(amplitudes, recoupling.reshape(rows // LANES, LANES))


def build(here, own, after, before, far, quota):
    count = quota * LANES
    mixed = jax.ShapeDtypeStruct((count, 4 * count), BF)
    tags = jax.ShapeDtypeStruct((4, TAGS, count), F32)
    return call(
        functools.partial(build_body, quota),
        (mixed, mixed, mixed, tags),
        [SM, VM, VM, VM, VM],
        [pltpu.VMEM((4, TAGS, count), F32)],
        name="build",
    )(here, own, after, before, far)


def cycle(here, sizes, raw, lo, hi, tags, mixed, quota):
    count = quota * LANES
    return call(
        functools.partial(cycle_body, quota),
        jax.ShapeDtypeStruct(raw.shape, BF),
        [SM, SM, VM, VM, VM, VM, ANY, ANY, ANY],
        [
            pltpu.VMEM(raw.shape, F32),
            pltpu.VMEM((4 * count, 2 * LANES), BF),
            pltpu.VMEM((4, count, 4 * count), BF),
            pltpu.VMEM((count, lo.shape[1]), BF),
            pltpu.SemaphoreType.DMA((3,)),
        ],
        name="cycle",
    )(here, sizes, raw, lo, hi, tags, *mixed)


def finish(raw, amplitudes, recoupling, denominators, orbs, quota):
    rows, width = amplitudes.shape
    return call(
        functools.partial(finish_body, orbs, quota),
        jax.ShapeDtypeStruct((rows, width), BF),
        [VM, VM, VM, VM],
        [pltpu.VMEM(raw.shape, F32), pltpu.VMEM((width // LANES, rows, LANES), F32)],
        name="finish",
    )(
        raw, amplitudes,
        recoupling.reshape(rows // LANES, LANES), denominators.reshape(rows // LANES, LANES),
    )


def shards(
    amplitudes, recoupling, denominators, interaction, pair_source, return_slot, channel_sizes
):
    chan_count = lax.axis_size("chan")
    orbs = lax.axis_size("orb")
    row_count, _ = amplitudes.shape
    quota = row_count // chan_count
    count = quota * LANES
    half = count // 2
    halves = pair_source.shape[1] // LANES
    peers = chan_count * orbs

    def shift(x, by):
        return lax.ppermute(x, "orb", [(i, (i + by) % orbs) for i in range(orbs)])

    def exchange(x):
        x = x.reshape(peers, quota, halves, LANES)
        x = lax.all_to_all(x, BOTH, split_axis=0, concat_axis=0, tiled=True)
        return x.reshape(peers * quota * halves, LANES)

    own = pick(pair_source, interaction, quota)
    after = shift(own, -1)
    before = shift(own, 1)
    outgoing, _ = lax.optimization_barrier((pack(amplitudes, recoupling, orbs, quota), own))
    raw = exchange(outgoing)
    lo = shift(after[:half], -1)
    hi = shift(before[half:count], 1)
    tag, _ = lax.optimization_barrier((own[count:], after))
    far = shift(tag, 2)
    here = lax.axis_index("orb").astype(jnp.int32).reshape(1)
    *mixed, tags = build(here, own, after, before, far, quota)
    back = cycle(here, channel_sizes, raw, lo, hi, tags, mixed, quota)
    returned = exchange(back)
    return finish(returned, amplitudes, recoupling, denominators, orbs, quota)


def solution(mesh):
    in_specs = (
        P(("chan", "orb"), None),
        P(("chan", "orb")),
        P(("chan", "orb")),
        P("chan", "orb", None),
        P("chan", "orb"),
        P(("chan", "orb")),
        P("chan"),
    )
    out_specs = P(("chan", "orb"), None)
    return jax.shard_map(
        shards, mesh=mesh, in_specs=in_specs, out_specs=out_specs, check_vma=False
    )
```

time: 274 us -> 182 us (0.66)
  waiting for transfers between devices: 134 us -> 50.4 us
  Pallas kernels: 0 us -> 32.1 us
  starting transfers between devices: 19 us -> 39.8 us
  local copies, waits for them, and re-layouts: 21.9 us -> 3.79 us
  between operations: 13.5 us -> 0.14 us
  other arithmetic: 10.1 us -> 0 us
  blocking collectives: 65.6 us -> 55.7 us
  matrix products: 7.09 us -> 0 us
    all_gather x1 -> x0, waiting for transfers between devices: 83.3 us -> none  [shards(): lax.all_gather(amp_block, 'orb', axis=1, tiled=True)]
    all_to_all x1, waiting for transfers between devices: 50.7 us -> 0.01 us  [exchange(): x = lax.all_to_all(x, BOTH, split_axis=0, concat_axis=0, tiled=True)]
    ppermute x0 -> x5, waiting for transfers between devices: none -> 50.3 us  [shift(): return lax.ppermute(x, 'orb', [(i, (i + by) % orbs) for i in range(orbs)])]
    pallas_call x0 -> x5, Pallas kernels: none -> 32.1 us  [the longest x1 11.7 us: cycle(): call(functools.partial(cycle_body, quota), jax.ShapeDtypeStruct(raw.shape...]
    ppermute x0 -> x5, starting transfers between devices: none -> 17.7 us  [shift(): return lax.ppermute(x, 'orb', [(i, (i + by) % orbs) for i in range(orbs)])]
    gather x3 -> x0, local copies, waits for them, and re-layouts: 12.7 us -> none  [the longest x2 7.34 us: shards(): jnp.take(cycle_local.reshape(blocks_here * rows_block, width), return_slo...]
    all_to_all x1, blocking collectives: 65.6 us -> 55.7 us  [exchange(): x = lax.all_to_all(x, BOTH, split_axis=0, concat_axis=0, tiled=True)]
    dot_general x1 -> x0, matrix products: 7.09 us -> none  [shards(): jnp.einsum('bik,bkj->bij', interaction, lax.all_gather(amp_block, 'orb',...]
  transfers between devices with their start and end apart: 2 -> 6, of which waited for: 2 -> 2; matrix products, arithmetic and copies ran while one was open for 0% -> 1% of each run, Pallas kernels for 0% -> 5%
where the time goes in v2:
time: 182 us
  blocking collectives  55.7 us (31%)
  waiting for transfers between devices  50.4 us (28%)
  starting transfers between devices  39.8 us (22%)
  Pallas kernels  32.1 us (18%)
  local copies, waits for them, and re-layouts  3.79 us (2%)
    all_to_all x1, blocking collectives, exchange(): x = lax.all_to_all(x, BOTH, split_axis=0, concat_axis=0, tiled=True)  55.7 us
    ppermute x5, waiting for transfers between devices, shift(): return lax.ppermute(x, 'orb', [(i, (i + by) % orbs) for i in range(orbs)])  50.3 us
    all_to_all x1, starting transfers between devices, exchange(): x = lax.all_to_all(x, BOTH, split_axis=0, concat_axis=0, tiled=True)  22.1 us
    ppermute x5, starting transfers between devices, shift(): return lax.ppermute(x, 'orb', [(i, (i + by) % orbs) for i in range(orbs)])  17.7 us
    pallas_call x1, Pallas kernels, cycle(): call(functools.partial(cycle_body, quota), jax.ShapeDtypeStruct(raw.shape...  11.7 us
    pallas_call x1, Pallas kernels, build(): call(functools.partial(build_body, quota), (mixed, mixed, mixed, tags), [...  8.62 us
    pallas_call x1, Pallas kernels, pick(): call(functools.partial(pick_body, quota), jax.ShapeDtypeStruct((quota * L...  4.54 us
    pallas_call x1, Pallas kernels, finish(): call(functools.partial(finish_body, orbs, quota), jax.ShapeDtypeStruct((r...  3.89 us
  transfers between devices with their start and end apart: 6, of which 2 were waited for; matrix products, arithmetic and copies ran while one was open for 1% of the time, Pallas kernels for 5%

profile of v2, /device:TPU:1, one launch (start us, length us, event | category | flops | bytes accessed | tf_op | source)
XLA Modules:
  0.0 181.8 jit_solution(14081005914444886400)
XLA Ops:
  0.0 4.5 %pick.1.own_ref = bf16[656,1024]{1,0:T(8,128)(2,1)} custom-call(s32[4,256]{1,0:T(4,128)} %src_ref.1, bf16[1024,1024]{1,0:T(8,128)(2,1)} %bitcast.12), custom_call_target="tpu_custom_call" | custom-call | tf_op jit(solution)/shard_map/pick/pallas_call | solution.py:201
  4.5 3.3 %pack.1 = bf16[5120,128]{1,0:T(8,128)(2,1)} custom-call(bf16[640,1024]{1,0:T(8,128)(2,1)} %amp_ref.3, f32[5,128]{1,0:T(8,128)} %bitcast.13), custom_call_target="tpu_custom_call" | custom-call | tf_op jit(solution)/shard_map/pack/pallas_call | solution.py:212
  7.9 0.0 copy-start
  7.9 22.1 %all-to-all-start = ((bf16[512,5,2,128]{3,2,1,0:T(2,128)(2,1)}), bf16[512,5,2,128]{3,2,1,0:T(2,128)(2,1)S(1)}, u32[]{:S(2)}, u32[]{:S(2)}) async-start(bf16[512,5,2,128]{3,2,1,0:T(2,128)(2,1)} %bitcast.8), calls=%async_computation | async-start | bytes 2621440 | tf_op jit(solution)/shard_map/all_to_all | solution.py:282
  30.0 0.0 copy-done
  30.0 4.5 %collective-permute-start = (bf16[656,1024]{1,0:T(8,128)(2,1)S(1)}, bf16[656,1024]{1,0:T(8,128)(2,1)S(1)}, u32[]{:S(2)}, u32[]{:S(2)}) collective-permute-start(bf16[656,1024]{1,0:T(8,128)(2,1)S(1)} %copy-done), channel_id=1, source_target_pairs={{0,3},{1,0},{2,1},{3,2},{4,7},{5,4},{6,5},{7,6},{8,11},{9,8},{10,9... | collective-permute-start | bytes 4030472 | tf_op jit(solution)/shard_map/ppermute | solution.py:278
  34.5 1.9 %collective-permute-start.2 = (bf16[656,1024]{1,0:T(8,128)(2,1)S(1)}, bf16[656,1024]{1,0:T(8,128)(2,1)S(1)}, u32[]{:S(2)}, u32[]{:S(2)}) collective-permute-start(bf16[656,1024]{1,0:T(8,128)(2,1)S(1)} %copy-done), channel_id=1, source_target_pairs={{0,1},{1,2},{2,3},{3,0},{4,5},{5,6},{6,7},{7,4},{8,9},{9,10},{10,1... | collective-permute-start | bytes 4030472 | tf_op jit(solution)/shard_map/ppermute | solution.py:278
  36.5 38.3 %collective-permute-done.after_ref = bf16[656,1024]{1,0:T(8,128)(2,1)S(1)} collective-permute-done((bf16[656,1024]{1,0:T(8,128)(2,1)S(1)}, bf16[656,1024]{1,0:T(8,128)(2,1)S(1)}, u32[]{:S(2)}, u32[]{:S(2)}) %collective-permute-start) | collective-permute-done | bytes 1343520 | tf_op jit(solution)/shard_map/ppermute | solution.py:278
  74.7 0.0 copy-start.2
  74.7 1.0 slice.12
  75.7 5.3 %collective-permute-start.1 = (bf16[320,1024]{1,0:T(8,128)(2,1)}, bf16[320,1024]{1,0:T(8,128)(2,1)S(1)}, u32[]{:S(2)}, u32[]{:S(2)}) collective-permute-start(bf16[320,1024]{1,0:T(8,128)(2,1)} %slice.12), channel_id=1, source_target_pairs={{0,3},{1,0},{2,1},{3,2},{4,7},{5,4},{6,5},{7,6},{8,11},{9,8},{10,9... | collective-permute-start | bytes 1966088 | tf_op jit(solution)/shard_map/ppermute | solution.py:278
  81.0 0.0 collective-permute-done.2.before_ref
  81.0 0.0 copy-start.3
  81.0 1.0 slice.13
  82.0 1.9 %collective-permute-start.3 = (bf16[320,1024]{1,0:T(8,128)(2,1)}, bf16[320,1024]{1,0:T(8,128)(2,1)}, u32[]{:S(2)}, u32[]{:S(2)}) collective-permute-start(bf16[320,1024]{1,0:T(8,128)(2,1)} %slice.13), channel_id=1, source_target_pairs={{0,1},{1,2},{2,3},{3,0},{4,5},{5,6},{6,7},{7,4},{8,9},{9,10},{10,1... | collective-permute-start | bytes 1966088 | tf_op jit(solution)/shard_map/ppermute | solution.py:278
  83.9 0.0 copy-done.2
  83.9 4.1 %collective-permute-start.4 = (bf16[16,1024]{1,0:T(8,128)(2,1)S(1)}, bf16[16,1024]{1,0:T(8,128)(2,1)S(1)}, u32[]{:S(2)}, u32[]{:S(2)}) collective-permute-start(bf16[16,1024]{1,0:T(8,128)(2,1)S(1)} %slice.14), channel_id=1, source_target_pairs={{0,2},{1,3},{2,0},{3,1},{4,6},{5,7},{6,4},{7,5},{8,10},{9,11},{10,... | collective-permute-start | bytes 98312 | tf_op jit(solution)/shard_map/ppermute | solution.py:278
  88.0 0.0 copy-done.3
  88.1 12.1 %collective-permute-done.4.far_ref = bf16[16,1024]{1,0:T(8,128)(2,1)S(1)} collective-permute-done((bf16[16,1024]{1,0:T(8,128)(2,1)S(1)}, bf16[16,1024]{1,0:T(8,128)(2,1)S(1)}, u32[]{:S(2)}, u32[]{:S(2)}) %collective-permute-start.4) | collective-permute-done | bytes 32800 | tf_op jit(solution)/shard_map/ppermute | solution.py:278
  100.1 0.0 copy-start.5
  100.1 0.6 copy-done.5
  100.7 8.6 %build.1 = (bf16[640,2560]{1,0:T(8,128)(2,1)}, bf16[640,2560]{1,0:T(8,128)(2,1)}, bf16[640,2560]{1,0:T(8,128)(2,1)}, f32[4,16,640]{2,1,0:T(8,128)}) custom-call(s32[1]{0:T(128)} %bitcast.here_ref, bf16[656,1024]{1,0:T(8,128)(2,1)} %pick.1.own_ref, bf16[656,1024]{1,0:T(8,128)(2,1)} %copy-done.2, bf16[656,1024]{1,0:T(8,128)(2,1)} %copy-done.3, ...), custom_call_target="tpu_custom_call" | custom-call | tf_op jit(solution)/shard_map/build/pallas_call | solution.py:225
  109.3 0.0 collective-permute-done.1.lo_ref
  109.4 0.0 copy-start.4
  109.4 0.0 collective-permute-done.3.hi_ref
  109.4 0.0 all-to-all-done
  109.4 0.0 copy-start.1
  109.4 0.8 copy-done.4
  110.2 0.4 copy-done.1
  110.6 11.7 %cycle.1 = bf16[5120,128]{1,0:T(8,128)(2,1)} custom-call(s32[1]{0:T(128)} %bitcast.here_ref, s32[4]{0:T(128)} %size_ref.1, bf16[5120,128]{1,0:T(8,128)(2,1)} %bitcast.10, bf16[320,1024]{1,0:T(8,128)(2,1)} %copy-done.4, bf16[320,1024]{1,0:T(8,128)(2,1)} %collective-permute-done.3.hi_ref, f32[4,16,640]{2,1,0:T(8,128)} %get-tuple-element.13.tags_ref, ...), custom_call_target="tpu_custom_call" | custom-call | tf_op jit(solution)/shard_map/cycle/pallas_call | solution.py:236
  122.3 55.7 %all_to_all.10 = bf16[512,5,2,128]{3,2,1,0:T(2,128)(2,1)} all-to-all(bf16[512,5,2,128]{3,2,1,0:T(2,128)(2,1)} %bitcast.11), channel_id=1, replica_groups=mesh['chan'=128,'orb'=4] {'chan','orb'}, dimensions={0} | all-to-all | bytes 2621440 | tf_op jit(solution)/shard_map/all_to_all | solution.py:282
  177.9 3.9 %finish.1 = bf16[640,1024]{1,0:T(8,128)(2,1)} custom-call(bf16[5120,128]{1,0:T(8,128)(2,1)} %bitcast.9, bf16[640,1024]{1,0:T(8,128)(2,1)} %amp_ref.3, f32[5,128]{1,0:T(8,128)} %bitcast.14, f32[5,128]{1,0:T(8,128)} %bitcast.15), custom_call_target="tpu_custom_call" | custom-call | tf_op jit(solution)/shard_map/finish/pallas_call | solution.py:253
  (1 shorter events, 0.0 us)
Async XLA Ops:
  7.9 22.2 %copy-start = (bf16[656,1024]{1,0:T(8,128)(2,1)S(1)}, bf16[656,1024]{1,0:T(8,128)(2,1)}, u32[]{:S(2)}) copy-start(bf16[656,1024]{1,0:T(8,128)(2,1)} %pick.1.own_ref) | copy-start | bytes 4030468
  7.9 101.5 %all-to-all-start = ((bf16[512,5,2,128]{3,2,1,0:T(2,128)(2,1)}), bf16[512,5,2,128]{3,2,1,0:T(2,128)(2,1)S(1)}, u32[]{:S(2)}, u32[]{:S(2)}) async-start(bf16[512,5,2,128]{3,2,1,0:T(2,128)(2,1)} %bitcast.8), calls=%async_computation | async-start | bytes 2621440 | tf_op jit(solution)/shard_map/all_to_all | solution.py:282
  30.0 44.7 %collective-permute-start = (bf16[656,1024]{1,0:T(8,128)(2,1)S(1)}, bf16[656,1024]{1,0:T(8,128)(2,1)S(1)}, u32[]{:S(2)}, u32[]{:S(2)}) collective-permute-start(bf16[656,1024]{1,0:T(8,128)(2,1)S(1)} %copy-done), channel_id=1, source_target_pairs={{0,3},{1,0},{2,1},{3,2},{4,7},{5,4},{6,5},{7,6},{8,11},{9,8},{10,9... | collective-permute-start | bytes 4030472 | tf_op jit(solution)/shard_map/ppermute | solution.py:278
  34.5 46.5 %collective-permute-start.2 = (bf16[656,1024]{1,0:T(8,128)(2,1)S(1)}, bf16[656,1024]{1,0:T(8,128)(2,1)S(1)}, u32[]{:S(2)}, u32[]{:S(2)}) collective-permute-start(bf16[656,1024]{1,0:T(8,128)(2,1)S(1)} %copy-done), channel_id=1, source_target_pairs={{0,1},{1,2},{2,3},{3,0},{4,5},{5,6},{6,7},{7,4},{8,9},{9,10},{10,1... | collective-permute-start | bytes 4030472 | tf_op jit(solution)/shard_map/ppermute | solution.py:278
  74.7 9.2 %copy-start.2 = (bf16[656,1024]{1,0:T(8,128)(2,1)}, bf16[656,1024]{1,0:T(8,128)(2,1)S(1)}, u32[]{:S(2)}) copy-start(bf16[656,1024]{1,0:T(8,128)(2,1)S(1)} %collective-permute-done.after_ref) | copy-start | bytes 4030468
  75.7 33.7 %collective-permute-start.1 = (bf16[320,1024]{1,0:T(8,128)(2,1)}, bf16[320,1024]{1,0:T(8,128)(2,1)S(1)}, u32[]{:S(2)}, u32[]{:S(2)}) collective-permute-start(bf16[320,1024]{1,0:T(8,128)(2,1)} %slice.12), channel_id=1, source_target_pairs={{0,3},{1,0},{2,1},{3,2},{4,7},{5,4},{6,5},{7,6},{8,11},{9,8},{10,9... | collective-permute-start | bytes 1966088 | tf_op jit(solution)/shard_map/ppermute | solution.py:278
  81.0 7.0 %copy-start.3 = (bf16[656,1024]{1,0:T(8,128)(2,1)}, bf16[656,1024]{1,0:T(8,128)(2,1)S(1)}, u32[]{:S(2)}) copy-start(bf16[656,1024]{1,0:T(8,128)(2,1)S(1)} %collective-permute-done.2.before_ref) | copy-start | bytes 4030468
  82.0 27.4 %collective-permute-start.3 = (bf16[320,1024]{1,0:T(8,128)(2,1)}, bf16[320,1024]{1,0:T(8,128)(2,1)}, u32[]{:S(2)}, u32[]{:S(2)}) collective-permute-start(bf16[320,1024]{1,0:T(8,128)(2,1)} %slice.13), channel_id=1, source_target_pairs={{0,1},{1,2},{2,3},{3,0},{4,5},{5,6},{6,7},{7,4},{8,9},{9,10},{10,1... | collective-permute-start | bytes 1966088 | tf_op jit(solution)/shard_map/ppermute | solution.py:278
  83.9 16.2 %collective-permute-start.4 = (bf16[16,1024]{1,0:T(8,128)(2,1)S(1)}, bf16[16,1024]{1,0:T(8,128)(2,1)S(1)}, u32[]{:S(2)}, u32[]{:S(2)}) collective-permute-start(bf16[16,1024]{1,0:T(8,128)(2,1)S(1)} %slice.14), channel_id=1, source_target_pairs={{0,2},{1,3},{2,0},{3,1},{4,6},{5,7},{6,4},{7,5},{8,10},{9,11},{10,... | collective-permute-start | bytes 98312 | tf_op jit(solution)/shard_map/ppermute | solution.py:278
  100.1 0.6 copy-start.5
  109.4 0.8 copy-start.4
  109.4 1.2 copy-start.1

commit v3 on v2

v3 whole, which is shorter than its diff:
```python
import functools

import jax
import jax.numpy as jnp
from jax import lax
from jax.experimental import pallas as pl
from jax.experimental.pallas import tpu as pltpu
from jax.sharding import PartitionSpec as P


BOTH = ("chan", "orb")
LANES = 128
TAGS = 16
BF = jnp.bfloat16
F32 = jnp.float32
VMEM_BYTES = 56 * 1024 * 1024
CHUNKS = 4

VM = pl.BlockSpec(memory_space=pltpu.VMEM)
SM = pl.BlockSpec(memory_space=pltpu.SMEM)
ANY = pl.BlockSpec(memory_space=pl.ANY)


def call(body, out_shape, in_specs, out_specs, scratch=(), **kw):
    return pl.pallas_call(
        body,
        out_shape=out_shape,
        in_specs=in_specs,
        out_specs=out_specs,
        scratch_shapes=list(scratch),
        compiler_params=pltpu.CompilerParams(vmem_limit_bytes=VMEM_BYTES),
        **kw,
    )


def one_hot(hit):
    return jnp.where(hit, 1.0, 0.0).astype(BF)


def column(rows):
    r, n = rows.shape
    tall = jnp.concatenate([rows, jnp.zeros((LANES - r, n), F32)], axis=0)
    return jnp.transpose(tall)


def pick_body(quota, src_ref, w_ref, out_ref, hit_ref):
    blocks, rows_block = src_ref.shape
    states, width = w_ref.shape
    count = quota * LANES
    src = jnp.concatenate([src_ref[c : c + 1, :] for c in range(blocks)], axis=1)
    sender = (src * 205) >> 10
    place = jnp.where(src >= 0, (src - sender * quota) * LANES + sender, -1)
    lane = lax.broadcasted_iota(jnp.int32, (TAGS, states), 1)
    which = lax.broadcasted_iota(jnp.int32, (TAGS, states), 0)
    labels = jnp.where(which == 0, lane // rows_block, jnp.where(which == 1, lane % rows_block, 0))
    labels = labels.astype(F32).astype(BF)
    out_ref[count:, count:] = jnp.zeros((TAGS, width - count), BF)
    for q in range(quota):
        at = lax.broadcasted_iota(jnp.int32, (LANES, states), 0) + q * LANES
        hit = one_hot(at == place)
        here = slice(q * LANES, (q + 1) * LANES)
        hit_ref[here, :] = hit
        out_ref[count:, here] = lax.dot_general(
            labels, hit, (((1,), (1,)), ((), ())), preferred_element_type=F32
        ).astype(BF)
    out_ref[:count, :] = jnp.dot(
        hit_ref[...], w_ref[...], preferred_element_type=F32
    ).astype(BF)


def spread_rows(value, out_ref):
    tall = column(value)
    for a in range(value.shape[0]):
        out_ref[a * LANES : (a + 1) * LANES, :] = jnp.broadcast_to(
            tall[:, a : a + 1], (LANES, LANES)
        )


def pack_body(
    orbs, quota, amp_any, rec_ref, out_any, amp_ref, scale_ref, tile_ref, flat_ref, out_ref,
    sem_in, sem_out,
):
    rows, width = amp_ref.shape
    tiles = width // LANES
    halves = tiles // orbs
    part = rows // CHUNKS
    groups = part // quota
    loads = []
    for j in range(CHUNKS):
        here = slice(j * part, (j + 1) * part)
        loads.append(pltpu.make_async_copy(amp_any.at[here], amp_ref.at[here], sem_in.at[j]))
        loads[j].start()
    spread_rows(rec_ref[...], scale_ref)
    stores = []
    for j in range(CHUNKS):
        here = slice(j * part, (j + 1) * part)
        loads[j].wait()
        for t in range(tiles):
            tile_ref[t, here, :] = (
                amp_ref[here, t * LANES : (t + 1) * LANES].astype(F32) * scale_ref[here, :]
            )
        for o in range(orbs):
            for q in range(quota):
                for h in range(halves):
                    piece = tile_ref[o * halves + h, pl.ds(j * part + q, groups, stride=quota), :]
                    at = j * part * tiles + (o * quota + q) * halves + h
                    flat_ref[pl.ds(at, groups, stride=orbs * quota * halves), :] = piece
        to = slice(j * part * tiles, (j + 1) * part * tiles)
        out_ref[to, :] = flat_ref[to, :].astype(BF)
        stores.append(pltpu.make_async_copy(out_ref.at[to], out_any.at[to], sem_out.at[j]))
        stores[j].start()
    for cp in stores:
        cp.wait()


def build_body(
    quota, here_ref, size_ref, own_ref, after_ref, before_ref, far_ref,
    m0, m1, m3, hot_ref, block_ref, owner_ref, limit_ref, tags_ref,
):
    count = quota * LANES
    rows_block = hot_ref.shape[1]
    orbs = hot_ref.shape[0]
    refs = (own_ref, after_ref, None, before_ref)
    for s, ref in enumerate(refs):
        tag = far_ref[:, :count] if ref is None else ref[count:, :count]
        tags_ref[s] = tag.astype(F32)
    here = here_ref[0]
    slot = lax.broadcasted_iota(jnp.int32, (rows_block, count), 0).astype(F32)
    for o in range(orbs):
        tag = tags_ref[(o + orbs - here) % orbs]
        hot_ref[o] = one_hot(slot == tag[1:2, :])
        block_ref[o] = tag[0:8, :]
        size = jnp.zeros((1, count), F32)
        for c in range(size_ref.shape[0]):
            live = (size_ref[c] // orbs).astype(F32)
            size = size + jnp.where(tag[0:1, :] == float(c), live, 0.0)
        limit_ref[o * count : (o + 1) * count, :] = jnp.broadcast_to(
            column(size)[:, 0:1], (count, LANES)
        )
    owner_ref[...] = jnp.broadcast_to(column(tags_ref[2])[:, 0:1], (count, LANES))
    for s, out in ((0, m0), (1, m1), (3, m3)):
        owner = column(tags_ref[s])[:, 0:1]
        for o in range(orbs):
            part = refs[s][:count, o * rows_block : (o + 1) * rows_block]
            spread = jnp.dot(part, hot_ref[o], preferred_element_type=F32)
            out[:, o * count : (o + 1) * count] = jnp.where(
                owner == block_ref[o, 0:1, :], spread, 0.0
            ).astype(BF)


def cycle_body(
    quota, here_ref, raw_any, lo_any, hi_any, hot_any, block_any, owner_any, limit_any,
    m0, m1, m3, out_any,
    raw_ref, far_ref, hot_ref, block_ref, owner_ref, limit_ref, mix_ref, flat_ref, rows_ref,
    out_ref, sem,
):
    orbs, rows_block, count = hot_ref.shape
    halves = rows_block // LANES
    half = count // 2
    here = here_ref[0]
    pairs = (
        (lo_any, far_ref.at[:half]), (hi_any, far_ref.at[half:]), (hot_any, hot_ref),
        (block_any, block_ref), (owner_any, owner_ref), (raw_any, raw_ref),
        (limit_any, limit_ref), (m0, mix_ref.at[0]), (m1, mix_ref.at[1]), (m3, mix_ref.at[3]),
    )
    copies = [pltpu.make_async_copy(a, b, sem.at[i]) for i, (a, b) in enumerate(pairs)]
    for cp in copies:
        cp.start()
    for cp in copies[:7]:
        cp.wait()
    owner = owner_ref[:, 0:1]
    step = orbs * quota * halves
    lane = lax.broadcasted_iota(jnp.int32, (LANES, LANES), 1).astype(F32)
    flat_ref[...] = raw_ref[...].astype(F32)
    for o in range(orbs):
        spread = jnp.dot(
            far_ref[:, o * rows_block : (o + 1) * rows_block], hot_ref[o],
            preferred_element_type=F32,
        )
        mix_ref[2, :, o * count : (o + 1) * count] = jnp.where(
            owner == block_ref[o, 0:1, :], spread, 0.0
        ).astype(BF)
        for q in range(quota):
            row = o * count + q * LANES
            for h in range(halves):
                piece = flat_ref[pl.ds((o * quota + q) * halves + h, LANES, stride=step), :]
                keep = lane + float(h * LANES) < limit_ref[row : row + LANES, :]
                rows_ref[row : row + LANES, h * LANES : (h + 1) * LANES] = jnp.where(
                    keep, piece, 0.0
                ).astype(BF)
    for cp in copies[7:]:
        cp.wait()
    for s in range(orbs):
        done = jnp.dot(mix_ref[s], rows_ref[...], preferred_element_type=F32)
        to = (here + s) % orbs
        for q in range(quota):
            for h in range(halves):
                flat_ref[pl.ds((to * quota + q) * halves + h, LANES, stride=step), :] = done[
                    q * LANES : (q + 1) * LANES, h * LANES : (h + 1) * LANES
                ]
    part = out_ref.shape[0] // CHUNKS
    for j in range(CHUNKS):
        rows = slice(j * part, (j + 1) * part)
        out_ref[rows, :] = flat_ref[rows, :].astype(BF)
        pltpu.make_async_copy(out_ref.at[rows], out_any.at[rows], sem.at[j]).start()
    for j in range(CHUNKS):
        rows = slice(j * part, (j + 1) * part)
        pltpu.make_async_copy(out_ref.at[rows], out_any.at[rows], sem.at[j]).wait()


def finish_body(
    orbs, quota, raw_any, amp_any, rec_ref, den_ref, out_any,
    raw_ref, amp_ref, scale_ref, flat_ref, tile_ref, out_ref, sem_in, sem_out,
):
    rows, width = amp_ref.shape
    tiles = width // LANES
    halves = tiles // orbs
    part = rows // CHUNKS
    groups = part // quota
    loads = []
    for j in range(CHUNKS):
        here = slice(j * part, (j + 1) * part)
        to = slice(j * part * tiles, (j + 1) * part * tiles)
        loads.append(pltpu.make_async_copy(raw_any.at[to], raw_ref.at[to], sem_in.at[0, j]))
        loads.append(pltpu.make_async_copy(amp_any.at[here], amp_ref.at[here], sem_in.at[1, j]))
    for cp in loads:
        cp.start()
    spread_rows(rec_ref[...] / den_ref[...], scale_ref)
    stores = []
    for j in range(CHUNKS):
        here = slice(j * part, (j + 1) * part)
        to = slice(j * part * tiles, (j + 1) * part * tiles)
        loads[2 * j].wait()
        loads[2 * j + 1].wait()
        flat_ref[to, :] = raw_ref[to, :].astype(F32)
        for o in range(orbs):
            for q in range(quota):
                for h in range(halves):
                    at = j * part * tiles + (o * quota + q) * halves + h
                    piece = flat_ref[pl.ds(at, groups, stride=orbs * quota * halves), :]
                    tile_ref[o * halves + h, pl.ds(j * part + q, groups, stride=quota), :] = piece
        for t in range(tiles):
            cols = slice(t * LANES, (t + 1) * LANES)
            move = scale_ref[here, :] * tile_ref[t, here, :]
            out_ref[here, cols] = (amp_ref[here, cols].astype(F32) + move).astype(BF)
        stores.append(pltpu.make_async_copy(out_ref.at[here], out_any.at[here], sem_out.at[j]))
        stores[j].start()
    for cp in stores:
        cp.wait()


def pick(pair_source, interaction, quota):
    blocks, rows_block, width = interaction.shape
    count = quota * LANES
    states = blocks * rows_block
    return call(
        functools.partial(pick_body, quota),
        jax.ShapeDtypeStruct((count + TAGS, width), BF),
        [VM, VM],
        VM,
        [pltpu.VMEM((count, states), BF)],
        name="pick",
    )(pair_source, interaction.reshape(states, width))


def pack(amplitudes, recoupling, orbs, quota):
    rows, width = amplitudes.shape
    tiles = width // LANES
    return call(
        functools.partial(pack_body, orbs, quota),
        jax.ShapeDtypeStruct((rows * tiles, LANES), BF),
        [ANY, VM],
        ANY,
        [
            pltpu.VMEM((rows, width), BF),
            pltpu.VMEM((rows, LANES), F32),
            pltpu.VMEM((tiles, rows, LANES), F32),
            pltpu.VMEM((rows * tiles, LANES), F32),
            pltpu.VMEM((rows * tiles, LANES), BF),
            pltpu.SemaphoreType.DMA((CHUNKS,)),
            pltpu.SemaphoreType.DMA((CHUNKS,)),
        ],
        name="pack",
    )(amplitudes, recoupling.reshape(rows // LANES, LANES))


def build(here, sizes, own, after, before, far, quota):
    count = quota * LANES
    mixed = jax.ShapeDtypeStruct((count, 4 * count), BF)
    outs = (
        mixed, mixed, mixed,
        jax.ShapeDtypeStruct((4, own.shape[1] // 4, count), BF),
        jax.ShapeDtypeStruct((4, 8, count), F32),
        jax.ShapeDtypeStruct((count, LANES), F32),
        jax.ShapeDtypeStruct((4 * count, LANES), F32),
    )
    return call(
        functools.partial(build_body, quota),
        outs,
        [SM, SM, VM, VM, VM, VM],
        (VM,) * len(outs),
        [pltpu.VMEM((4, TAGS, count), F32)],
        name="build",
    )(here, sizes, own, after, before, far)


def cycle(here, raw, lo, hi, m0, m1, m3, hot, block, owner, limit, quota):
    count = quota * LANES
    return call(
        functools.partial(cycle_body, quota),
        jax.ShapeDtypeStruct(raw.shape, BF),
        [SM] + [ANY] * 10,
        ANY,
        [
            pltpu.VMEM(raw.shape, BF),
            pltpu.VMEM((count, lo.shape[1]), BF),
            pltpu.VMEM(hot.shape, BF),
            pltpu.VMEM(block.shape, F32),
            pltpu.VMEM(owner.shape, F32),
            pltpu.VMEM(limit.shape, F32),
            pltpu.VMEM((4, count, 4 * count), BF),
            pltpu.VMEM(raw.shape, F32),
            pltpu.VMEM((4 * count, hot.shape[1]), BF),
            pltpu.VMEM(raw.shape, BF),
            pltpu.SemaphoreType.DMA((10,)),
        ],
        name="cycle",
    )(here, raw, lo, hi, hot, block, owner, limit, m0, m1, m3)


def finish(raw, amplitudes, recoupling, denominators, orbs, quota):
    rows, width = amplitudes.shape
    tiles = width // LANES
    return call(
        functools.partial(finish_body, orbs, quota),
        jax.ShapeDtypeStruct((rows, width), BF),
        [ANY, ANY, VM, VM],
        ANY,
        [
            pltpu.VMEM((rows * tiles, LANES), BF),
            pltpu.VMEM((rows, width), BF),
            pltpu.VMEM((rows, LANES), F32),
            pltpu.VMEM((rows * tiles, LANES), F32),
            pltpu.VMEM((tiles, rows, LANES), F32),
            pltpu.VMEM((rows, width), BF),
            pltpu.SemaphoreType.DMA((2, CHUNKS)),
            pltpu.SemaphoreType.DMA((CHUNKS,)),
        ],
        name="finish",
    )(
        raw, amplitudes,
        recoupling.reshape(rows // LANES, LANES), denominators.reshape(rows // LANES, LANES),
    )


def shards(
    amplitudes, recoupling, denominators, interaction, pair_source, return_slot, channel_sizes
):
    chan_count = lax.axis_size("chan")
    orbs = lax.axis_size("orb")
    row_count, _ = amplitudes.shape
    quota = row_count // chan_count
    count = quota * LANES
    half = count // 2
    halves = pair_source.shape[1] // LANES
    peers = chan_count * orbs

    def shift(x, by):
        return lax.ppermute(x, "orb", [(i, (i + by) % orbs) for i in range(orbs)])

    def exchange(x):
        x = x.reshape(peers, quota, halves, LANES)
        x = lax.all_to_all(x, BOTH, split_axis=0, concat_axis=0, tiled=True)
        return x.reshape(peers * quota * halves, LANES)

    own = pick(pair_source, interaction, quota)
    after = shift(own, -1)
    before = shift(own, 1)
    outgoing, _ = lax.optimization_barrier((pack(amplitudes, recoupling, orbs, quota), own))
    raw = exchange(outgoing)
    far = shift(own[count:], 2)
    lo = shift(after[:half], -1)
    hi = shift(before[half:count], 1)
    here = lax.axis_index("orb").astype(jnp.int32).reshape(1)
    built = build(here, channel_sizes, own, after, before, far, quota)
    back = cycle(here, raw, lo, hi, *built, quota)
    returned = exchange(back)
    return finish(returned, amplitudes, recoupling, denominators, orbs, quota)


def solution(mesh):
    in_specs = (
        P(("chan", "orb"), None),
        P(("chan", "orb")),
        P(("chan", "orb")),
        P("chan", "orb", None),
        P("chan", "orb"),
        P(("chan", "orb")),
        P("chan"),
    )
    out_specs = P(("chan", "orb"), None)
    return jax.shard_map(
        shards, mesh=mesh, in_specs=in_specs, out_specs=out_specs, check_vma=False
    )
```

time: 182 us -> 181 us (level)
  no operation moved by 1% of the time
where the time goes in v3:
time: 181 us
  blocking collectives  55.7 us (31%)
  waiting for transfers between devices  50.4 us (28%)
  starting transfers between devices  39.9 us (22%)
  Pallas kernels  30.6 us (17%)
  local copies, waits for them, and re-layouts  3.77 us (2%)
    all_to_all x1, blocking collectives, exchange(): x = lax.all_to_all(x, BOTH, split_axis=0, concat_axis=0, tiled=True)  55.7 us
    ppermute x5, waiting for transfers between devices, shift(): return lax.ppermute(x, 'orb', [(i, (i + by) % orbs) for i in range(orbs)])  50.4 us
    all_to_all x1, starting transfers between devices, exchange(): x = lax.all_to_all(x, BOTH, split_axis=0, concat_axis=0, tiled=True)  22.2 us
    ppermute x5, starting transfers between devices, shift(): return lax.ppermute(x, 'orb', [(i, (i + by) % orbs) for i in range(orbs)])  17.7 us
    pallas_call x1, Pallas kernels, cycle(): call(functools.partial(cycle_body, quota), jax.ShapeDtypeStruct(raw.shape...  10.6 us
    pallas_call x1, Pallas kernels, build(): call(functools.partial(build_body, quota), outs, [SM, SM, VM, VM, VM, VM]...  8.39 us
    pallas_call x1, Pallas kernels, pick(): call(functools.partial(pick_body, quota), jax.ShapeDtypeStruct((count + T...  4.53 us
    pallas_call x1, Pallas kernels, finish(): call(functools.partial(finish_body, orbs, quota), jax.ShapeDtypeStruct((r...  3.83 us
  transfers between devices with their start and end apart: 6, of which 2 were waited for; matrix products, arithmetic and copies ran while one was open for 1% of the time, Pallas kernels for 5%

profile of v3, /device:TPU:1, one launch (start us, length us, event | category | flops | bytes accessed | tf_op | source)
XLA Modules:
  0.0 180.6 jit_solution(11514054180723652783)
XLA Ops:
  0.0 4.5 %pick.1.own_ref = bf16[656,1024]{1,0:T(8,128)(2,1)} custom-call(s32[4,256]{1,0:T(4,128)} %src_ref.1, bf16[1024,1024]{1,0:T(8,128)(2,1)} %bitcast.12), custom_call_target="tpu_custom_call" | custom-call | tf_op jit(solution)/shard_map/pick/pallas_call | solution.py:256
  4.5 3.3 %pack.1 = bf16[5120,128]{1,0:T(8,128)(2,1)} custom-call(bf16[640,1024]{1,0:T(8,128)(2,1)} %amp_any.3, f32[5,128]{1,0:T(8,128)} %bitcast.13), custom_call_target="tpu_custom_call" | custom-call | tf_op jit(solution)/shard_map/pack/pallas_call | solution.py:269
  7.8 0.0 copy-start
  7.8 22.2 %all-to-all-start = ((bf16[512,5,2,128]{3,2,1,0:T(2,128)(2,1)}), bf16[512,5,2,128]{3,2,1,0:T(2,128)(2,1)S(1)}, u32[]{:S(2)}, u32[]{:S(2)}) async-start(bf16[512,5,2,128]{3,2,1,0:T(2,128)(2,1)} %bitcast.10), calls=%async_computation | async-start | bytes 2621440 | tf_op jit(solution)/shard_map/all_to_all | solution.py:373
  30.0 0.0 copy-done
  30.0 4.5 %collective-permute-start = (bf16[656,1024]{1,0:T(8,128)(2,1)S(1)}, bf16[656,1024]{1,0:T(8,128)(2,1)S(1)}, u32[]{:S(2)}, u32[]{:S(2)}) collective-permute-start(bf16[656,1024]{1,0:T(8,128)(2,1)S(1)} %copy-done), channel_id=1, source_target_pairs={{0,3},{1,0},{2,1},{3,2},{4,7},{5,4},{6,5},{7,6},{8,11},{9,8},{10,9... | collective-permute-start | bytes 4030472 | tf_op jit(solution)/shard_map/ppermute | solution.py:369
  34.5 1.9 %collective-permute-start.2 = (bf16[656,1024]{1,0:T(8,128)(2,1)S(1)}, bf16[656,1024]{1,0:T(8,128)(2,1)S(1)}, u32[]{:S(2)}, u32[]{:S(2)}) collective-permute-start(bf16[656,1024]{1,0:T(8,128)(2,1)S(1)} %copy-done), channel_id=1, source_target_pairs={{0,1},{1,2},{2,3},{3,0},{4,5},{5,6},{6,7},{7,4},{8,9},{9,10},{10,1... | collective-permute-start | bytes 4030472 | tf_op jit(solution)/shard_map/ppermute | solution.py:369
  36.4 38.3 %collective-permute-done.after_ref = bf16[656,1024]{1,0:T(8,128)(2,1)S(1)} collective-permute-done((bf16[656,1024]{1,0:T(8,128)(2,1)S(1)}, bf16[656,1024]{1,0:T(8,128)(2,1)S(1)}, u32[]{:S(2)}, u32[]{:S(2)}) %collective-permute-start) | collective-permute-done | bytes 1343520 | tf_op jit(solution)/shard_map/ppermute | solution.py:369
  74.7 0.0 copy-start.2
  74.7 0.9 slice.12
  75.6 5.3 %collective-permute-start.1 = (bf16[320,1024]{1,0:T(8,128)(2,1)}, bf16[320,1024]{1,0:T(8,128)(2,1)S(1)}, u32[]{:S(2)}, u32[]{:S(2)}) collective-permute-start(bf16[320,1024]{1,0:T(8,128)(2,1)} %slice.12), channel_id=1, source_target_pairs={{0,3},{1,0},{2,1},{3,2},{4,7},{5,4},{6,5},{7,6},{8,11},{9,8},{10,9... | collective-permute-start | bytes 1966088 | tf_op jit(solution)/shard_map/ppermute | solution.py:369
  80.9 0.0 collective-permute-done.2.before_ref
  81.0 0.0 copy-start.3
  81.0 1.0 slice.13
  81.9 0.0 copy-done.2
  81.9 1.9 %collective-permute-start.3 = (bf16[320,1024]{1,0:T(8,128)(2,1)}, bf16[320,1024]{1,0:T(8,128)(2,1)}, u32[]{:S(2)}, u32[]{:S(2)}) collective-permute-start(bf16[320,1024]{1,0:T(8,128)(2,1)} %slice.13), channel_id=1, source_target_pairs={{0,1},{1,2},{2,3},{3,0},{4,5},{5,6},{6,7},{7,4},{8,9},{9,10},{10,1... | collective-permute-start | bytes 1966088 | tf_op jit(solution)/shard_map/ppermute | solution.py:369
  83.9 0.0 copy-done.3
  83.9 4.1 %collective-permute-start.4 = (bf16[16,1024]{1,0:T(8,128)(2,1)S(1)}, bf16[16,1024]{1,0:T(8,128)(2,1)S(1)}, u32[]{:S(2)}, u32[]{:S(2)}) collective-permute-start(bf16[16,1024]{1,0:T(8,128)(2,1)S(1)} %slice.14), channel_id=1, source_target_pairs={{0,2},{1,3},{2,0},{3,1},{4,6},{5,7},{6,4},{7,5},{8,10},{9,11},{10,... | collective-permute-start | bytes 98312 | tf_op jit(solution)/shard_map/ppermute | solution.py:369
  88.0 12.1 %collective-permute-done.4.far_ref = bf16[16,1024]{1,0:T(8,128)(2,1)S(1)} collective-permute-done((bf16[16,1024]{1,0:T(8,128)(2,1)S(1)}, bf16[16,1024]{1,0:T(8,128)(2,1)S(1)}, u32[]{:S(2)}, u32[]{:S(2)}) %collective-permute-start.4) | collective-permute-done | bytes 32800 | tf_op jit(solution)/shard_map/ppermute | solution.py:369
  100.1 0.0 copy-start.5
  100.1 0.6 copy-done.5
  100.7 8.4 %build.1 = (bf16[640,2560]{1,0:T(8,128)(2,1)}, bf16[640,2560]{1,0:T(8,128)(2,1)}, bf16[640,2560]{1,0:T(8,128)(2,1)}, bf16[4,256,640]{2,1,0:T(8,128)(2,1)}, f32[4...) custom-call(s32[1]{0:T(128)} %bitcast.here_ref, s32[4]{0:T(128)} %size_ref.1, ...), custom_call_target="tpu_custom_call" | custom-call | tf_op jit(solution)/shard_map/build/pallas_call | solution.py:297
  109.1 0.0 collective-permute-done.1.lo_any
  109.1 0.0 copy-start.4
  109.1 0.0 collective-permute-done.3.hi_any
  109.1 0.0 all-to-all-done
  109.1 0.0 copy-start.1
  109.1 0.8 copy-done.4
  109.9 0.4 copy-done.1
  110.3 10.6 %cycle.1 = bf16[5120,128]{1,0:T(8,128)(2,1)} custom-call(s32[1]{0:T(128)} %bitcast.here_ref, bf16[5120,128]{1,0:T(8,128)(2,1)} %bitcast.8, bf16[320,1024]{1,0:T(8,128)(2,1)} %copy-done.4, bf16[320,1024]{1,0:T(8,128)(2,1)} %collective-permute-done.3.hi_any, bf16[4,256,640]{2,1,0:T(8,128)(2,1)} %get-tuple-element.14.hot_any, ...), custom_call_target="tpu_custom_call" | custom-call | tf_op jit(solution)/shard_map/cycle/pallas_call | solution.py:309
  120.9 55.7 %all_to_all.10 = bf16[512,5,2,128]{3,2,1,0:T(2,128)(2,1)} all-to-all(bf16[512,5,2,128]{3,2,1,0:T(2,128)(2,1)} %bitcast.9), channel_id=1, replica_groups=mesh['chan'=128,'orb'=4] {'chan','orb'}, dimensions={0} | all-to-all | bytes 2621440 | tf_op jit(solution)/shard_map/all_to_all | solution.py:373
  176.6 3.8 %finish.1 = bf16[640,1024]{1,0:T(8,128)(2,1)} custom-call(bf16[5120,128]{1,0:T(8,128)(2,1)} %bitcast.11, bf16[640,1024]{1,0:T(8,128)(2,1)} %amp_any.3, f32[5,128]{1,0:T(8,128)} %bitcast.14, f32[5,128]{1,0:T(8,128)} %bitcast.15), custom_call_target="tpu_custom_call" | custom-call | tf_op jit(solution)/shard_map/finish/pallas_call | solution.py:334
  (1 shorter events, 0.0 us)
Async XLA Ops:
  7.8 22.2 %copy-start = (bf16[656,1024]{1,0:T(8,128)(2,1)S(1)}, bf16[656,1024]{1,0:T(8,128)(2,1)}, u32[]{:S(2)}) copy-start(bf16[656,1024]{1,0:T(8,128)(2,1)} %pick.1.own_ref) | copy-start | bytes 4030468
  7.8 101.3 %all-to-all-start = ((bf16[512,5,2,128]{3,2,1,0:T(2,128)(2,1)}), bf16[512,5,2,128]{3,2,1,0:T(2,128)(2,1)S(1)}, u32[]{:S(2)}, u32[]{:S(2)}) async-start(bf16[512,5,2,128]{3,2,1,0:T(2,128)(2,1)} %bitcast.10), calls=%async_computation | async-start | bytes 2621440 | tf_op jit(solution)/shard_map/all_to_all | solution.py:373
  30.0 44.7 %collective-permute-start = (bf16[656,1024]{1,0:T(8,128)(2,1)S(1)}, bf16[656,1024]{1,0:T(8,128)(2,1)S(1)}, u32[]{:S(2)}, u32[]{:S(2)}) collective-permute-start(bf16[656,1024]{1,0:T(8,128)(2,1)S(1)} %copy-done), channel_id=1, source_target_pairs={{0,3},{1,0},{2,1},{3,2},{4,7},{5,4},{6,5},{7,6},{8,11},{9,8},{10,9... | collective-permute-start | bytes 4030472 | tf_op jit(solution)/shard_map/ppermute | solution.py:369
  34.5 46.5 %collective-permute-start.2 = (bf16[656,1024]{1,0:T(8,128)(2,1)S(1)}, bf16[656,1024]{1,0:T(8,128)(2,1)S(1)}, u32[]{:S(2)}, u32[]{:S(2)}) collective-permute-start(bf16[656,1024]{1,0:T(8,128)(2,1)S(1)} %copy-done), channel_id=1, source_target_pairs={{0,1},{1,2},{2,3},{3,0},{4,5},{5,6},{6,7},{7,4},{8,9},{9,10},{10,1... | collective-permute-start | bytes 4030472 | tf_op jit(solution)/shard_map/ppermute | solution.py:369
  74.7 7.3 %copy-start.2 = (bf16[656,1024]{1,0:T(8,128)(2,1)}, bf16[656,1024]{1,0:T(8,128)(2,1)S(1)}, u32[]{:S(2)}) copy-start(bf16[656,1024]{1,0:T(8,128)(2,1)S(1)} %collective-permute-done.after_ref) | copy-start | bytes 4030468
  75.6 33.4 %collective-permute-start.1 = (bf16[320,1024]{1,0:T(8,128)(2,1)}, bf16[320,1024]{1,0:T(8,128)(2,1)S(1)}, u32[]{:S(2)}, u32[]{:S(2)}) collective-permute-start(bf16[320,1024]{1,0:T(8,128)(2,1)} %slice.12), channel_id=1, source_target_pairs={{0,3},{1,0},{2,1},{3,2},{4,7},{5,4},{6,5},{7,6},{8,11},{9,8},{10,9... | collective-permute-start | bytes 1966088 | tf_op jit(solution)/shard_map/ppermute | solution.py:369
  81.0 2.9 %copy-start.3 = (bf16[656,1024]{1,0:T(8,128)(2,1)}, bf16[656,1024]{1,0:T(8,128)(2,1)S(1)}, u32[]{:S(2)}) copy-start(bf16[656,1024]{1,0:T(8,128)(2,1)S(1)} %collective-permute-done.2.before_ref) | copy-start | bytes 4030468
  81.9 27.1 %collective-permute-start.3 = (bf16[320,1024]{1,0:T(8,128)(2,1)}, bf16[320,1024]{1,0:T(8,128)(2,1)}, u32[]{:S(2)}, u32[]{:S(2)}) collective-permute-start(bf16[320,1024]{1,0:T(8,128)(2,1)} %slice.13), channel_id=1, source_target_pairs={{0,1},{1,2},{2,3},{3,0},{4,5},{5,6},{6,7},{7,4},{8,9},{9,10},{10,1... | collective-permute-start | bytes 1966088 | tf_op jit(solution)/shard_map/ppermute | solution.py:369
  83.9 16.2 %collective-permute-start.4 = (bf16[16,1024]{1,0:T(8,128)(2,1)S(1)}, bf16[16,1024]{1,0:T(8,128)(2,1)S(1)}, u32[]{:S(2)}, u32[]{:S(2)}) collective-permute-start(bf16[16,1024]{1,0:T(8,128)(2,1)S(1)} %slice.14), channel_id=1, source_target_pairs={{0,2},{1,3},{2,0},{3,1},{4,6},{5,7},{6,4},{7,5},{8,10},{9,11},{10,... | collective-permute-start | bytes 98312 | tf_op jit(solution)/shard_map/ppermute | solution.py:369
  100.1 0.6 copy-start.5
  109.1 0.8 copy-start.4
  109.1 1.2 copy-start.1

commit v4 on v3

--- a/solution.py
+++ b/solution.py
@@ -13,7 +13,7 @@
 TAGS = 16
 BF = jnp.bfloat16
 F32 = jnp.float32
-VMEM_BYTES = 56 * 1024 * 1024
+VMEM_BYTES = 48 * 1024 * 1024
 CHUNKS = 4
 
 VM = pl.BlockSpec(memory_space=pltpu.VMEM)
@@ -31,6 +31,10 @@
         compiler_params=pltpu.CompilerParams(vmem_limit_bytes=VMEM_BYTES),
         **kw,
     )
+
+
+def near(x):
+    return pltpu.with_memory_space_constraint(x, pltpu.VMEM)
 
 
 def one_hot(hit):
@@ -77,24 +81,17 @@
 
 
 def pack_body(
-    orbs, quota, amp_any, rec_ref, out_any, amp_ref, scale_ref, tile_ref, flat_ref, out_ref,
-    sem_in, sem_out,
+    orbs, quota, amp_ref, rec_ref, out_any, scale_ref, tile_ref, flat_ref, out_ref, sem_out
 ):
     rows, width = amp_ref.shape
     tiles = width // LANES
     halves = tiles // orbs
     part = rows // CHUNKS
     groups = part // quota
-    loads = []
-    for j in range(CHUNKS):
-        here = slice(j * part, (j + 1) * part)
-        loads.append(pltpu.make_async_copy(amp_any.at[here], amp_ref.at[here], sem_in.at[j]))
-        loads[j].start()
     spread_rows(rec_ref[...], scale_ref)
     stores = []
     for j in range(CHUNKS):
         here = slice(j * part, (j + 1) * part)
-        loads[j].wait()
         for t in range(tiles):
             tile_ref[t, here, :] = (
                 amp_ref[here, t * LANES : (t + 1) * LANES].astype(F32) * scale_ref[here, :]
@@ -149,89 +146,86 @@
 
 
 def cycle_body(
-    quota, here_ref, raw_any, lo_any, hi_any, hot_any, block_any, owner_any, limit_any,
-    m0, m1, m3, out_any,
-    raw_ref, far_ref, hot_ref, block_ref, owner_ref, limit_ref, mix_ref, flat_ref, rows_ref,
-    out_ref, sem,
-):
-    orbs, rows_block, count = hot_ref.shape
-    halves = rows_block // LANES
-    half = count // 2
-    here = here_ref[0]
+    quota, here_ref, raw_ref, limit_any, hot_any, block_any, owner_any, m0, m1, m3,
+    rows_ref, flat_ref, hot_ref, block_ref, owner_ref, wide_ref, limit_ref, mix_ref, sem,
+):
+    count = m0.shape[0]
+    orbs = m0.shape[1] // count
+    halves = rows_ref.shape[1] // LANES
     pairs = (
-        (lo_any, far_ref.at[:half]), (hi_any, far_ref.at[half:]), (hot_any, hot_ref),
-        (block_any, block_ref), (owner_any, owner_ref), (raw_any, raw_ref),
-        (limit_any, limit_ref), (m0, mix_ref.at[0]), (m1, mix_ref.at[1]), (m3, mix_ref.at[3]),
+        (limit_any, limit_ref), (m0, mix_ref.at[0]), (m1, mix_ref.at[1]), (m3, mix_ref.at[2]),
+        (hot_any, hot_ref), (block_any, block_ref), (owner_any, owner_ref),
     )
     copies = [pltpu.make_async_copy(a, b, sem.at[i]) for i, (a, b) in enumerate(pairs)]
     for cp in copies:
         cp.start()
-    for cp in copies[:7]:
-        cp.wait()
-    owner = owner_ref[:, 0:1]
+    here = here_ref[0]
     step = orbs * quota * halves
     lane = lax.broadcasted_iota(jnp.int32, (LANES, LANES), 1).astype(F32)
-    flat_ref[...] = raw_ref[...].astype(F32)
+    wide_ref[...] = raw_ref[...].astype(F32)
+    copies[0].wait()
     for o in range(orbs):
-        spread = jnp.dot(
-            far_ref[:, o * rows_block : (o + 1) * rows_block], hot_ref[o],
-            preferred_element_type=F32,
-        )
-        mix_ref[2, :, o * count : (o + 1) * count] = jnp.where(
-            owner == block_ref[o, 0:1, :], spread, 0.0
-        ).astype(BF)
         for q in range(quota):
             row = o * count + q * LANES
             for h in range(halves):
-                piece = flat_ref[pl.ds((o * quota + q) * halves + h, LANES, stride=step), :]
+                piece = wide_ref[pl.ds((o * quota + q) * halves + h, LANES, stride=step), :]
                 keep = lane + float(h * LANES) < limit_ref[row : row + LANES, :]
                 rows_ref[row : row + LANES, h * LANES : (h + 1) * LANES] = jnp.where(
                     keep, piece, 0.0
                 ).astype(BF)
-    for cp in copies[7:]:
+    for i, s in enumerate((0, 1, 3)):
+        copies[1 + i].wait()
+        scatter(quota, (here + s) % orbs, step, mix_ref[i], rows_ref, flat_ref)
+    for cp in copies[4:]:
         cp.wait()
-    for s in range(orbs):
-        done = jnp.dot(mix_ref[s], rows_ref[...], preferred_element_type=F32)
-        to = (here + s) % orbs
-        for q in range(quota):
-            for h in range(halves):
-                flat_ref[pl.ds((to * quota + q) * halves + h, LANES, stride=step), :] = done[
-                    q * LANES : (q + 1) * LANES, h * LANES : (h + 1) * LANES
-                ]
-    part = out_ref.shape[0] // CHUNKS
-    for j in range(CHUNKS):
-        rows = slice(j * part, (j + 1) * part)
-        out_ref[rows, :] = flat_ref[rows, :].astype(BF)
-        pltpu.make_async_copy(out_ref.at[rows], out_any.at[rows], sem.at[j]).start()
-    for j in range(CHUNKS):
-        rows = slice(j * part, (j + 1) * part)
-        pltpu.make_async_copy(out_ref.at[rows], out_any.at[rows], sem.at[j]).wait()
+
+
+def scatter(quota, to, step, mix, rows_ref, flat_ref):
+    halves = rows_ref.shape[1] // LANES
+    done = jnp.dot(mix, rows_ref[...], preferred_element_type=F32)
+    for q in range(quota):
+        for h in range(halves):
+            flat_ref[pl.ds((to * quota + q) * halves + h, LANES, stride=step), :] = done[
+                q * LANES : (q + 1) * LANES, h * LANES : (h + 1) * LANES
+            ]
+
+
+def close_body(
+    quota, here_ref, lo_ref, hi_ref, hot_ref, block_ref, owner_ref, rows_ref, flat_in,
+    out_ref, flat_ref, mix_ref,
+):
+    orbs, rows_block, count = hot_ref.shape
+    half = count // 2
+    step = orbs * quota * (rows_block // LANES)
+    for i, ref in enumerate((lo_ref, hi_ref)):
+        at = slice(i * half, (i + 1) * half)
+        owner = owner_ref[at, 0:1]
+        for o in range(orbs):
+            spread = jnp.dot(
+                ref[:, o * rows_block : (o + 1) * rows_block], hot_ref[o],
+                preferred_element_type=F32,
+            )
+            mix_ref[at, o * count : (o + 1) * count] = jnp.where(
+                owner == block_ref[o, 0:1, :], spread, 0.0
+            ).astype(BF)
+    scatter(quota, (here_ref[0] + 2) % orbs, step, mix_ref[...], rows_ref, flat_ref)
+    out_ref[...] = flat_ref[...].astype(BF)
 
 
 def finish_body(
-    orbs, quota, raw_any, amp_any, rec_ref, den_ref, out_any,
-    raw_ref, amp_ref, scale_ref, flat_ref, tile_ref, out_ref, sem_in, sem_out,
+    orbs, quota, raw_ref, amp_ref, rec_ref, den_ref, out_any,
+    scale_ref, flat_ref, tile_ref, out_ref, sem_out,
 ):
     rows, width = amp_ref.shape
     tiles = width // LANES
     halves = tiles // orbs
     part = rows // CHUNKS
     groups = part // quota
-    loads = []
-    for j in range(CHUNKS):
-        here = slice(j * part, (j + 1) * part)
-        to = slice(j * part * tiles, (j + 1) * part * tiles)
-        loads.append(pltpu.make_async_copy(raw_any.at[to], raw_ref.at[to], sem_in.at[0, j]))
-        loads.append(pltpu.make_async_copy(amp_any.at[here], amp_ref.at[here], sem_in.at[1, j]))
-    for cp in loads:
-        cp.start()
     spread_rows(rec_ref[...] / den_ref[...], scale_ref)
     stores = []
     for j in range(CHUNKS):
         here = slice(j * part, (j + 1) * part)
         to = slice(j * part * tiles, (j + 1) * part * tiles)
-        loads[2 * j].wait()
-        loads[2 * j + 1].wait()
         flat_ref[to, :] = raw_ref[to, :].astype(F32)
         for o in range(orbs):
             for q in range(quota):
@@ -268,31 +262,29 @@
     tiles = width // LANES
     return call(
         functools.partial(pack_body, orbs, quota),
-        jax.ShapeDtypeStruct((rows * tiles, LANES), BF),
-        [ANY, VM],
+        pltpu.HBM((rows * tiles, LANES), BF),
+        [VM, VM],
         ANY,
         [
-            pltpu.VMEM((rows, width), BF),
             pltpu.VMEM((rows, LANES), F32),
             pltpu.VMEM((tiles, rows, LANES), F32),
             pltpu.VMEM((rows * tiles, LANES), F32),
             pltpu.VMEM((rows * tiles, LANES), BF),
             pltpu.SemaphoreType.DMA((CHUNKS,)),
-            pltpu.SemaphoreType.DMA((CHUNKS,)),
         ],
         name="pack",
-    )(amplitudes, recoupling.reshape(rows // LANES, LANES))
+    )(near(amplitudes), recoupling.reshape(rows // LANES, LANES))
 
 
 def build(here, sizes, own, after, before, far, quota):
     count = quota * LANES
-    mixed = jax.ShapeDtypeStruct((count, 4 * count), BF)
+    mixed = pltpu.HBM((count, 4 * count), BF)
     outs = (
         mixed, mixed, mixed,
-        jax.ShapeDtypeStruct((4, own.shape[1] // 4, count), BF),
-        jax.ShapeDtypeStruct((4, 8, count), F32),
-        jax.ShapeDtypeStruct((count, LANES), F32),
-        jax.ShapeDtypeStruct((4 * count, LANES), F32),
+        pltpu.HBM((4, own.shape[1] // 4, count), BF),
+        pltpu.HBM((4, 8, count), F32),
+        pltpu.HBM((count, LANES), F32),
+        pltpu.HBM((4 * count, LANES), F32),
     )
     return call(
         functools.partial(build_body, quota),
@@ -304,28 +296,41 @@
     )(here, sizes, own, after, before, far)
 
 
-def cycle(here, raw, lo, hi, m0, m1, m3, hot, block, owner, limit, quota):
+def cycle(here, raw, m0, m1, m3, hot, block, owner, limit, quota):
     count = quota * LANES
     return call(
         functools.partial(cycle_body, quota),
-        jax.ShapeDtypeStruct(raw.shape, BF),
-        [SM] + [ANY] * 10,
-        ANY,
-        [
-            pltpu.VMEM(raw.shape, BF),
-            pltpu.VMEM((count, lo.shape[1]), BF),
+        (
+            pltpu.VMEM((4 * count, 2 * LANES), BF),
+            pltpu.VMEM(raw.shape, F32),
             pltpu.VMEM(hot.shape, BF),
             pltpu.VMEM(block.shape, F32),
             pltpu.VMEM(owner.shape, F32),
+        ),
+        [SM, VM] + [ANY] * 7,
+        (VM,) * 5,
+        [
+            pltpu.VMEM(raw.shape, F32),
             pltpu.VMEM(limit.shape, F32),
-            pltpu.VMEM((4, count, 4 * count), BF),
-            pltpu.VMEM(raw.shape, F32),
-            pltpu.VMEM((4 * count, hot.shape[1]), BF),
-            pltpu.VMEM(raw.shape, BF),
-            pltpu.SemaphoreType.DMA((10,)),
+            pltpu.VMEM((3, count, 4 * count), BF),
+            pltpu.SemaphoreType.DMA((7,)),
         ],
         name="cycle",
-    )(here, raw, lo, hi, hot, block, owner, limit, m0, m1, m3)
+    )(here, near(raw), limit, hot, block, owner, m0, m1, m3)
+
+
+def close(here, lo, hi, hot, block, owner, rows, flat, quota):
+    count = quota * LANES
+    out, _ = call(
+        functools.partial(close_body, quota),
+        (pltpu.VMEM(flat.shape, BF), pltpu.VMEM(flat.shape, F32)),
+        [SM] + [VM] * 7,
+        (VM, VM),
+        [pltpu.VMEM((count, 4 * count), BF)],
+        input_output_aliases={7: 1},
+        name="close",
+    )(here, lo, hi, near(hot), near(block), near(owner), near(rows), near(flat))
+    return out
 
 
 def finish(raw, amplitudes, recoupling, denominators, orbs, quota):
@@ -334,21 +339,18 @@
     return call(
         functools.partial(finish_body, orbs, quota),
         jax.ShapeDtypeStruct((rows, width), BF),
-        [ANY, ANY, VM, VM],
+        [VM, VM, VM, VM],
         ANY,
         [
-            pltpu.VMEM((rows * tiles, LANES), BF),
-            pltpu.VMEM((rows, width), BF),
             pltpu.VMEM((rows, LANES), F32),
             pltpu.VMEM((rows * tiles, LANES), F32),
             pltpu.VMEM((tiles, rows, LANES), F32),
             pltpu.VMEM((rows, width), BF),
-            pltpu.SemaphoreType.DMA((2, CHUNKS)),
             pltpu.SemaphoreType.DMA((CHUNKS,)),
         ],
         name="finish",
     )(
-        raw, amplitudes,
+        near(raw), near(amplitudes),
         recoupling.reshape(rows // LANES, LANES), denominators.reshape(rows // LANES, LANES),
     )
 
@@ -382,8 +384,13 @@
     lo = shift(after[:half], -1)
     hi = shift(before[half:count], 1)
     here = lax.axis_index("orb").astype(jnp.int32).reshape(1)
-    built = build(here, channel_sizes, own, after, before, far, quota)
-    back = cycle(here, raw, lo, hi, *built, quota)
+    m0, m1, m3, hot, block, owner, limit = build(
+        here, channel_sizes, own, after, before, far, quota
+    )
+    rows, flat, hot, block, owner = cycle(
+        here, raw, m0, m1, m3, hot, block, owner, limit, quota
+    )
+    back = close(here, lo, hi, hot, block, owner, rows, flat, quota)
     returned = exchange(back)
     return finish(returned, amplitudes, recoupling, denominators, orbs, quota)
 

time: 181 us -> 176 us (0.972)
  Pallas kernels: 30.6 us -> 23.5 us
  waiting for transfers between devices: 50.4 us -> 46.2 us
  blocking collectives: 55.7 us -> 59.2 us
  local copies, waits for them, and re-layouts: 3.77 us -> 6.69 us
    ppermute x5, waiting for transfers between devices: 50.4 us -> 46.2 us  [shift(): return lax.ppermute(x, 'orb', [(i, (i + by) % orbs) for i in range(orbs)])]
    unnamed x12 -> x24, local copies, waits for them, and re-layouts: 1.85 us -> 5.76 us
    all_to_all x1, blocking collectives: 55.7 us -> 59.2 us  [exchange(): x = lax.all_to_all(x, BOTH, split_axis=0, concat_axis=0, tiled=True)]
    pallas_call x1, Pallas kernels: 4.53 us -> 1.86 us  [pick(): call(functools.partial(pick_body, quota), jax.ShapeDtypeStruct((count + T...]
    pallas_call x1, Pallas kernels: 3.83 us -> 1.98 us  [finish(): call(functools.partial(finish_body, orbs, quota), jax.ShapeDtypeStruct((r...]
    pallas_call x2 -> x3, Pallas kernels: 13.8 us -> 12.3 us  [the longest x1 7.07 us: cycle(): call(functools.partial(cycle_body, quota), (pltpu.VMEM((4 * count, 2 * LA...]
  transfers between devices with their start and end apart: 6 -> 6, of which waited for: 2 -> 2; matrix products, arithmetic and copies ran while one was open for 1% -> 1% of each run, Pallas kernels for 5% -> 8%
where the time goes in v4:
time: 176 us; the launch traced here: 175 us
  blocking collectives  59.2 us (34%)
  waiting for transfers between devices  46.2 us (26%)
  starting transfers between devices  39.6 us (22%)
  Pallas kernels  23.5 us (13%)
  local copies, waits for them, and re-layouts  6.69 us (4%)
    all_to_all x1, blocking collectives, exchange(): x = lax.all_to_all(x, BOTH, split_axis=0, concat_axis=0, tiled=True)  59.2 us
    ppermute x5, waiting for transfers between devices, shift(): return lax.ppermute(x, 'orb', [(i, (i + by) % orbs) for i in range(orbs)])  46.2 us
    all_to_all x1, starting transfers between devices, exchange(): x = lax.all_to_all(x, BOTH, split_axis=0, concat_axis=0, tiled=True)  22.2 us
    ppermute x5, starting transfers between devices, shift(): return lax.ppermute(x, 'orb', [(i, (i + by) % orbs) for i in range(orbs)])  17.4 us
    pallas_call x1, Pallas kernels, build(): call(functools.partial(build_body, quota), outs, [SM, SM, VM, VM, VM, VM]...  7.36 us
    pallas_call x1, Pallas kernels, cycle(): call(functools.partial(cycle_body, quota), (pltpu.VMEM((4 * count, 2 * LA...  7.07 us
    unnamed x24, local copies, waits for them, and re-layouts  5.76 us
  transfers between devices with their start and end apart: 6, of which 2 were waited for; matrix products, arithmetic and copies ran while one was open for 1% of the time, Pallas kernels for 8%

profile of v4, /device:TPU:1, one launch (start us, length us, event | category | flops | bytes accessed | tf_op | source)
XLA Modules:
  0.0 175.4 jit_solution(3718881008256756653)
XLA Ops:
  0.0 0.0 copy-start
  0.0 1.3 copy-done
  1.3 0.0 copy-start.7
  1.3 0.7 copy-done.7
  2.0 0.0 copy-start.6
  2.0 0.0 copy-start.9
  2.0 1.8 %pack.1 = bf16[5120,128]{1,0:T(8,128)(2,1)} custom-call(bf16[640,1024]{1,0:T(8,128)(2,1)S(1)} %copy-done, f32[5,128]{1,0:T(8,128)S(1)} %bitcast.12), custom_call_target="tpu_custom_call" | custom-call | tf_op jit(solution)/shard_map/pack/pallas_call | solution.py:263
  3.8 0.0 copy-done.6
  3.8 0.0 copy-done.9
  3.8 1.9 %pick.1.own_ref = bf16[656,1024]{1,0:T(8,128)(2,1)S(1)} custom-call(s32[4,256]{1,0:T(4,128)S(1)} %copy-done.9, bf16[1024,1024]{1,0:T(8,128)(2,1)S(1)} %bitcast.10), custom_call_target="tpu_custom_call" | custom-call | tf_op jit(solution)/shard_map/pick/pallas_call | solution.py:250
  5.7 22.2 %all-to-all-start = ((bf16[512,5,2,128]{3,2,1,0:T(2,128)(2,1)}), bf16[512,5,2,128]{3,2,1,0:T(2,128)(2,1)S(1)}, u32[]{:S(2)}, u32[]{:S(2)}) async-start(bf16[512,5,2,128]{3,2,1,0:T(2,128)(2,1)} %bitcast.15), calls=%async_computation | async-start | bytes 2621440 | tf_op jit(solution)/shard_map/all_to_all | solution.py:375
  27.8 0.0 copy-start.11
  27.8 3.3 %collective-permute-start.2 = (bf16[656,1024]{1,0:T(8,128)(2,1)S(1)}, bf16[656,1024]{1,0:T(8,128)(2,1)S(1)}, u32[]{:S(2)}, u32[]{:S(2)}) collective-permute-start(bf16[656,1024]{1,0:T(8,128)(2,1)S(1)} %pick.1.own_ref), channel_id=1, source_target_pairs={{0,1},{1,2},{2,3},{3,0},{4,5},{5,6},{6,7},{7,4},{8,9},{9,10},{10,1... | collective-permute-start | bytes 4030472 | tf_op jit(solution)/shard_map/ppermute | solution.py:371
  31.1 3.2 %collective-permute-start = (bf16[656,1024]{1,0:T(8,128)(2,1)S(1)}, bf16[656,1024]{1,0:T(8,128)(2,1)S(1)}, u32[]{:S(2)}, u32[]{:S(2)}) collective-permute-start(bf16[656,1024]{1,0:T(8,128)(2,1)S(1)} %pick.1.own_ref), channel_id=1, source_target_pairs={{0,3},{1,0},{2,1},{3,2},{4,7},{5,4},{6,5},{7,6},{8,11},{9,8},{10,9... | collective-permute-start | bytes 4030472 | tf_op jit(solution)/shard_map/ppermute | solution.py:371
  34.3 38.5 %collective-permute-done.2.before_ref = bf16[656,1024]{1,0:T(8,128)(2,1)S(1)} collective-permute-done((bf16[656,1024]{1,0:T(8,128)(2,1)S(1)}, bf16[656,1024]{1,0:T(8,128)(2,1)S(1)}, u32[]{:S(2)}, u32[]{:S(2)}) %collective-permute-start.2) | collective-permute-done | bytes 1343520 | tf_op jit(solution)/shard_map/ppermute | solution.py:371
  72.8 0.0 copy-start.2
  72.9 2.9 %collective-permute-start.3 = (bf16[320,1024]{1,0:T(8,128)(2,1)S(1)}, bf16[320,1024]{1,0:T(8,128)(2,1)}, u32[]{:S(2)}, u32[]{:S(2)}) collective-permute-start(bf16[320,1024]{1,0:T(8,128)(2,1)S(1)} %slice.13), channel_id=1, source_target_pairs={{0,1},{1,2},{2,3},{3,0},{4,5},{5,6},{6,7},{7,4},{8,9},{9,10},{10,1... | collective-permute-start | bytes 1966088 | tf_op jit(solution)/shard_map/ppermute | solution.py:371
  75.8 0.0 collective-permute-done.after_ref
  75.8 0.9 slice.12
  76.7 0.0 copy-done.2
  76.7 0.0 copy-start.4
  76.7 1.1 copy-done.4
  77.8 4.2 %collective-permute-start.1 = (bf16[320,1024]{1,0:T(8,128)(2,1)}, bf16[320,1024]{1,0:T(8,128)(2,1)}, u32[]{:S(2)}, u32[]{:S(2)}) collective-permute-start(bf16[320,1024]{1,0:T(8,128)(2,1)} %slice.12), channel_id=1, source_target_pairs={{0,3},{1,0},{2,1},{3,2},{4,7},{5,4},{6,5},{7,6},{8,11},{9,8},{10,9... | collective-permute-start | bytes 1966088 | tf_op jit(solution)/shard_map/ppermute | solution.py:371
  82.0 3.8 %collective-permute-start.4 = (bf16[16,1024]{1,0:T(8,128)(2,1)S(1)}, bf16[16,1024]{1,0:T(8,128)(2,1)S(1)}, u32[]{:S(2)}, u32[]{:S(2)}) collective-permute-start(bf16[16,1024]{1,0:T(8,128)(2,1)S(1)} %slice.14), channel_id=1, source_target_pairs={{0,2},{1,3},{2,0},{3,1},{4,6},{5,7},{6,4},{7,5},{8,10},{9,11},{10,... | collective-permute-start | bytes 98312 | tf_op jit(solution)/shard_map/ppermute | solution.py:371
  85.8 7.7 %collective-permute-done.4.far_ref = bf16[16,1024]{1,0:T(8,128)(2,1)S(1)} collective-permute-done((bf16[16,1024]{1,0:T(8,128)(2,1)S(1)}, bf16[16,1024]{1,0:T(8,128)(2,1)S(1)}, u32[]{:S(2)}, u32[]{:S(2)}) %collective-permute-start.4) | collective-permute-done | bytes 32800 | tf_op jit(solution)/shard_map/ppermute | solution.py:371
  93.5 0.0 copy-done.11
  93.5 0.0 copy-start.3
  93.5 1.3 copy-done.3
  94.8 0.0 copy-start.5
  94.8 1.3 copy-done.5
  96.1 7.4 %build.1 = (bf16[640,2560]{1,0:T(8,128)(2,1)}, bf16[640,2560]{1,0:T(8,128)(2,1)}, bf16[640,2560]{1,0:T(8,128)(2,1)}, bf16[4,256,640]{2,1,0:T(8,128)(2,1)}, f32[4...) custom-call(s32[1]{0:T(128)} %bitcast.here_ref, s32[4]{0:T(128)S(1)} %copy-done.11, ...), custom_call_target="tpu_custom_call" | custom-call | tf_op jit(solution)/shard_map/build/pallas_call | solution.py:289
  103.5 0.0 all-to-all-done
  103.5 7.1 %cycle.1 = (bf16[2560,256]{1,0:T(8,128)(2,1)S(1)}, f32[5120,128]{1,0:T(8,128)S(1)}, bf16[4,256,640]{2,1,0:T(8,128)(2,1)S(1)}, f32[4,8,640]{2,1,0:T(8,128)S(1)}, f32[640,128]{1,0:T(8,128)S(1)}) custom-call(s32[1]{0:T(128)} %bitcast.here_ref, bf16[5120,128]{1,0:T(8,128)(2,1)S(1)} %bitcast.8, f32[2560,128]{1,0:T(8,128)} %get-tuple-element.20.limit_any, ...), custom_call_target="tpu_custom_call" | custom-call | tf_op jit(solution)/shard_map/cycle/pallas_call | solution.py:301
  110.6 0.0 collective-permute-done.3.hi_ref
  110.6 0.0 collective-permute-done.1.lo_ref
  110.6 3.5 %close.1 = (bf16[5120,128]{1,0:T(8,128)(2,1)S(1)}, f32[5120,128]{1,0:T(8,128)S(1)}) custom-call(s32[1]{0:T(128)} %bitcast.here_ref, bf16[320,1024]{1,0:T(8,128)(2,1)} %collective-permute-done.1.lo_ref, bf16[320,1024]{1,0:T(8,128)(2,1)} %collective-permute-done.3.hi_ref, ...), custom_call_target="tpu_custom_call", output_to_operand_aliasing={{1}: (7, {})} | custom-call | tf_op jit(solution)/shard_map/close/pallas_call | solution.py:324
  114.1 0.0 copy-start.1
  114.1 0.0 copy-start.8
  114.1 0.0 copy-start.10
  114.1 59.2 %all_to_all.10 = bf16[512,5,2,128]{3,2,1,0:T(2,128)(2,1)S(1)} all-to-all(bf16[512,5,2,128]{3,2,1,0:T(2,128)(2,1)S(1)} %bitcast.11), channel_id=1, replica_groups=mesh['chan'=128,'orb'=4] {'chan','orb'}, dimensions={0} | all-to-all | bytes 2621440 | tf_op jit(solution)/shard_map/all_to_all | solution.py:375
  173.3 0.0 copy-done.1
  173.3 0.0 copy-done.8
  173.3 0.0 copy-done.10
  173.3 2.0 %finish.1 = bf16[640,1024]{1,0:T(8,128)(2,1)} custom-call(bf16[5120,128]{1,0:T(8,128)(2,1)S(1)} %bitcast.9, bf16[640,1024]{1,0:T(8,128)(2,1)S(1)} %copy-done.1, f32[5,128]{1,0:T(8,128)S(1)} %bitcast.13, f32[5,128]{1,0:T(8,128)S(1)} %bitcast.14), custom_call_target="tpu_custom_call" | custom-call | tf_op jit(solution)/shard_map/finish/pallas_call | solution.py:339
  (2 shorter events, 0.0 us)
Async XLA Ops:
  0.0 1.3 copy-start
  1.3 0.7 copy-start.7
  2.0 1.8 %copy-start.6 = (bf16[4,256,1024]{2,1,0:T(8,128)(2,1)S(1)}, bf16[4,256,1024]{2,1,0:T(8,128)(2,1)}, u32[]{:S(2)}) copy-start(bf16[4,256,1024]{2,1,0:T(8,128)(2,1)} %param.10) | copy-start | bytes 6291460
  2.0 1.8 %copy-start.9 = (s32[4,256]{1,0:T(4,128)S(1)}, s32[4,256]{1,0:T(4,128)}, u32[]{:S(2)}) copy-start(s32[4,256]{1,0:T(4,128)} %src_ref.1) | copy-start | bytes 12292
  5.7 97.8 %all-to-all-start = ((bf16[512,5,2,128]{3,2,1,0:T(2,128)(2,1)}), bf16[512,5,2,128]{3,2,1,0:T(2,128)(2,1)S(1)}, u32[]{:S(2)}, u32[]{:S(2)}) async-start(bf16[512,5,2,128]{3,2,1,0:T(2,128)(2,1)} %bitcast.15), calls=%async_computation | async-start | bytes 2621440 | tf_op jit(solution)/shard_map/all_to_all | solution.py:375
  27.8 65.7 %copy-start.11 = (s32[4]{0:T(128)S(1)}, s32[4]{0:T(128)}, u32[]{:S(2)}) copy-start(s32[4]{0:T(128)} %size_ref.1) | copy-start | bytes 52
  27.8 45.0 %collective-permute-start.2 = (bf16[656,1024]{1,0:T(8,128)(2,1)S(1)}, bf16[656,1024]{1,0:T(8,128)(2,1)S(1)}, u32[]{:S(2)}, u32[]{:S(2)}) collective-permute-start(bf16[656,1024]{1,0:T(8,128)(2,1)S(1)} %pick.1.own_ref), channel_id=1, source_target_pairs={{0,1},{1,2},{2,3},{3,0},{4,5},{5,6},{6,7},{7,4},{8,9},{9,10},{10,1... | collective-permute-start | bytes 4030472 | tf_op jit(solution)/shard_map/ppermute | solution.py:371
  31.1 44.7 %collective-permute-start = (bf16[656,1024]{1,0:T(8,128)(2,1)S(1)}, bf16[656,1024]{1,0:T(8,128)(2,1)S(1)}, u32[]{:S(2)}, u32[]{:S(2)}) collective-permute-start(bf16[656,1024]{1,0:T(8,128)(2,1)S(1)} %pick.1.own_ref), channel_id=1, source_target_pairs={{0,3},{1,0},{2,1},{3,2},{4,7},{5,4},{6,5},{7,6},{8,11},{9,8},{10,9... | collective-permute-start | bytes 4030472 | tf_op jit(solution)/shard_map/ppermute | solution.py:371
  72.8 3.9 %copy-start.2 = (bf16[656,1024]{1,0:T(8,128)(2,1)}, bf16[656,1024]{1,0:T(8,128)(2,1)S(1)}, u32[]{:S(2)}) copy-start(bf16[656,1024]{1,0:T(8,128)(2,1)S(1)} %collective-permute-done.2.before_ref) | copy-start | bytes 4030468
  72.9 37.7 %collective-permute-start.3 = (bf16[320,1024]{1,0:T(8,128)(2,1)S(1)}, bf16[320,1024]{1,0:T(8,128)(2,1)}, u32[]{:S(2)}, u32[]{:S(2)}) collective-permute-start(bf16[320,1024]{1,0:T(8,128)(2,1)S(1)} %slice.13), channel_id=1, source_target_pairs={{0,1},{1,2},{2,3},{3,0},{4,5},{5,6},{6,7},{7,4},{8,9},{9,10},{10,1... | collective-permute-start | bytes 1966088 | tf_op jit(solution)/shard_map/ppermute | solution.py:371
  76.7 1.1 copy-start.4
  77.8 32.8 %collective-permute-start.1 = (bf16[320,1024]{1,0:T(8,128)(2,1)}, bf16[320,1024]{1,0:T(8,128)(2,1)}, u32[]{:S(2)}, u32[]{:S(2)}) collective-permute-start(bf16[320,1024]{1,0:T(8,128)(2,1)} %slice.12), channel_id=1, source_target_pairs={{0,3},{1,0},{2,1},{3,2},{4,7},{5,4},{6,5},{7,6},{8,11},{9,8},{10,9... | collective-permute-start | bytes 1966088 | tf_op jit(solution)/shard_map/ppermute | solution.py:371
  82.0 11.5 %collective-permute-start.4 = (bf16[16,1024]{1,0:T(8,128)(2,1)S(1)}, bf16[16,1024]{1,0:T(8,128)(2,1)S(1)}, u32[]{:S(2)}, u32[]{:S(2)}) collective-permute-start(bf16[16,1024]{1,0:T(8,128)(2,1)S(1)} %slice.14), channel_id=1, source_target_pairs={{0,2},{1,3},{2,0},{3,1},{4,6},{5,7},{6,4},{7,5},{8,10},{9,11},{10,... | collective-permute-start | bytes 98312 | tf_op jit(solution)/shard_map/ppermute | solution.py:371
  93.5 1.3 copy-start.3
  94.8 1.3 copy-start.5
  114.1 59.2 %copy-start.1 = (bf16[640,1024]{1,0:T(8,128)(2,1)S(1)}, bf16[640,1024]{1,0:T(8,128)(2,1)}, u32[]{:S(2)}) copy-start(bf16[640,1024]{1,0:T(8,128)(2,1)} %amp_ref.3) | copy-start | bytes 3932164
  114.1 59.2 %copy-start.8 = (f32[640]{0:T(1024)S(1)}, f32[640]{0:T(1024)}, u32[]{:S(2)}) copy-start(f32[640]{0:T(1024)} %param.8) | copy-start | bytes 7684
  114.1 59.2 %copy-start.10 = (f32[640]{0:T(1024)S(1)}, f32[640]{0:T(1024)}, u32[]{:S(2)}) copy-start(f32[640]{0:T(1024)} %param.9) | copy-start | bytes 7684

commit v5 on v4

--- a/solution.py
+++ b/solution.py
@@ -37,6 +37,10 @@
     return pltpu.with_memory_space_constraint(x, pltpu.VMEM)
 
 
+def apart(x):
+    return pltpu.with_memory_space_constraint(x, pltpu.HBM)
+
+
 def one_hot(hit):
     return jnp.where(hit, 1.0, 0.0).astype(BF)
 
@@ -47,10 +51,18 @@
     return jnp.transpose(tall)
 
 
-def pick_body(quota, src_ref, w_ref, out_ref, hit_ref):
+def pick_body(quota, src_any, w_any, out_ref, src_ref, w_ref, hit_ref, sem_src, sem_w):
     blocks, rows_block = src_ref.shape
     states, width = w_ref.shape
     count = quota * LANES
+    index = pltpu.make_async_copy(src_any, src_ref, sem_src)
+    index.start()
+    loads = []
+    for c in range(blocks):
+        at = slice(c * rows_block, (c + 1) * rows_block)
+        loads.append(pltpu.make_async_copy(w_any.at[at], w_ref.at[at], sem_w.at[c]))
+        loads[c].start()
+    index.wait()
     src = jnp.concatenate([src_ref[c : c + 1, :] for c in range(blocks)], axis=1)
     sender = (src * 205) >> 10
     place = jnp.where(src >= 0, (src - sender * quota) * LANES + sender, -1)
@@ -67,6 +79,8 @@
         out_ref[count:, here] = lax.dot_general(
             labels, hit, (((1,), (1,)), ((), ())), preferred_element_type=F32
         ).astype(BF)
+    for cp in loads:
+        cp.wait()
     out_ref[:count, :] = jnp.dot(
         hit_ref[...], w_ref[...], preferred_element_type=F32
     ).astype(BF)
@@ -110,19 +124,45 @@
         cp.wait()
 
 
-def build_body(
-    quota, here_ref, size_ref, own_ref, after_ref, before_ref, far_ref,
-    m0, m1, m3, hot_ref, block_ref, owner_ref, limit_ref, tags_ref,
-):
-    count = quota * LANES
-    rows_block = hot_ref.shape[1]
-    orbs = hot_ref.shape[0]
-    refs = (own_ref, after_ref, None, before_ref)
-    for s, ref in enumerate(refs):
-        tag = far_ref[:, :count] if ref is None else ref[count:, :count]
-        tags_ref[s] = tag.astype(F32)
+def mix(w, hot_ref, block_ref, owner, out_ref):
+    orbs, rows_block, count = hot_ref.shape
+    for o in range(orbs):
+        spread = jnp.dot(
+            w[:, o * rows_block : (o + 1) * rows_block], hot_ref[o], preferred_element_type=F32
+        )
+        out_ref[:, o * count : (o + 1) * count] = jnp.where(
+            owner == block_ref[o, 0:1, :], spread, 0.0
+        ).astype(BF)
+
+
+def cycle_body(
+    quota, here_ref, size_ref, raw_ref, far_ref, own_any, after_any, before_any,
+    rows_ref, flat_ref, hot_ref, block_ref, owner_ref,
+    wide_ref, tag_ref, tags_ref, w_ref, mix_ref, sem_tag, sem_w,
+):
+    orbs, rows_block, count = hot_ref.shape
+    halves = rows_block // LANES
+    sources = (own_any, after_any, before_any)
+    tag_copies = [
+        pltpu.make_async_copy(src.at[count:], tag_ref.at[i], sem_tag.at[i])
+        for i, src in enumerate(sources)
+    ]
+    copies = [
+        pltpu.make_async_copy(src.at[:count], w_ref.at[i], sem_w.at[i])
+        for i, src in enumerate(sources)
+    ]
+    for cp in tag_copies + copies:
+        cp.start()
     here = here_ref[0]
+    step = orbs * quota * halves
+    lane = lax.broadcasted_iota(jnp.int32, (LANES, LANES), 1).astype(F32)
     slot = lax.broadcasted_iota(jnp.int32, (rows_block, count), 0).astype(F32)
+    wide_ref[...] = raw_ref[...].astype(F32)
+    for cp in tag_copies:
+        cp.wait()
+    tags_ref[2] = far_ref[:, :count].astype(F32)
+    for i, s in enumerate((0, 1, 3)):
+        tags_ref[s] = tag_ref[i, :, :count].astype(F32)
     for o in range(orbs):
         tag = tags_ref[(o + orbs - here) % orbs]
         hot_ref[o] = one_hot(slot == tag[1:2, :])
@@ -131,53 +171,20 @@
         for c in range(size_ref.shape[0]):
             live = (size_ref[c] // orbs).astype(F32)
             size = size + jnp.where(tag[0:1, :] == float(c), live, 0.0)
-        limit_ref[o * count : (o + 1) * count, :] = jnp.broadcast_to(
-            column(size)[:, 0:1], (count, LANES)
-        )
-    owner_ref[...] = jnp.broadcast_to(column(tags_ref[2])[:, 0:1], (count, LANES))
-    for s, out in ((0, m0), (1, m1), (3, m3)):
-        owner = column(tags_ref[s])[:, 0:1]
-        for o in range(orbs):
-            part = refs[s][:count, o * rows_block : (o + 1) * rows_block]
-            spread = jnp.dot(part, hot_ref[o], preferred_element_type=F32)
-            out[:, o * count : (o + 1) * count] = jnp.where(
-                owner == block_ref[o, 0:1, :], spread, 0.0
-            ).astype(BF)
-
-
-def cycle_body(
-    quota, here_ref, raw_ref, limit_any, hot_any, block_any, owner_any, m0, m1, m3,
-    rows_ref, flat_ref, hot_ref, block_ref, owner_ref, wide_ref, limit_ref, mix_ref, sem,
-):
-    count = m0.shape[0]
-    orbs = m0.shape[1] // count
-    halves = rows_ref.shape[1] // LANES
-    pairs = (
-        (limit_any, limit_ref), (m0, mix_ref.at[0]), (m1, mix_ref.at[1]), (m3, mix_ref.at[2]),
-        (hot_any, hot_ref), (block_any, block_ref), (owner_any, owner_ref),
-    )
-    copies = [pltpu.make_async_copy(a, b, sem.at[i]) for i, (a, b) in enumerate(pairs)]
-    for cp in copies:
-        cp.start()
-    here = here_ref[0]
-    step = orbs * quota * halves
-    lane = lax.broadcasted_iota(jnp.int32, (LANES, LANES), 1).astype(F32)
-    wide_ref[...] = raw_ref[...].astype(F32)
-    copies[0].wait()
-    for o in range(orbs):
+        size = column(size)[:, 0:1]
         for q in range(quota):
             row = o * count + q * LANES
             for h in range(halves):
                 piece = wide_ref[pl.ds((o * quota + q) * halves + h, LANES, stride=step), :]
-                keep = lane + float(h * LANES) < limit_ref[row : row + LANES, :]
+                keep = lane + float(h * LANES) < size[q * LANES : (q + 1) * LANES]
                 rows_ref[row : row + LANES, h * LANES : (h + 1) * LANES] = jnp.where(
                     keep, piece, 0.0
                 ).astype(BF)
+    owner_ref[...] = jnp.broadcast_to(column(tags_ref[2])[:, 0:1], (count, LANES))
     for i, s in enumerate((0, 1, 3)):
-        copies[1 + i].wait()
+        copies[i].wait()
+        mix(w_ref.at[i], hot_ref, block_ref, column(tags_ref[s])[:, 0:1], mix_ref.at[i])
         scatter(quota, (here + s) % orbs, step, mix_ref[i], rows_ref, flat_ref)
-    for cp in copies[4:]:
-        cp.wait()
 
 
 def scatter(quota, to, step, mix, rows_ref, flat_ref):
@@ -199,15 +206,7 @@
     step = orbs * quota * (rows_block // LANES)
     for i, ref in enumerate((lo_ref, hi_ref)):
         at = slice(i * half, (i + 1) * half)
-        owner = owner_ref[at, 0:1]
-        for o in range(orbs):
-            spread = jnp.dot(
-                ref[:, o * rows_block : (o + 1) * rows_block], hot_ref[o],
-                preferred_element_type=F32,
-            )
-            mix_ref[at, o * count : (o + 1) * count] = jnp.where(
-                owner == block_ref[o, 0:1, :], spread, 0.0
-            ).astype(BF)
+        mix(ref, hot_ref, block_ref, owner_ref[at, 0:1], mix_ref.at[at])
     scatter(quota, (here_ref[0] + 2) % orbs, step, mix_ref[...], rows_ref, flat_ref)
     out_ref[...] = flat_ref[...].astype(BF)
 
@@ -249,12 +248,18 @@
     states = blocks * rows_block
     return call(
         functools.partial(pick_body, quota),
-        jax.ShapeDtypeStruct((count + TAGS, width), BF),
-        [VM, VM],
+        pltpu.VMEM((count + TAGS, width), BF),
+        [ANY, ANY],
         VM,
-        [pltpu.VMEM((count, states), BF)],
+        [
+            pltpu.VMEM((blocks, rows_block), jnp.int32),
+            pltpu.VMEM((states, width), BF),
+            pltpu.VMEM((count, states), BF),
+            pltpu.SemaphoreType.DMA,
+            pltpu.SemaphoreType.DMA((blocks,)),
+        ],
         name="pick",
-    )(pair_source, interaction.reshape(states, width))
+    )(apart(pair_source), apart(interaction.reshape(states, width)))
 
 
 def pack(amplitudes, recoupling, orbs, quota):
@@ -276,47 +281,31 @@
     )(near(amplitudes), recoupling.reshape(rows // LANES, LANES))
 
 
-def build(here, sizes, own, after, before, far, quota):
-    count = quota * LANES
-    mixed = pltpu.HBM((count, 4 * count), BF)
-    outs = (
-        mixed, mixed, mixed,
-        pltpu.HBM((4, own.shape[1] // 4, count), BF),
-        pltpu.HBM((4, 8, count), F32),
-        pltpu.HBM((count, LANES), F32),
-        pltpu.HBM((4 * count, LANES), F32),
-    )
-    return call(
-        functools.partial(build_body, quota),
-        outs,
-        [SM, SM, VM, VM, VM, VM],
-        (VM,) * len(outs),
-        [pltpu.VMEM((4, TAGS, count), F32)],
-        name="build",
-    )(here, sizes, own, after, before, far)
-
-
-def cycle(here, raw, m0, m1, m3, hot, block, owner, limit, quota):
-    count = quota * LANES
+def cycle(here, sizes, raw, far, own, after, before, quota):
+    count = quota * LANES
+    width = own.shape[1]
     return call(
         functools.partial(cycle_body, quota),
         (
             pltpu.VMEM((4 * count, 2 * LANES), BF),
             pltpu.VMEM(raw.shape, F32),
-            pltpu.VMEM(hot.shape, BF),
-            pltpu.VMEM(block.shape, F32),
-            pltpu.VMEM(owner.shape, F32),
+            pltpu.VMEM((4, 2 * LANES, count), BF),
+            pltpu.VMEM((4, 8, count), F32),
+            pltpu.VMEM((count, LANES), F32),
         ),
-        [SM, VM] + [ANY] * 7,
+        [SM, SM, VM, VM] + [ANY] * 3,
         (VM,) * 5,
         [
             pltpu.VMEM(raw.shape, F32),
-            pltpu.VMEM(limit.shape, F32),
+            pltpu.VMEM((3, TAGS, width), BF),
+            pltpu.VMEM((4, TAGS, count), F32),
+            pltpu.VMEM((3, count, width), BF),
             pltpu.VMEM((3, count, 4 * count), BF),
-            pltpu.SemaphoreType.DMA((7,)),
+            pltpu.SemaphoreType.DMA((3,)),
+            pltpu.SemaphoreType.DMA((3,)),
         ],
         name="cycle",
-    )(here, near(raw), limit, hot, block, owner, m0, m1, m3)
+    )(here, sizes, near(raw), near(far), own, after, before)
 
 
 def close(here, lo, hi, hot, block, owner, rows, flat, quota):
@@ -329,7 +318,7 @@
         [pltpu.VMEM((count, 4 * count), BF)],
         input_output_aliases={7: 1},
         name="close",
-    )(here, lo, hi, near(hot), near(block), near(owner), near(rows), near(flat))
+    )(here, apart(lo), apart(hi), near(hot), near(block), near(owner), near(rows), near(flat))
     return out
 
 
@@ -384,11 +373,8 @@
     lo = shift(after[:half], -1)
     hi = shift(before[half:count], 1)
     here = lax.axis_index("orb").astype(jnp.int32).reshape(1)
-    m0, m1, m3, hot, block, owner, limit = build(
-        here, channel_sizes, own, after, before, far, quota
-    )
     rows, flat, hot, block, owner = cycle(
-        here, raw, m0, m1, m3, hot, block, owner, limit, quota
+        here, channel_sizes, raw, far, own, after, before, quota
     )
     back = close(here, lo, hi, hot, block, owner, rows, flat, quota)
     returned = exchange(back)

time: 176 us -> 171 us (0.972)
  local copies, waits for them, and re-layouts: 6.69 us -> 1.01 us
  waiting for transfers between devices: 46.2 us -> 50.8 us
  blocking collectives: 59.2 us -> 54.8 us
    pallas_call x2 -> x1, Pallas kernels: 9.22 us -> 3.44 us  [pick(): call(functools.partial(pick_body, quota), pltpu.VMEM((count + TAGS, width...]
    unnamed x24 -> x12, local copies, waits for them, and re-layouts: 5.76 us -> 0.03 us
    pallas_call x1, Pallas kernels: 7.07 us -> 12.4 us  [cycle(): call(functools.partial(cycle_body, quota), (pltpu.VMEM((4 * count, 2 * LA...]
    ppermute x5, waiting for transfers between devices: 46.2 us -> 50.8 us  [shift(): return lax.ppermute(x, 'orb', [(i, (i + by) % orbs) for i in range(orbs)])]
    all_to_all x1, blocking collectives: 59.2 us -> 54.8 us  [exchange(): x = lax.all_to_all(x, BOTH, split_axis=0, concat_axis=0, tiled=True)]
    all_to_all x1, starting transfers between devices: 22.2 us -> 24 us  [exchange(): x = lax.all_to_all(x, BOTH, split_axis=0, concat_axis=0, tiled=True)]
  transfers between devices with their start and end apart: 6 -> 6, of which waited for: 2 -> 2; matrix products, arithmetic and copies ran while one was open for 1% -> 1% of each run, Pallas kernels for 8% -> 7%
where the time goes in v5:
time: 171 us
  blocking collectives  54.8 us (32%)
  waiting for transfers between devices  50.8 us (30%)
  starting transfers between devices  40.9 us (24%)
  Pallas kernels  23.1 us (14%)
    all_to_all x1, blocking collectives, exchange(): x = lax.all_to_all(x, BOTH, split_axis=0, concat_axis=0, tiled=True)  54.8 us
    ppermute x5, waiting for transfers between devices, shift(): return lax.ppermute(x, 'orb', [(i, (i + by) % orbs) for i in range(orbs)])  50.8 us
    all_to_all x1, starting transfers between devices, exchange(): x = lax.all_to_all(x, BOTH, split_axis=0, concat_axis=0, tiled=True)  24 us
    ppermute x5, starting transfers between devices, shift(): return lax.ppermute(x, 'orb', [(i, (i + by) % orbs) for i in range(orbs)])  16.9 us
    pallas_call x1, Pallas kernels, cycle(): call(functools.partial(cycle_body, quota), (pltpu.VMEM((4 * count, 2 * LA...  12.4 us
    pallas_call x1, Pallas kernels, close(): call(functools.partial(close_body, quota), (pltpu.VMEM(flat.shape, BF), p...  3.49 us
    pallas_call x1, Pallas kernels, pick(): call(functools.partial(pick_body, quota), pltpu.VMEM((count + TAGS, width...  3.44 us
  transfers between devices with their start and end apart: 6, of which 2 were waited for; matrix products, arithmetic and copies ran while one was open for 1% of the time, Pallas kernels for 7%

profile of v5, /device:TPU:1, one launch (start us, length us, event | category | flops | bytes accessed | tf_op | source)
XLA Modules:
  0.0 170.9 jit_solution(4997420163619203307)
XLA Ops:
  0.0 0.0 copy-start.1
  0.0 0.0 copy-start.2
  0.0 3.4 %pick.1.own_any = bf16[656,1024]{1,0:T(8,128)(2,1)S(1)} custom-call(s32[4,256]{1,0:T(4,128)} %src_any.1, bf16[1024,1024]{1,0:T(8,128)(2,1)} %bitcast.14), custom_call_target="tpu_custom_call" | custom-call | tf_op jit(solution)/shard_map/pick/pallas_call | solution.py:249
  3.4 0.0 copy-start
  3.5 0.0 copy-done.1
  3.5 0.0 copy-done.2
  3.5 1.8 %pack.1 = bf16[5120,128]{1,0:T(8,128)(2,1)} custom-call(bf16[640,1024]{1,0:T(8,128)(2,1)S(1)} %copy-done.1, f32[5,128]{1,0:T(8,128)S(1)} %bitcast.10), custom_call_target="tpu_custom_call" | custom-call | tf_op jit(solution)/shard_map/pack/pallas_call | solution.py:268
  5.2 24.0 %all-to-all-start = ((bf16[512,5,2,128]{3,2,1,0:T(2,128)(2,1)}), bf16[512,5,2,128]{3,2,1,0:T(2,128)(2,1)}, u32[]{:S(2)}, u32[]{:S(2)}) async-start(bf16[512,5,2,128]{3,2,1,0:T(2,128)(2,1)} %bitcast.13), calls=%async_computation | async-start | bytes 2621440 | tf_op jit(solution)/shard_map/all_to_all | solution.py:364
  29.2 4.5 %collective-permute-start = (bf16[656,1024]{1,0:T(8,128)(2,1)S(1)}, bf16[656,1024]{1,0:T(8,128)(2,1)S(1)}, u32[]{:S(2)}, u32[]{:S(2)}) collective-permute-start(bf16[656,1024]{1,0:T(8,128)(2,1)S(1)} %pick.1.own_any), channel_id=1, source_target_pairs={{0,3},{1,0},{2,1},{3,2},{4,7},{5,4},{6,5},{7,6},{8,11},{9,8},{10,9... | collective-permute-start | bytes 4030472 | tf_op jit(solution)/shard_map/ppermute | solution.py:360
  33.7 1.9 %collective-permute-start.2 = (bf16[656,1024]{1,0:T(8,128)(2,1)S(1)}, bf16[656,1024]{1,0:T(8,128)(2,1)S(1)}, u32[]{:S(2)}, u32[]{:S(2)}) collective-permute-start(bf16[656,1024]{1,0:T(8,128)(2,1)S(1)} %pick.1.own_any), channel_id=1, source_target_pairs={{0,1},{1,2},{2,3},{3,0},{4,5},{5,6},{6,7},{7,4},{8,9},{9,10},{10,1... | collective-permute-start | bytes 4030472 | tf_op jit(solution)/shard_map/ppermute | solution.py:360
  35.6 38.6 %collective-permute-done.after_any = bf16[656,1024]{1,0:T(8,128)(2,1)S(1)} collective-permute-done((bf16[656,1024]{1,0:T(8,128)(2,1)S(1)}, bf16[656,1024]{1,0:T(8,128)(2,1)S(1)}, u32[]{:S(2)}, u32[]{:S(2)}) %collective-permute-start) | collective-permute-done | bytes 1343520 | tf_op jit(solution)/shard_map/ppermute | solution.py:360
  74.3 0.0 copy-start.4
  74.3 5.3 %collective-permute-start.1 = (bf16[320,1024]{1,0:T(8,128)(2,1)S(1)}, bf16[320,1024]{1,0:T(8,128)(2,1)}, u32[]{:S(2)}, u32[]{:S(2)}) collective-permute-start(bf16[320,1024]{1,0:T(8,128)(2,1)S(1)} %slice.12), channel_id=1, source_target_pairs={{0,3},{1,0},{2,1},{3,2},{4,7},{5,4},{6,5},{7,6},{8,11},{9,8},{10,9... | collective-permute-start | bytes 1966088 | tf_op jit(solution)/shard_map/ppermute | solution.py:360
  79.6 0.0 collective-permute-done.2.before_any
  79.6 0.0 copy-start.5
  79.7 0.9 slice.13
  80.6 0.0 copy-done.4
  80.6 1.9 %collective-permute-start.3 = (bf16[320,1024]{1,0:T(8,128)(2,1)}, bf16[320,1024]{1,0:T(8,128)(2,1)}, u32[]{:S(2)}, u32[]{:S(2)}) collective-permute-start(bf16[320,1024]{1,0:T(8,128)(2,1)} %slice.13), channel_id=1, source_target_pairs={{0,1},{1,2},{2,3},{3,0},{4,5},{5,6},{6,7},{7,4},{8,9},{9,10},{10,1... | collective-permute-start | bytes 1966088 | tf_op jit(solution)/shard_map/ppermute | solution.py:360
  82.5 0.0 copy-done
  82.5 0.0 copy-done.5
  82.5 3.3 %collective-permute-start.4 = (bf16[16,1024]{1,0:T(8,128)(2,1)S(1)}, bf16[16,1024]{1,0:T(8,128)(2,1)S(1)}, u32[]{:S(2)}, u32[]{:S(2)}) collective-permute-start(bf16[16,1024]{1,0:T(8,128)(2,1)S(1)} %slice.14), channel_id=1, source_target_pairs={{0,2},{1,3},{2,0},{3,1},{4,6},{5,7},{6,4},{7,5},{8,10},{9,11},{10,... | collective-permute-start | bytes 98312 | tf_op jit(solution)/shard_map/ppermute | solution.py:360
  85.8 12.1 %collective-permute-done.4.far_ref = bf16[16,1024]{1,0:T(8,128)(2,1)S(1)} collective-permute-done((bf16[16,1024]{1,0:T(8,128)(2,1)S(1)}, bf16[16,1024]{1,0:T(8,128)(2,1)S(1)}, u32[]{:S(2)}, u32[]{:S(2)}) %collective-permute-start.4) | collective-permute-done | bytes 32800 | tf_op jit(solution)/shard_map/ppermute | solution.py:360
  98.0 0.0 all-to-all-done
  98.0 12.4 %cycle.1 = (bf16[2560,256]{1,0:T(8,128)(2,1)S(1)}, f32[5120,128]{1,0:T(8,128)S(1)}, bf16[4,256,640]{2,1,0:T(8,128)(2,1)S(1)}, f32[4,8,640]{2,1,0:T(8,128)S(1)}, f32[640,128]{1,0:T(8,128)S(1)}) custom-call(s32[1]{0:T(128)} %bitcast.here_ref, s32[4]{0:T(128)} %size_ref.1, bf16[5120,128]{1,0:T(8,128)(2,1)} %bitcast.4.raw_ref, ...), custom_call_target="tpu_custom_call" | custom-call | tf_op jit(solution)/shard_map/cycle/pallas_call | solution.py:287
  110.4 0.0 collective-permute-done.1.lo_ref
  110.4 0.0 collective-permute-done.3.hi_ref
  110.4 3.5 %close.1 = (bf16[5120,128]{1,0:T(8,128)(2,1)S(1)}, f32[5120,128]{1,0:T(8,128)S(1)}) custom-call(s32[1]{0:T(128)} %bitcast.here_ref, bf16[320,1024]{1,0:T(8,128)(2,1)} %collective-permute-done.1.lo_ref, bf16[320,1024]{1,0:T(8,128)(2,1)} %collective-permute-done.3.hi_ref, ...), custom_call_target="tpu_custom_call", output_to_operand_aliasing={{1}: (7, {})} | custom-call | tf_op jit(solution)/shard_map/close/pallas_call | solution.py:313
  113.9 0.0 copy-start.3
  113.9 54.8 %all_to_all.10 = bf16[512,5,2,128]{3,2,1,0:T(2,128)(2,1)S(1)} all-to-all(bf16[512,5,2,128]{3,2,1,0:T(2,128)(2,1)S(1)} %bitcast.9), channel_id=1, replica_groups=mesh['chan'=128,'orb'=4] {'chan','orb'}, dimensions={0} | all-to-all | bytes 2621440 | tf_op jit(solution)/shard_map/all_to_all | solution.py:364
  168.7 0.0 copy-done.3
  168.7 2.0 %finish.1 = bf16[640,1024]{1,0:T(8,128)(2,1)} custom-call(bf16[5120,128]{1,0:T(8,128)(2,1)S(1)} %bitcast.8, bf16[640,1024]{1,0:T(8,128)(2,1)S(1)} %copy-done.1, f32[5,128]{1,0:T(8,128)S(1)} %bitcast.11, f32[5,128]{1,0:T(8,128)S(1)} %bitcast.12), custom_call_target="tpu_custom_call" | custom-call | tf_op jit(solution)/shard_map/finish/pallas_call | solution.py:328
  (2 shorter events, 0.0 us)
Async XLA Ops:
  0.0 3.5 %copy-start.1 = (bf16[640,1024]{1,0:T(8,128)(2,1)S(1)}, bf16[640,1024]{1,0:T(8,128)(2,1)}, u32[]{:S(2)}) copy-start(bf16[640,1024]{1,0:T(8,128)(2,1)} %amp_ref.3) | copy-start | bytes 3932164
  0.0 3.5 %copy-start.2 = (f32[640]{0:T(1024)S(1)}, f32[640]{0:T(1024)}, u32[]{:S(2)}) copy-start(f32[640]{0:T(1024)} %param.8) | copy-start | bytes 7684
  3.4 79.1 %copy-start = (bf16[656,1024]{1,0:T(8,128)(2,1)}, bf16[656,1024]{1,0:T(8,128)(2,1)S(1)}, u32[]{:S(2)}) copy-start(bf16[656,1024]{1,0:T(8,128)(2,1)S(1)} %pick.1.own_any) | copy-start | bytes 4030468
  5.2 92.7 %all-to-all-start = ((bf16[512,5,2,128]{3,2,1,0:T(2,128)(2,1)}), bf16[512,5,2,128]{3,2,1,0:T(2,128)(2,1)}, u32[]{:S(2)}, u32[]{:S(2)}) async-start(bf16[512,5,2,128]{3,2,1,0:T(2,128)(2,1)} %bitcast.13), calls=%async_computation | async-start | bytes 2621440 | tf_op jit(solution)/shard_map/all_to_all | solution.py:364
  29.2 45.0 %collective-permute-start = (bf16[656,1024]{1,0:T(8,128)(2,1)S(1)}, bf16[656,1024]{1,0:T(8,128)(2,1)S(1)}, u32[]{:S(2)}, u32[]{:S(2)}) collective-permute-start(bf16[656,1024]{1,0:T(8,128)(2,1)S(1)} %pick.1.own_any), channel_id=1, source_target_pairs={{0,3},{1,0},{2,1},{3,2},{4,7},{5,4},{6,5},{7,6},{8,11},{9,8},{10,9... | collective-permute-start | bytes 4030472 | tf_op jit(solution)/shard_map/ppermute | solution.py:360
  33.7 45.9 %collective-permute-start.2 = (bf16[656,1024]{1,0:T(8,128)(2,1)S(1)}, bf16[656,1024]{1,0:T(8,128)(2,1)S(1)}, u32[]{:S(2)}, u32[]{:S(2)}) collective-permute-start(bf16[656,1024]{1,0:T(8,128)(2,1)S(1)} %pick.1.own_any), channel_id=1, source_target_pairs={{0,1},{1,2},{2,3},{3,0},{4,5},{5,6},{6,7},{7,4},{8,9},{9,10},{10,1... | collective-permute-start | bytes 4030472 | tf_op jit(solution)/shard_map/ppermute | solution.py:360
  74.3 6.3 %copy-start.4 = (bf16[656,1024]{1,0:T(8,128)(2,1)}, bf16[656,1024]{1,0:T(8,128)(2,1)S(1)}, u32[]{:S(2)}) copy-start(bf16[656,1024]{1,0:T(8,128)(2,1)S(1)} %collective-permute-done.after_any) | copy-start | bytes 4030468
  74.3 36.1 %collective-permute-start.1 = (bf16[320,1024]{1,0:T(8,128)(2,1)S(1)}, bf16[320,1024]{1,0:T(8,128)(2,1)}, u32[]{:S(2)}, u32[]{:S(2)}) collective-permute-start(bf16[320,1024]{1,0:T(8,128)(2,1)S(1)} %slice.12), channel_id=1, source_target_pairs={{0,3},{1,0},{2,1},{3,2},{4,7},{5,4},{6,5},{7,6},{8,11},{9,8},{10,9... | collective-permute-start | bytes 1966088 | tf_op jit(solution)/shard_map/ppermute | solution.py:360
  79.6 2.9 %copy-start.5 = (bf16[656,1024]{1,0:T(8,128)(2,1)}, bf16[656,1024]{1,0:T(8,128)(2,1)S(1)}, u32[]{:S(2)}) copy-start(bf16[656,1024]{1,0:T(8,128)(2,1)S(1)} %collective-permute-done.2.before_any) | copy-start | bytes 4030468
  80.6 29.8 %collective-permute-start.3 = (bf16[320,1024]{1,0:T(8,128)(2,1)}, bf16[320,1024]{1,0:T(8,128)(2,1)}, u32[]{:S(2)}, u32[]{:S(2)}) collective-permute-start(bf16[320,1024]{1,0:T(8,128)(2,1)} %slice.13), channel_id=1, source_target_pairs={{0,1},{1,2},{2,3},{3,0},{4,5},{5,6},{6,7},{7,4},{8,9},{9,10},{10,1... | collective-permute-start | bytes 1966088 | tf_op jit(solution)/shard_map/ppermute | solution.py:360
  82.5 15.4 %collective-permute-start.4 = (bf16[16,1024]{1,0:T(8,128)(2,1)S(1)}, bf16[16,1024]{1,0:T(8,128)(2,1)S(1)}, u32[]{:S(2)}, u32[]{:S(2)}) collective-permute-start(bf16[16,1024]{1,0:T(8,128)(2,1)S(1)} %slice.14), channel_id=1, source_target_pairs={{0,2},{1,3},{2,0},{3,1},{4,6},{5,7},{6,4},{7,5},{8,10},{9,11},{10,... | collective-permute-start | bytes 98312 | tf_op jit(solution)/shard_map/ppermute | solution.py:360
  113.9 54.8 %copy-start.3 = (f32[640]{0:T(1024)S(1)}, f32[640]{0:T(1024)}, u32[]{:S(2)}) copy-start(f32[640]{0:T(1024)} %param.9) | copy-start | bytes 7684

commit v6 on v5

--- a/solution.py
+++ b/solution.py
@@ -66,19 +66,18 @@
     src = jnp.concatenate([src_ref[c : c + 1, :] for c in range(blocks)], axis=1)
     sender = (src * 205) >> 10
     place = jnp.where(src >= 0, (src - sender * quota) * LANES + sender, -1)
-    lane = lax.broadcasted_iota(jnp.int32, (TAGS, states), 1)
-    which = lax.broadcasted_iota(jnp.int32, (TAGS, states), 0)
-    labels = jnp.where(which == 0, lane // rows_block, jnp.where(which == 1, lane % rows_block, 0))
+    state = lax.broadcasted_iota(jnp.int32, (states, LANES), 0)
+    which = lax.broadcasted_iota(jnp.int32, (states, LANES), 1)
+    labels = jnp.where(
+        which == 0, state // rows_block, jnp.where(which == 1, state % rows_block, 0)
+    )
     labels = labels.astype(F32).astype(BF)
-    out_ref[count:, count:] = jnp.zeros((TAGS, width - count), BF)
     for q in range(quota):
         at = lax.broadcasted_iota(jnp.int32, (LANES, states), 0) + q * LANES
-        hit = one_hot(at == place)
-        here = slice(q * LANES, (q + 1) * LANES)
-        hit_ref[here, :] = hit
-        out_ref[count:, here] = lax.dot_general(
-            labels, hit, (((1,), (1,)), ((), ())), preferred_element_type=F32
-        ).astype(BF)
+        hit_ref[q * LANES : (q + 1) * LANES, :] = one_hot(at == place)
+    tags = jnp.transpose(jnp.dot(hit_ref[...], labels, preferred_element_type=F32))
+    out_ref[count:, count:] = jnp.zeros((TAGS, width - count), BF)
+    out_ref[count:, :count] = tags[:TAGS].astype(BF)
     for cp in loads:
         cp.wait()
     out_ref[:count, :] = jnp.dot(
@@ -131,14 +130,14 @@
             w[:, o * rows_block : (o + 1) * rows_block], hot_ref[o], preferred_element_type=F32
         )
         out_ref[:, o * count : (o + 1) * count] = jnp.where(
-            owner == block_ref[o, 0:1, :], spread, 0.0
-        ).astype(BF)
+            owner == block_ref[o, 0:1, :], spread.astype(BF), jnp.zeros((), BF)
+        )
 
 
 def cycle_body(
-    quota, here_ref, size_ref, raw_ref, far_ref, own_any, after_any, before_any,
+    quota, here_ref, size_ref, raw_any, far_ref, own_any, after_any, before_any,
     rows_ref, flat_ref, hot_ref, block_ref, owner_ref,
-    wide_ref, tag_ref, tags_ref, w_ref, mix_ref, sem_tag, sem_w,
+    raw_ref, wide_ref, tag_ref, tags_ref, w_ref, mix_ref, sem_tag, sem_w,
 ):
     orbs, rows_block, count = hot_ref.shape
     halves = rows_block // LANES
@@ -151,39 +150,47 @@
         pltpu.make_async_copy(src.at[:count], w_ref.at[i], sem_w.at[i])
         for i, src in enumerate(sources)
     ]
-    for cp in tag_copies + copies:
+    raw_copy = pltpu.make_async_copy(raw_any, raw_ref, sem_w.at[3])
+    for cp in (*tag_copies, raw_copy, *copies):
         cp.start()
     here = here_ref[0]
     step = orbs * quota * halves
     lane = lax.broadcasted_iota(jnp.int32, (LANES, LANES), 1).astype(F32)
-    slot = lax.broadcasted_iota(jnp.int32, (rows_block, count), 0).astype(F32)
-    wide_ref[...] = raw_ref[...].astype(F32)
+    slot = lax.broadcasted_iota(jnp.int32, (rows_block, count), 0).astype(F32).astype(BF)
     for cp in tag_copies:
         cp.wait()
-    tags_ref[2] = far_ref[:, :count].astype(F32)
+    tags_ref[2] = far_ref[:, :count]
     for i, s in enumerate((0, 1, 3)):
-        tags_ref[s] = tag_ref[i, :, :count].astype(F32)
+        tags_ref[s] = tag_ref[i, :, :count]
+    sizes = []
     for o in range(orbs):
         tag = tags_ref[(o + orbs - here) % orbs]
-        hot_ref[o] = one_hot(slot == tag[1:2, :])
-        block_ref[o] = tag[0:8, :]
+        hot_ref[o] = jnp.where(slot == tag[1:2, :], jnp.ones((), BF), jnp.zeros((), BF))
+        block_ref[o] = tag
+        blocks = tag[0:1, :].astype(F32)
         size = jnp.zeros((1, count), F32)
         for c in range(size_ref.shape[0]):
             live = (size_ref[c] // orbs).astype(F32)
-            size = size + jnp.where(tag[0:1, :] == float(c), live, 0.0)
-        size = column(size)[:, 0:1]
+            size = size + jnp.where(blocks == float(c), live, 0.0)
+        sizes.append(size)
+    sizes = column(jnp.concatenate(sizes, axis=0))
+    owners = column(jnp.concatenate([tags_ref[s, 0:1, :].astype(F32) for s in range(orbs)], axis=0))
+    owner_ref[...] = jnp.broadcast_to(owners[:, 2:3], (count, LANES)).astype(BF)
+    raw_copy.wait()
+    wide_ref[...] = raw_ref[...].astype(F32)
+    for o in range(orbs):
         for q in range(quota):
             row = o * count + q * LANES
+            size = sizes[q * LANES : (q + 1) * LANES, o : o + 1]
             for h in range(halves):
                 piece = wide_ref[pl.ds((o * quota + q) * halves + h, LANES, stride=step), :]
-                keep = lane + float(h * LANES) < size[q * LANES : (q + 1) * LANES]
                 rows_ref[row : row + LANES, h * LANES : (h + 1) * LANES] = jnp.where(
-                    keep, piece, 0.0
+                    lane + float(h * LANES) < size, piece, 0.0
                 ).astype(BF)
-    owner_ref[...] = jnp.broadcast_to(column(tags_ref[2])[:, 0:1], (count, LANES))
     for i, s in enumerate((0, 1, 3)):
         copies[i].wait()
-        mix(w_ref.at[i], hot_ref, block_ref, column(tags_ref[s])[:, 0:1], mix_ref.at[i])
+        owner = jnp.broadcast_to(owners[:, s : s + 1], (count, LANES)).astype(BF)
+        mix(w_ref.at[i], hot_ref, block_ref, owner[:, 0:1], mix_ref.at[i])
         scatter(quota, (here + s) % orbs, step, mix_ref[i], rows_ref, flat_ref)
 
 
@@ -198,15 +205,17 @@
 
 
 def close_body(
-    quota, here_ref, lo_ref, hi_ref, hot_ref, block_ref, owner_ref, rows_ref, flat_in,
-    out_ref, flat_ref, mix_ref,
+    quota, here_ref, lo_any, hi_ref, hot_ref, block_ref, owner_ref, rows_ref, flat_in,
+    out_ref, flat_ref, lo_ref, mix_ref, sem,
 ):
     orbs, rows_block, count = hot_ref.shape
     half = count // 2
     step = orbs * quota * (rows_block // LANES)
-    for i, ref in enumerate((lo_ref, hi_ref)):
-        at = slice(i * half, (i + 1) * half)
-        mix(ref, hot_ref, block_ref, owner_ref[at, 0:1], mix_ref.at[at])
+    load = pltpu.make_async_copy(lo_any, lo_ref, sem)
+    load.start()
+    mix(hi_ref, hot_ref, block_ref, owner_ref[half:, 0:1], mix_ref.at[half:])
+    load.wait()
+    mix(lo_ref, hot_ref, block_ref, owner_ref[:half, 0:1], mix_ref.at[:half])
     scatter(quota, (here_ref[0] + 2) % orbs, step, mix_ref[...], rows_ref, flat_ref)
     out_ref[...] = flat_ref[...].astype(BF)
 
@@ -290,22 +299,23 @@
             pltpu.VMEM((4 * count, 2 * LANES), BF),
             pltpu.VMEM(raw.shape, F32),
             pltpu.VMEM((4, 2 * LANES, count), BF),
-            pltpu.VMEM((4, 8, count), F32),
-            pltpu.VMEM((count, LANES), F32),
+            pltpu.VMEM((4, TAGS, count), BF),
+            pltpu.VMEM((count, LANES), BF),
         ),
-        [SM, SM, VM, VM] + [ANY] * 3,
+        [SM, SM, ANY, VM] + [ANY] * 3,
         (VM,) * 5,
         [
+            pltpu.VMEM(raw.shape, BF),
             pltpu.VMEM(raw.shape, F32),
             pltpu.VMEM((3, TAGS, width), BF),
-            pltpu.VMEM((4, TAGS, count), F32),
+            pltpu.VMEM((4, TAGS, count), BF),
             pltpu.VMEM((3, count, width), BF),
             pltpu.VMEM((3, count, 4 * count), BF),
             pltpu.SemaphoreType.DMA((3,)),
-            pltpu.SemaphoreType.DMA((3,)),
+            pltpu.SemaphoreType.DMA((4,)),
         ],
         name="cycle",
-    )(here, sizes, near(raw), near(far), own, after, before)
+    )(here, sizes, raw, far, own, after, before)
 
 
 def close(here, lo, hi, hot, block, owner, rows, flat, quota):
@@ -313,12 +323,16 @@
     out, _ = call(
         functools.partial(close_body, quota),
         (pltpu.VMEM(flat.shape, BF), pltpu.VMEM(flat.shape, F32)),
-        [SM] + [VM] * 7,
+        [SM, ANY] + [VM] * 6,
         (VM, VM),
-        [pltpu.VMEM((count, 4 * count), BF)],
+        [
+            pltpu.VMEM(lo.shape, BF),
+            pltpu.VMEM((count, 4 * count), BF),
+            pltpu.SemaphoreType.DMA,
+        ],
         input_output_aliases={7: 1},
         name="close",
-    )(here, apart(lo), apart(hi), near(hot), near(block), near(owner), near(rows), near(flat))
+    )(here, apart(lo), near(hi), near(hot), near(block), near(owner), near(rows), near(flat))
     return out
 
 

time: 171 us -> 171 us (level)
  no operation moved by 1% of the time
where the time goes in v6:
time: 171 us; the launch traced here: 170 us
  blocking collectives  54.8 us (32%)
  waiting for transfers between devices  50.8 us (30%)
  starting transfers between devices  40.8 us (24%)
  Pallas kernels  21.5 us (13%)
  local copies, waits for them, and re-layouts  1.92 us (1%)
    all_to_all x1, blocking collectives, exchange(): x = lax.all_to_all(x, BOTH, split_axis=0, concat_axis=0, tiled=True)  54.8 us
    ppermute x5, waiting for transfers between devices, shift(): return lax.ppermute(x, 'orb', [(i, (i + by) % orbs) for i in range(orbs)])  50.8 us
    all_to_all x1, starting transfers between devices, exchange(): x = lax.all_to_all(x, BOTH, split_axis=0, concat_axis=0, tiled=True)  24 us
    ppermute x5, starting transfers between devices, shift(): return lax.ppermute(x, 'orb', [(i, (i + by) % orbs) for i in range(orbs)])  16.9 us
    pallas_call x1, Pallas kernels, cycle(): call(functools.partial(cycle_body, quota), (pltpu.VMEM((4 * count, 2 * LA...  11.6 us
    pallas_call x1, Pallas kernels, pick(): call(functools.partial(pick_body, quota), pltpu.VMEM((count + TAGS, width...  3.43 us
  transfers between devices with their start and end apart: 6, of which 2 were waited for; matrix products, arithmetic and copies ran while one was open for 1% of the time, Pallas kernels for 7%

profile of v6, /device:TPU:1, one launch (start us, length us, event | category | flops | bytes accessed | tf_op | source)
XLA Modules:
  0.0 170.2 jit_solution(6725172905439675456)
XLA Ops:
  0.0 0.0 copy-start.1
  0.0 0.0 copy-start.2
  0.0 3.4 %pick.1.own_any = bf16[656,1024]{1,0:T(8,128)(2,1)S(1)} custom-call(s32[4,256]{1,0:T(4,128)} %src_any.1, bf16[1024,1024]{1,0:T(8,128)(2,1)} %bitcast.14), custom_call_target="tpu_custom_call" | custom-call | tf_op jit(solution)/shard_map/pick/pallas_call | solution.py:258
  3.4 0.0 copy-start
  3.5 0.0 copy-done.1
  3.5 0.0 copy-done.2
  3.5 1.8 %pack.1 = bf16[5120,128]{1,0:T(8,128)(2,1)} custom-call(bf16[640,1024]{1,0:T(8,128)(2,1)S(1)} %copy-done.1, f32[5,128]{1,0:T(8,128)S(1)} %bitcast.10), custom_call_target="tpu_custom_call" | custom-call | tf_op jit(solution)/shard_map/pack/pallas_call | solution.py:277
  5.2 24.0 %all-to-all-start = ((bf16[512,5,2,128]{3,2,1,0:T(2,128)(2,1)}), bf16[512,5,2,128]{3,2,1,0:T(2,128)(2,1)}, u32[]{:S(2)}, u32[]{:S(2)}) async-start(bf16[512,5,2,128]{3,2,1,0:T(2,128)(2,1)} %bitcast.13), calls=%async_computation | async-start | bytes 2621440 | tf_op jit(solution)/shard_map/all_to_all | solution.py:378
  29.2 0.0 copy-start.4
  29.2 4.5 %collective-permute-start = (bf16[656,1024]{1,0:T(8,128)(2,1)S(1)}, bf16[656,1024]{1,0:T(8,128)(2,1)S(1)}, u32[]{:S(2)}, u32[]{:S(2)}) collective-permute-start(bf16[656,1024]{1,0:T(8,128)(2,1)S(1)} %pick.1.own_any), channel_id=1, source_target_pairs={{0,3},{1,0},{2,1},{3,2},{4,7},{5,4},{6,5},{7,6},{8,11},{9,8},{10,9... | collective-permute-start | bytes 4030472 | tf_op jit(solution)/shard_map/ppermute | solution.py:374
  33.7 1.9 %collective-permute-start.2 = (bf16[656,1024]{1,0:T(8,128)(2,1)S(1)}, bf16[656,1024]{1,0:T(8,128)(2,1)S(1)}, u32[]{:S(2)}, u32[]{:S(2)}) collective-permute-start(bf16[656,1024]{1,0:T(8,128)(2,1)S(1)} %pick.1.own_any), channel_id=1, source_target_pairs={{0,1},{1,2},{2,3},{3,0},{4,5},{5,6},{6,7},{7,4},{8,9},{9,10},{10,1... | collective-permute-start | bytes 4030472 | tf_op jit(solution)/shard_map/ppermute | solution.py:374
  35.6 38.6 %collective-permute-done.after_any = bf16[656,1024]{1,0:T(8,128)(2,1)S(1)} collective-permute-done((bf16[656,1024]{1,0:T(8,128)(2,1)S(1)}, bf16[656,1024]{1,0:T(8,128)(2,1)S(1)}, u32[]{:S(2)}, u32[]{:S(2)}) %collective-permute-start) | collective-permute-done | bytes 1343520 | tf_op jit(solution)/shard_map/ppermute | solution.py:374
  74.3 0.0 copy-start.5
  74.3 0.9 slice.12
  75.2 5.3 %collective-permute-start.1 = (bf16[320,1024]{1,0:T(8,128)(2,1)}, bf16[320,1024]{1,0:T(8,128)(2,1)}, u32[]{:S(2)}, u32[]{:S(2)}) collective-permute-start(bf16[320,1024]{1,0:T(8,128)(2,1)} %slice.12), channel_id=1, source_target_pairs={{0,3},{1,0},{2,1},{3,2},{4,7},{5,4},{6,5},{7,6},{8,11},{9,8},{10,9... | collective-permute-start | bytes 1966088 | tf_op jit(solution)/shard_map/ppermute | solution.py:374
  80.5 0.0 collective-permute-done.2.before_any
  80.5 0.0 copy-start.6
  80.6 0.9 slice.13
  81.5 0.0 copy-done.5
  81.5 1.9 %collective-permute-start.3 = (bf16[320,1024]{1,0:T(8,128)(2,1)}, bf16[320,1024]{1,0:T(8,128)(2,1)S(1)}, u32[]{:S(2)}, u32[]{:S(2)}) collective-permute-start(bf16[320,1024]{1,0:T(8,128)(2,1)} %slice.13), channel_id=1, source_target_pairs={{0,1},{1,2},{2,3},{3,0},{4,5},{5,6},{6,7},{7,4},{8,9},{9,10},{10,1... | collective-permute-start | bytes 1966088 | tf_op jit(solution)/shard_map/ppermute | solution.py:374
  83.4 0.0 copy-done
  83.4 0.0 copy-done.6
  83.4 3.3 %collective-permute-start.4 = (bf16[16,1024]{1,0:T(8,128)(2,1)S(1)}, bf16[16,1024]{1,0:T(8,128)(2,1)S(1)}, u32[]{:S(2)}, u32[]{:S(2)}) collective-permute-start(bf16[16,1024]{1,0:T(8,128)(2,1)S(1)} %slice.14), channel_id=1, source_target_pairs={{0,2},{1,3},{2,0},{3,1},{4,6},{5,7},{6,4},{7,5},{8,10},{9,11},{10,... | collective-permute-start | bytes 98312 | tf_op jit(solution)/shard_map/ppermute | solution.py:374
  86.7 12.1 %collective-permute-done.4.far_ref = bf16[16,1024]{1,0:T(8,128)(2,1)S(1)} collective-permute-done((bf16[16,1024]{1,0:T(8,128)(2,1)S(1)}, bf16[16,1024]{1,0:T(8,128)(2,1)S(1)}, u32[]{:S(2)}, u32[]{:S(2)}) %collective-permute-start.4) | collective-permute-done | bytes 32800 | tf_op jit(solution)/shard_map/ppermute | solution.py:374
  98.9 0.0 all-to-all-done
  98.9 0.0 copy-done.4
  98.9 11.6 %cycle.1 = (bf16[2560,256]{1,0:T(8,128)(2,1)S(1)}, f32[5120,128]{1,0:T(8,128)S(1)}, bf16[4,256,640]{2,1,0:T(8,128)(2,1)S(1)}, bf16[4,16,640]{2,1,0:T(8,128)(2,1)S(1)}, bf16[640,128]{1,0:T(8,128)(2,1)S(1)}) custom-call(s32[1]{0:T(128)} %bitcast.here_ref, s32[4]{0:T(128)S(1)} %copy-done.4, bf16[5120,128]{1,0:T(8,128)(2,1)} %bitcast.4.raw_any, ...), custom_call_target="tpu_custom_call" | custom-call | tf_op jit(solution)/shard_map/cycle/pallas_call | solution.py:296
  110.5 0.0 collective-permute-done.1.lo_any
  110.5 0.0 collective-permute-done.3.hi_ref
  110.5 2.8 %close.1 = (bf16[5120,128]{1,0:T(8,128)(2,1)S(1)}, f32[5120,128]{1,0:T(8,128)S(1)}) custom-call(s32[1]{0:T(128)} %bitcast.here_ref, bf16[320,1024]{1,0:T(8,128)(2,1)} %collective-permute-done.1.lo_any, bf16[320,1024]{1,0:T(8,128)(2,1)S(1)} %collective-permute-done.3.hi_ref, ...), custom_call_target="tpu_custom_call", output_to_operand_aliasing={{1}: (7, {})} | custom-call | tf_op jit(solution)/shard_map/close/pallas_call | solution.py:323
  113.3 0.0 copy-start.3
  113.3 54.8 %all_to_all.10 = bf16[512,5,2,128]{3,2,1,0:T(2,128)(2,1)S(1)} all-to-all(bf16[512,5,2,128]{3,2,1,0:T(2,128)(2,1)S(1)} %bitcast.9), channel_id=1, replica_groups=mesh['chan'=128,'orb'=4] {'chan','orb'}, dimensions={0} | all-to-all | bytes 2621440 | tf_op jit(solution)/shard_map/all_to_all | solution.py:378
  168.1 0.0 copy-done.3
  168.1 2.0 %finish.1 = bf16[640,1024]{1,0:T(8,128)(2,1)} custom-call(bf16[5120,128]{1,0:T(8,128)(2,1)S(1)} %bitcast.8, bf16[640,1024]{1,0:T(8,128)(2,1)S(1)} %copy-done.1, f32[5,128]{1,0:T(8,128)S(1)} %bitcast.11, f32[5,128]{1,0:T(8,128)S(1)} %bitcast.12), custom_call_target="tpu_custom_call" | custom-call | tf_op jit(solution)/shard_map/finish/pallas_call | solution.py:342
  (1 shorter events, 0.0 us)
Async XLA Ops:
  0.0 3.5 %copy-start.1 = (bf16[640,1024]{1,0:T(8,128)(2,1)S(1)}, bf16[640,1024]{1,0:T(8,128)(2,1)}, u32[]{:S(2)}) copy-start(bf16[640,1024]{1,0:T(8,128)(2,1)} %amp_ref.3) | copy-start | bytes 3932164
  0.0 3.5 %copy-start.2 = (f32[640]{0:T(1024)S(1)}, f32[640]{0:T(1024)}, u32[]{:S(2)}) copy-start(f32[640]{0:T(1024)} %param.8) | copy-start | bytes 7684
  3.4 80.0 %copy-start = (bf16[656,1024]{1,0:T(8,128)(2,1)}, bf16[656,1024]{1,0:T(8,128)(2,1)S(1)}, u32[]{:S(2)}) copy-start(bf16[656,1024]{1,0:T(8,128)(2,1)S(1)} %pick.1.own_any) | copy-start | bytes 4030468
  5.2 93.6 %all-to-all-start = ((bf16[512,5,2,128]{3,2,1,0:T(2,128)(2,1)}), bf16[512,5,2,128]{3,2,1,0:T(2,128)(2,1)}, u32[]{:S(2)}, u32[]{:S(2)}) async-start(bf16[512,5,2,128]{3,2,1,0:T(2,128)(2,1)} %bitcast.13), calls=%async_computation | async-start | bytes 2621440 | tf_op jit(solution)/shard_map/all_to_all | solution.py:378
  29.2 69.7 %copy-start.4 = (s32[4]{0:T(128)S(1)}, s32[4]{0:T(128)}, u32[]{:S(2)}) copy-start(s32[4]{0:T(128)} %size_ref.1) | copy-start | bytes 52
  29.2 45.0 %collective-permute-start = (bf16[656,1024]{1,0:T(8,128)(2,1)S(1)}, bf16[656,1024]{1,0:T(8,128)(2,1)S(1)}, u32[]{:S(2)}, u32[]{:S(2)}) collective-permute-start(bf16[656,1024]{1,0:T(8,128)(2,1)S(1)} %pick.1.own_any), channel_id=1, source_target_pairs={{0,3},{1,0},{2,1},{3,2},{4,7},{5,4},{6,5},{7,6},{8,11},{9,8},{10,9... | collective-permute-start | bytes 4030472 | tf_op jit(solution)/shard_map/ppermute | solution.py:374
  33.7 46.8 %collective-permute-start.2 = (bf16[656,1024]{1,0:T(8,128)(2,1)S(1)}, bf16[656,1024]{1,0:T(8,128)(2,1)S(1)}, u32[]{:S(2)}, u32[]{:S(2)}) collective-permute-start(bf16[656,1024]{1,0:T(8,128)(2,1)S(1)} %pick.1.own_any), channel_id=1, source_target_pairs={{0,1},{1,2},{2,3},{3,0},{4,5},{5,6},{6,7},{7,4},{8,9},{9,10},{10,1... | collective-permute-start | bytes 4030472 | tf_op jit(solution)/shard_map/ppermute | solution.py:374
  74.3 7.2 %copy-start.5 = (bf16[656,1024]{1,0:T(8,128)(2,1)}, bf16[656,1024]{1,0:T(8,128)(2,1)S(1)}, u32[]{:S(2)}) copy-start(bf16[656,1024]{1,0:T(8,128)(2,1)S(1)} %collective-permute-done.after_any) | copy-start | bytes 4030468
  75.2 35.2 %collective-permute-start.1 = (bf16[320,1024]{1,0:T(8,128)(2,1)}, bf16[320,1024]{1,0:T(8,128)(2,1)}, u32[]{:S(2)}, u32[]{:S(2)}) collective-permute-start(bf16[320,1024]{1,0:T(8,128)(2,1)} %slice.12), channel_id=1, source_target_pairs={{0,3},{1,0},{2,1},{3,2},{4,7},{5,4},{6,5},{7,6},{8,11},{9,8},{10,9... | collective-permute-start | bytes 1966088 | tf_op jit(solution)/shard_map/ppermute | solution.py:374
  80.5 2.9 %copy-start.6 = (bf16[656,1024]{1,0:T(8,128)(2,1)}, bf16[656,1024]{1,0:T(8,128)(2,1)S(1)}, u32[]{:S(2)}) copy-start(bf16[656,1024]{1,0:T(8,128)(2,1)S(1)} %collective-permute-done.2.before_any) | copy-start | bytes 4030468
  81.5 29.0 %collective-permute-start.3 = (bf16[320,1024]{1,0:T(8,128)(2,1)}, bf16[320,1024]{1,0:T(8,128)(2,1)S(1)}, u32[]{:S(2)}, u32[]{:S(2)}) collective-permute-start(bf16[320,1024]{1,0:T(8,128)(2,1)} %slice.13), channel_id=1, source_target_pairs={{0,1},{1,2},{2,3},{3,0},{4,5},{5,6},{6,7},{7,4},{8,9},{9,10},{10,1... | collective-permute-start | bytes 1966088 | tf_op jit(solution)/shard_map/ppermute | solution.py:374
  83.4 15.4 %collective-permute-start.4 = (bf16[16,1024]{1,0:T(8,128)(2,1)S(1)}, bf16[16,1024]{1,0:T(8,128)(2,1)S(1)}, u32[]{:S(2)}, u32[]{:S(2)}) collective-permute-start(bf16[16,1024]{1,0:T(8,128)(2,1)S(1)} %slice.14), channel_id=1, source_target_pairs={{0,2},{1,3},{2,0},{3,1},{4,6},{5,7},{6,4},{7,5},{8,10},{9,11},{10,... | collective-permute-start | bytes 98312 | tf_op jit(solution)/shard_map/ppermute | solution.py:374
  113.3 54.8 %copy-start.3 = (f32[640]{0:T(1024)S(1)}, f32[640]{0:T(1024)}, u32[]{:S(2)}) copy-start(f32[640]{0:T(1024)} %param.9) | copy-start | bytes 7684

commit v7 on v6

--- a/solution.py
+++ b/solution.py
@@ -208,8 +208,8 @@
     quota, here_ref, lo_any, hi_ref, hot_ref, block_ref, owner_ref, rows_ref, flat_in,
     out_ref, flat_ref, lo_ref, mix_ref, sem,
 ):
-    orbs, rows_block, count = hot_ref.shape
-    half = count // 2
+    orbs, rows_block, _ = hot_ref.shape
+    half = lo_ref.shape[0]
     step = orbs * quota * (rows_block // LANES)
     load = pltpu.make_async_copy(lo_any, lo_ref, sem)
     load.start()
@@ -366,7 +366,7 @@
     row_count, _ = amplitudes.shape
     quota = row_count // chan_count
     count = quota * LANES
-    half = count // 2
+    early = count * 23 // 40
     halves = pair_source.shape[1] // LANES
     peers = chan_count * orbs
 
@@ -384,8 +384,8 @@
     outgoing, _ = lax.optimization_barrier((pack(amplitudes, recoupling, orbs, quota), own))
     raw = exchange(outgoing)
     far = shift(own[count:], 2)
-    lo = shift(after[:half], -1)
-    hi = shift(before[half:count], 1)
+    lo = shift(after[:early], -1)
+    hi = shift(before[early:count], 1)
     here = lax.axis_index("orb").astype(jnp.int32).reshape(1)
     rows, flat, hot, block, owner = cycle(
         here, channel_sizes, raw, far, own, after, before, quota

time: 171 us -> 169 us (0.988)
  waiting for transfers between devices: 50.8 us -> 48.7 us
    ppermute x5, waiting for transfers between devices: 50.8 us -> 48.7 us  [shift(): return lax.ppermute(x, 'orb', [(i, (i + by) % orbs) for i in range(orbs)])]
where the time goes in v7:
time: 169 us; the launch traced here: 168 us
  blocking collectives  54.8 us (32%)
  waiting for transfers between devices  48.7 us (29%)
  starting transfers between devices  40.8 us (24%)
  Pallas kernels  21.6 us (13%)
  local copies, waits for them, and re-layouts  1.91 us (1%)
    all_to_all x1, blocking collectives, exchange(): x = lax.all_to_all(x, BOTH, split_axis=0, concat_axis=0, tiled=True)  54.8 us
    ppermute x5, waiting for transfers between devices, shift(): return lax.ppermute(x, 'orb', [(i, (i + by) % orbs) for i in range(orbs)])  48.7 us
    all_to_all x1, starting transfers between devices, exchange(): x = lax.all_to_all(x, BOTH, split_axis=0, concat_axis=0, tiled=True)  24 us
    ppermute x5, starting transfers between devices, shift(): return lax.ppermute(x, 'orb', [(i, (i + by) % orbs) for i in range(orbs)])  16.9 us
    pallas_call x1, Pallas kernels, cycle(): call(functools.partial(cycle_body, quota), (pltpu.VMEM((4 * count, 2 * LA...  11.6 us
    pallas_call x1, Pallas kernels, pick(): call(functools.partial(pick_body, quota), pltpu.VMEM((count + TAGS, width...  3.43 us
  transfers between devices with their start and end apart: 6, of which 2 were waited for; matrix products, arithmetic and copies ran while one was open for 1% of the time, Pallas kernels for 7%

profile of v7, /device:TPU:1, one launch (start us, length us, event | category | flops | bytes accessed | tf_op | source)
XLA Modules:
  0.0 168.2 jit_solution(7256870663960848021)
XLA Ops:
  0.0 0.0 copy-start.1
  0.0 0.0 copy-start.2
  0.0 3.4 %pick.1.own_any = bf16[656,1024]{1,0:T(8,128)(2,1)S(1)} custom-call(s32[4,256]{1,0:T(4,128)} %src_any.1, bf16[1024,1024]{1,0:T(8,128)(2,1)} %bitcast.14), custom_call_target="tpu_custom_call" | custom-call | tf_op jit(solution)/shard_map/pick/pallas_call | solution.py:258
  3.4 0.0 copy-start
  3.5 0.0 copy-done.1
  3.5 0.0 copy-done.2
  3.5 1.8 %pack.1 = bf16[5120,128]{1,0:T(8,128)(2,1)} custom-call(bf16[640,1024]{1,0:T(8,128)(2,1)S(1)} %copy-done.1, f32[5,128]{1,0:T(8,128)S(1)} %bitcast.10), custom_call_target="tpu_custom_call" | custom-call | tf_op jit(solution)/shard_map/pack/pallas_call | solution.py:277
  5.2 24.0 %all-to-all-start = ((bf16[512,5,2,128]{3,2,1,0:T(2,128)(2,1)}), bf16[512,5,2,128]{3,2,1,0:T(2,128)(2,1)}, u32[]{:S(2)}, u32[]{:S(2)}) async-start(bf16[512,5,2,128]{3,2,1,0:T(2,128)(2,1)} %bitcast.13), calls=%async_computation | async-start | bytes 2621440 | tf_op jit(solution)/shard_map/all_to_all | solution.py:378
  29.2 0.0 copy-start.4
  29.2 4.5 %collective-permute-start = (bf16[656,1024]{1,0:T(8,128)(2,1)S(1)}, bf16[656,1024]{1,0:T(8,128)(2,1)S(1)}, u32[]{:S(2)}, u32[]{:S(2)}) collective-permute-start(bf16[656,1024]{1,0:T(8,128)(2,1)S(1)} %pick.1.own_any), channel_id=1, source_target_pairs={{0,3},{1,0},{2,1},{3,2},{4,7},{5,4},{6,5},{7,6},{8,11},{9,8},{10,9... | collective-permute-start | bytes 4030472 | tf_op jit(solution)/shard_map/ppermute | solution.py:374
  33.7 1.9 %collective-permute-start.2 = (bf16[656,1024]{1,0:T(8,128)(2,1)S(1)}, bf16[656,1024]{1,0:T(8,128)(2,1)S(1)}, u32[]{:S(2)}, u32[]{:S(2)}) collective-permute-start(bf16[656,1024]{1,0:T(8,128)(2,1)S(1)} %pick.1.own_any), channel_id=1, source_target_pairs={{0,1},{1,2},{2,3},{3,0},{4,5},{5,6},{6,7},{7,4},{8,9},{9,10},{10,1... | collective-permute-start | bytes 4030472 | tf_op jit(solution)/shard_map/ppermute | solution.py:374
  35.6 38.6 %collective-permute-done.after_any = bf16[656,1024]{1,0:T(8,128)(2,1)S(1)} collective-permute-done((bf16[656,1024]{1,0:T(8,128)(2,1)S(1)}, bf16[656,1024]{1,0:T(8,128)(2,1)S(1)}, u32[]{:S(2)}, u32[]{:S(2)}) %collective-permute-start) | collective-permute-done | bytes 1343520 | tf_op jit(solution)/shard_map/ppermute | solution.py:374
  74.3 0.0 copy-start.5
  74.3 1.0 slice.12
  75.3 5.3 %collective-permute-start.1 = (bf16[368,1024]{1,0:T(8,128)(2,1)}, bf16[368,1024]{1,0:T(8,128)(2,1)}, u32[]{:S(2)}, u32[]{:S(2)}) collective-permute-start(bf16[368,1024]{1,0:T(8,128)(2,1)} %slice.12), channel_id=1, source_target_pairs={{0,3},{1,0},{2,1},{3,2},{4,7},{5,4},{6,5},{7,6},{8,11},{9,8},{10,9... | collective-permute-start | bytes 2261000 | tf_op jit(solution)/shard_map/ppermute | solution.py:374
  80.6 0.0 collective-permute-done.2.before_any
  80.6 0.0 copy-start.6
  80.6 0.9 slice.13
  81.5 1.9 %collective-permute-start.3 = (bf16[272,1024]{1,0:T(8,128)(2,1)}, bf16[272,1024]{1,0:T(8,128)(2,1)S(1)}, u32[]{:S(2)}, u32[]{:S(2)}) collective-permute-start(bf16[272,1024]{1,0:T(8,128)(2,1)} %slice.13), channel_id=1, source_target_pairs={{0,1},{1,2},{2,3},{3,0},{4,5},{5,6},{6,7},{7,4},{8,9},{9,10},{10,1... | collective-permute-start | bytes 1671176 | tf_op jit(solution)/shard_map/ppermute | solution.py:374
  83.4 0.0 copy-done
  83.4 0.0 copy-done.5
  83.4 3.3 %collective-permute-start.4 = (bf16[16,1024]{1,0:T(8,128)(2,1)S(1)}, bf16[16,1024]{1,0:T(8,128)(2,1)S(1)}, u32[]{:S(2)}, u32[]{:S(2)}) collective-permute-start(bf16[16,1024]{1,0:T(8,128)(2,1)S(1)} %slice.14), channel_id=1, source_target_pairs={{0,2},{1,3},{2,0},{3,1},{4,6},{5,7},{6,4},{7,5},{8,10},{9,11},{10,... | collective-permute-start | bytes 98312 | tf_op jit(solution)/shard_map/ppermute | solution.py:374
  86.7 0.0 copy-done.6
  86.7 10.0 %collective-permute-done.4.far_ref = bf16[16,1024]{1,0:T(8,128)(2,1)S(1)} collective-permute-done((bf16[16,1024]{1,0:T(8,128)(2,1)S(1)}, bf16[16,1024]{1,0:T(8,128)(2,1)S(1)}, u32[]{:S(2)}, u32[]{:S(2)}) %collective-permute-start.4) | collective-permute-done | bytes 32800 | tf_op jit(solution)/shard_map/ppermute | solution.py:374
  96.8 0.0 all-to-all-done
  96.8 0.0 copy-done.4
  96.8 11.6 %cycle.1 = (bf16[2560,256]{1,0:T(8,128)(2,1)S(1)}, f32[5120,128]{1,0:T(8,128)S(1)}, bf16[4,256,640]{2,1,0:T(8,128)(2,1)S(1)}, bf16[4,16,640]{2,1,0:T(8,128)(2,1)S(1)}, bf16[640,128]{1,0:T(8,128)(2,1)S(1)}) custom-call(s32[1]{0:T(128)} %bitcast.here_ref, s32[4]{0:T(128)S(1)} %copy-done.4, bf16[5120,128]{1,0:T(8,128)(2,1)} %bitcast.4.raw_any, ...), custom_call_target="tpu_custom_call" | custom-call | tf_op jit(solution)/shard_map/cycle/pallas_call | solution.py:296
  108.3 0.0 collective-permute-done.3.hi_ref
  108.4 0.0 collective-permute-done.1.lo_any
  108.4 2.9 %close.1 = (bf16[5120,128]{1,0:T(8,128)(2,1)S(1)}, f32[5120,128]{1,0:T(8,128)S(1)}) custom-call(s32[1]{0:T(128)} %bitcast.here_ref, bf16[368,1024]{1,0:T(8,128)(2,1)} %collective-permute-done.1.lo_any, bf16[272,1024]{1,0:T(8,128)(2,1)S(1)} %collective-permute-done.3.hi_ref, ...), custom_call_target="tpu_custom_call", output_to_operand_aliasing={{1}: (7, {})} | custom-call | tf_op jit(solution)/shard_map/close/pallas_call | solution.py:323
  111.3 0.0 copy-start.3
  111.3 54.8 %all_to_all.10 = bf16[512,5,2,128]{3,2,1,0:T(2,128)(2,1)S(1)} all-to-all(bf16[512,5,2,128]{3,2,1,0:T(2,128)(2,1)S(1)} %bitcast.9), channel_id=1, replica_groups=mesh['chan'=128,'orb'=4] {'chan','orb'}, dimensions={0} | all-to-all | bytes 2621440 | tf_op jit(solution)/shard_map/all_to_all | solution.py:378
  166.0 0.0 copy-done.3
  166.0 2.0 %finish.1 = bf16[640,1024]{1,0:T(8,128)(2,1)} custom-call(bf16[5120,128]{1,0:T(8,128)(2,1)S(1)} %bitcast.8, bf16[640,1024]{1,0:T(8,128)(2,1)S(1)} %copy-done.1, f32[5,128]{1,0:T(8,128)S(1)} %bitcast.11, f32[5,128]{1,0:T(8,128)S(1)} %bitcast.12), custom_call_target="tpu_custom_call" | custom-call | tf_op jit(solution)/shard_map/finish/pallas_call | solution.py:342
  (1 shorter events, 0.0 us)
Async XLA Ops:
  0.0 3.5 %copy-start.1 = (bf16[640,1024]{1,0:T(8,128)(2,1)S(1)}, bf16[640,1024]{1,0:T(8,128)(2,1)}, u32[]{:S(2)}) copy-start(bf16[640,1024]{1,0:T(8,128)(2,1)} %amp_ref.3) | copy-start | bytes 3932164
  0.0 3.5 %copy-start.2 = (f32[640]{0:T(1024)S(1)}, f32[640]{0:T(1024)}, u32[]{:S(2)}) copy-start(f32[640]{0:T(1024)} %param.8) | copy-start | bytes 7684
  3.4 80.0 %copy-start = (bf16[656,1024]{1,0:T(8,128)(2,1)}, bf16[656,1024]{1,0:T(8,128)(2,1)S(1)}, u32[]{:S(2)}) copy-start(bf16[656,1024]{1,0:T(8,128)(2,1)S(1)} %pick.1.own_any) | copy-start | bytes 4030468
  5.2 91.5 %all-to-all-start = ((bf16[512,5,2,128]{3,2,1,0:T(2,128)(2,1)}), bf16[512,5,2,128]{3,2,1,0:T(2,128)(2,1)}, u32[]{:S(2)}, u32[]{:S(2)}) async-start(bf16[512,5,2,128]{3,2,1,0:T(2,128)(2,1)} %bitcast.13), calls=%async_computation | async-start | bytes 2621440 | tf_op jit(solution)/shard_map/all_to_all | solution.py:378
  29.2 67.5 %copy-start.4 = (s32[4]{0:T(128)S(1)}, s32[4]{0:T(128)}, u32[]{:S(2)}) copy-start(s32[4]{0:T(128)} %size_ref.1) | copy-start | bytes 52
  29.2 45.0 %collective-permute-start = (bf16[656,1024]{1,0:T(8,128)(2,1)S(1)}, bf16[656,1024]{1,0:T(8,128)(2,1)S(1)}, u32[]{:S(2)}, u32[]{:S(2)}) collective-permute-start(bf16[656,1024]{1,0:T(8,128)(2,1)S(1)} %pick.1.own_any), channel_id=1, source_target_pairs={{0,3},{1,0},{2,1},{3,2},{4,7},{5,4},{6,5},{7,6},{8,11},{9,8},{10,9... | collective-permute-start | bytes 4030472 | tf_op jit(solution)/shard_map/ppermute | solution.py:374
  33.7 46.9 %collective-permute-start.2 = (bf16[656,1024]{1,0:T(8,128)(2,1)S(1)}, bf16[656,1024]{1,0:T(8,128)(2,1)S(1)}, u32[]{:S(2)}, u32[]{:S(2)}) collective-permute-start(bf16[656,1024]{1,0:T(8,128)(2,1)S(1)} %pick.1.own_any), channel_id=1, source_target_pairs={{0,1},{1,2},{2,3},{3,0},{4,5},{5,6},{6,7},{7,4},{8,9},{9,10},{10,1... | collective-permute-start | bytes 4030472 | tf_op jit(solution)/shard_map/ppermute | solution.py:374
  74.3 9.2 %copy-start.5 = (bf16[656,1024]{1,0:T(8,128)(2,1)}, bf16[656,1024]{1,0:T(8,128)(2,1)S(1)}, u32[]{:S(2)}) copy-start(bf16[656,1024]{1,0:T(8,128)(2,1)S(1)} %collective-permute-done.after_any) | copy-start | bytes 4030468
  75.3 33.1 %collective-permute-start.1 = (bf16[368,1024]{1,0:T(8,128)(2,1)}, bf16[368,1024]{1,0:T(8,128)(2,1)}, u32[]{:S(2)}, u32[]{:S(2)}) collective-permute-start(bf16[368,1024]{1,0:T(8,128)(2,1)} %slice.12), channel_id=1, source_target_pairs={{0,3},{1,0},{2,1},{3,2},{4,7},{5,4},{6,5},{7,6},{8,11},{9,8},{10,9... | collective-permute-start | bytes 2261000 | tf_op jit(solution)/shard_map/ppermute | solution.py:374
  80.6 6.1 %copy-start.6 = (bf16[656,1024]{1,0:T(8,128)(2,1)}, bf16[656,1024]{1,0:T(8,128)(2,1)S(1)}, u32[]{:S(2)}) copy-start(bf16[656,1024]{1,0:T(8,128)(2,1)S(1)} %collective-permute-done.2.before_any) | copy-start | bytes 4030468
  81.5 26.9 %collective-permute-start.3 = (bf16[272,1024]{1,0:T(8,128)(2,1)}, bf16[272,1024]{1,0:T(8,128)(2,1)S(1)}, u32[]{:S(2)}, u32[]{:S(2)}) collective-permute-start(bf16[272,1024]{1,0:T(8,128)(2,1)} %slice.13), channel_id=1, source_target_pairs={{0,1},{1,2},{2,3},{3,0},{4,5},{5,6},{6,7},{7,4},{8,9},{9,10},{10,1... | collective-permute-start | bytes 1671176 | tf_op jit(solution)/shard_map/ppermute | solution.py:374
  83.4 13.3 %collective-permute-start.4 = (bf16[16,1024]{1,0:T(8,128)(2,1)S(1)}, bf16[16,1024]{1,0:T(8,128)(2,1)S(1)}, u32[]{:S(2)}, u32[]{:S(2)}) collective-permute-start(bf16[16,1024]{1,0:T(8,128)(2,1)S(1)} %slice.14), channel_id=1, source_target_pairs={{0,2},{1,3},{2,0},{3,1},{4,6},{5,7},{6,4},{7,5},{8,10},{9,11},{10,... | collective-permute-start | bytes 98312 | tf_op jit(solution)/shard_map/ppermute | solution.py:374
  111.3 54.8 %copy-start.3 = (f32[640]{0:T(1024)S(1)}, f32[640]{0:T(1024)}, u32[]{:S(2)}) copy-start(f32[640]{0:T(1024)} %param.9) | copy-start | bytes 7684

commit v8 on v7

--- a/solution.py
+++ b/solution.py
@@ -176,8 +176,13 @@
     sizes = column(jnp.concatenate(sizes, axis=0))
     owners = column(jnp.concatenate([tags_ref[s, 0:1, :].astype(F32) for s in range(orbs)], axis=0))
     owner_ref[...] = jnp.broadcast_to(owners[:, 2:3], (count, LANES)).astype(BF)
-    raw_copy.wait()
+    owner = [
+        jnp.broadcast_to(owners[:, s : s + 1], (count, LANES)).astype(BF) for s in range(orbs)
+    ]
+    for cp in (raw_copy, *copies):
+        cp.wait()
     wide_ref[...] = raw_ref[...].astype(F32)
+    mix(w_ref.at[0], hot_ref, block_ref, owner[0][:, 0:1], mix_ref.at[0])
     for o in range(orbs):
         for q in range(quota):
             row = o * count + q * LANES
@@ -187,10 +192,9 @@
                 rows_ref[row : row + LANES, h * LANES : (h + 1) * LANES] = jnp.where(
                     lane + float(h * LANES) < size, piece, 0.0
                 ).astype(BF)
+    mix(w_ref.at[1], hot_ref, block_ref, owner[1][:, 0:1], mix_ref.at[1])
+    mix(w_ref.at[2], hot_ref, block_ref, owner[3][:, 0:1], mix_ref.at[2])
     for i, s in enumerate((0, 1, 3)):
-        copies[i].wait()
-        owner = jnp.broadcast_to(owners[:, s : s + 1], (count, LANES)).astype(BF)
-        mix(w_ref.at[i], hot_ref, block_ref, owner[:, 0:1], mix_ref.at[i])
         scatter(quota, (here + s) % orbs, step, mix_ref[i], rows_ref, flat_ref)
 
 

time: 169 us -> 167 us (0.988)
  Pallas kernels: 21.6 us -> 19.7 us
    pallas_call x1, Pallas kernels: 11.6 us -> 9.61 us  [cycle(): call(functools.partial(cycle_body, quota), (pltpu.VMEM((4 * count, 2 * LA...]
  transfers between devices with their start and end apart: 6 -> 6, of which waited for: 2 -> 2; matrix products, arithmetic and copies ran while one was open for 1% -> 1% of each run, Pallas kernels for 7% -> 6%
where the time goes in v8:
time: 167 us; the launch traced here: 166 us
  blocking collectives  54.8 us (33%)
  waiting for transfers between devices  48.7 us (29%)
  starting transfers between devices  40.8 us (24%)
  Pallas kernels  19.7 us (12%)
  local copies, waits for them, and re-layouts  1.91 us (1%)
    all_to_all x1, blocking collectives, exchange(): x = lax.all_to_all(x, BOTH, split_axis=0, concat_axis=0, tiled=True)  54.8 us
    ppermute x5, waiting for transfers between devices, shift(): return lax.ppermute(x, 'orb', [(i, (i + by) % orbs) for i in range(orbs)])  48.7 us
    all_to_all x1, starting transfers between devices, exchange(): x = lax.all_to_all(x, BOTH, split_axis=0, concat_axis=0, tiled=True)  24 us
    ppermute x5, starting transfers between devices, shift(): return lax.ppermute(x, 'orb', [(i, (i + by) % orbs) for i in range(orbs)])  16.9 us
    pallas_call x1, Pallas kernels, cycle(): call(functools.partial(cycle_body, quota), (pltpu.VMEM((4 * count, 2 * LA...  9.61 us
    pallas_call x1, Pallas kernels, pick(): call(functools.partial(pick_body, quota), pltpu.VMEM((count + TAGS, width...  3.43 us
  transfers between devices with their start and end apart: 6, of which 2 were waited for; matrix products, arithmetic and copies ran while one was open for 1% of the time, Pallas kernels for 6%

profile of v8, /device:TPU:1, one launch (start us, length us, event | category | flops | bytes accessed | tf_op | source)
XLA Modules:
  0.0 166.2 jit_solution(15265470412273297810)
XLA Ops:
  0.0 0.0 copy-start.1
  0.0 0.0 copy-start.2
  0.0 3.4 %pick.1.own_any = bf16[656,1024]{1,0:T(8,128)(2,1)S(1)} custom-call(s32[4,256]{1,0:T(4,128)} %src_any.1, bf16[1024,1024]{1,0:T(8,128)(2,1)} %bitcast.14), custom_call_target="tpu_custom_call" | custom-call | tf_op jit(solution)/shard_map/pick/pallas_call | solution.py:262
  3.4 0.0 copy-start
  3.5 0.0 copy-done.1
  3.5 0.0 copy-done.2
  3.5 1.8 %pack.1 = bf16[5120,128]{1,0:T(8,128)(2,1)} custom-call(bf16[640,1024]{1,0:T(8,128)(2,1)S(1)} %copy-done.1, f32[5,128]{1,0:T(8,128)S(1)} %bitcast.10), custom_call_target="tpu_custom_call" | custom-call | tf_op jit(solution)/shard_map/pack/pallas_call | solution.py:281
  5.2 24.0 %all-to-all-start = ((bf16[512,5,2,128]{3,2,1,0:T(2,128)(2,1)}), bf16[512,5,2,128]{3,2,1,0:T(2,128)(2,1)}, u32[]{:S(2)}, u32[]{:S(2)}) async-start(bf16[512,5,2,128]{3,2,1,0:T(2,128)(2,1)} %bitcast.13), calls=%async_computation | async-start | bytes 2621440 | tf_op jit(solution)/shard_map/all_to_all | solution.py:382
  29.2 0.0 copy-start.4
  29.2 4.5 %collective-permute-start = (bf16[656,1024]{1,0:T(8,128)(2,1)S(1)}, bf16[656,1024]{1,0:T(8,128)(2,1)S(1)}, u32[]{:S(2)}, u32[]{:S(2)}) collective-permute-start(bf16[656,1024]{1,0:T(8,128)(2,1)S(1)} %pick.1.own_any), channel_id=1, source_target_pairs={{0,3},{1,0},{2,1},{3,2},{4,7},{5,4},{6,5},{7,6},{8,11},{9,8},{10,9... | collective-permute-start | bytes 4030472 | tf_op jit(solution)/shard_map/ppermute | solution.py:378
  33.7 1.9 %collective-permute-start.2 = (bf16[656,1024]{1,0:T(8,128)(2,1)S(1)}, bf16[656,1024]{1,0:T(8,128)(2,1)S(1)}, u32[]{:S(2)}, u32[]{:S(2)}) collective-permute-start(bf16[656,1024]{1,0:T(8,128)(2,1)S(1)} %pick.1.own_any), channel_id=1, source_target_pairs={{0,1},{1,2},{2,3},{3,0},{4,5},{5,6},{6,7},{7,4},{8,9},{9,10},{10,1... | collective-permute-start | bytes 4030472 | tf_op jit(solution)/shard_map/ppermute | solution.py:378
  35.6 38.6 %collective-permute-done.after_any = bf16[656,1024]{1,0:T(8,128)(2,1)S(1)} collective-permute-done((bf16[656,1024]{1,0:T(8,128)(2,1)S(1)}, bf16[656,1024]{1,0:T(8,128)(2,1)S(1)}, u32[]{:S(2)}, u32[]{:S(2)}) %collective-permute-start) | collective-permute-done | bytes 1343520 | tf_op jit(solution)/shard_map/ppermute | solution.py:378
  74.3 0.0 copy-start.5
  74.3 1.0 slice.12
  75.3 5.3 %collective-permute-start.1 = (bf16[368,1024]{1,0:T(8,128)(2,1)}, bf16[368,1024]{1,0:T(8,128)(2,1)}, u32[]{:S(2)}, u32[]{:S(2)}) collective-permute-start(bf16[368,1024]{1,0:T(8,128)(2,1)} %slice.12), channel_id=1, source_target_pairs={{0,3},{1,0},{2,1},{3,2},{4,7},{5,4},{6,5},{7,6},{8,11},{9,8},{10,9... | collective-permute-start | bytes 2261000 | tf_op jit(solution)/shard_map/ppermute | solution.py:378
  80.6 0.0 collective-permute-done.2.before_any
  80.6 0.0 copy-start.6
  80.6 0.9 slice.13
  81.5 1.9 %collective-permute-start.3 = (bf16[272,1024]{1,0:T(8,128)(2,1)}, bf16[272,1024]{1,0:T(8,128)(2,1)S(1)}, u32[]{:S(2)}, u32[]{:S(2)}) collective-permute-start(bf16[272,1024]{1,0:T(8,128)(2,1)} %slice.13), channel_id=1, source_target_pairs={{0,1},{1,2},{2,3},{3,0},{4,5},{5,6},{6,7},{7,4},{8,9},{9,10},{10,1... | collective-permute-start | bytes 1671176 | tf_op jit(solution)/shard_map/ppermute | solution.py:378
  83.4 0.0 copy-done
  83.4 0.0 copy-done.5
  83.4 3.3 %collective-permute-start.4 = (bf16[16,1024]{1,0:T(8,128)(2,1)S(1)}, bf16[16,1024]{1,0:T(8,128)(2,1)S(1)}, u32[]{:S(2)}, u32[]{:S(2)}) collective-permute-start(bf16[16,1024]{1,0:T(8,128)(2,1)S(1)} %slice.14), channel_id=1, source_target_pairs={{0,2},{1,3},{2,0},{3,1},{4,6},{5,7},{6,4},{7,5},{8,10},{9,11},{10,... | collective-permute-start | bytes 98312 | tf_op jit(solution)/shard_map/ppermute | solution.py:378
  86.7 0.0 copy-done.6
  86.7 10.0 %collective-permute-done.4.far_ref = bf16[16,1024]{1,0:T(8,128)(2,1)S(1)} collective-permute-done((bf16[16,1024]{1,0:T(8,128)(2,1)S(1)}, bf16[16,1024]{1,0:T(8,128)(2,1)S(1)}, u32[]{:S(2)}, u32[]{:S(2)}) %collective-permute-start.4) | collective-permute-done | bytes 32800 | tf_op jit(solution)/shard_map/ppermute | solution.py:378
  96.8 0.0 all-to-all-done
  96.8 0.0 copy-done.4
  96.8 9.6 %cycle.1 = (bf16[2560,256]{1,0:T(8,128)(2,1)S(1)}, f32[5120,128]{1,0:T(8,128)S(1)}, bf16[4,256,640]{2,1,0:T(8,128)(2,1)S(1)}, bf16[4,16,640]{2,1,0:T(8,128)(2,1)S(1)}, bf16[640,128]{1,0:T(8,128)(2,1)S(1)}) custom-call(s32[1]{0:T(128)} %bitcast.here_ref, s32[4]{0:T(128)S(1)} %copy-done.4, bf16[5120,128]{1,0:T(8,128)(2,1)} %bitcast.4.raw_any, ...), custom_call_target="tpu_custom_call" | custom-call | tf_op jit(solution)/shard_map/cycle/pallas_call | solution.py:300
  106.4 0.0 collective-permute-done.3.hi_ref
  106.4 0.0 collective-permute-done.1.lo_any
  106.4 2.9 %close.1 = (bf16[5120,128]{1,0:T(8,128)(2,1)S(1)}, f32[5120,128]{1,0:T(8,128)S(1)}) custom-call(s32[1]{0:T(128)} %bitcast.here_ref, bf16[368,1024]{1,0:T(8,128)(2,1)} %collective-permute-done.1.lo_any, bf16[272,1024]{1,0:T(8,128)(2,1)S(1)} %collective-permute-done.3.hi_ref, ...), custom_call_target="tpu_custom_call", output_to_operand_aliasing={{1}: (7, {})} | custom-call | tf_op jit(solution)/shard_map/close/pallas_call | solution.py:327
  109.3 0.0 copy-start.3
  109.3 54.8 %all_to_all.10 = bf16[512,5,2,128]{3,2,1,0:T(2,128)(2,1)S(1)} all-to-all(bf16[512,5,2,128]{3,2,1,0:T(2,128)(2,1)S(1)} %bitcast.9), channel_id=1, replica_groups=mesh['chan'=128,'orb'=4] {'chan','orb'}, dimensions={0} | all-to-all | bytes 2621440 | tf_op jit(solution)/shard_map/all_to_all | solution.py:382
  164.1 0.0 copy-done.3
  164.1 2.0 %finish.1 = bf16[640,1024]{1,0:T(8,128)(2,1)} custom-call(bf16[5120,128]{1,0:T(8,128)(2,1)S(1)} %bitcast.8, bf16[640,1024]{1,0:T(8,128)(2,1)S(1)} %copy-done.1, f32[5,128]{1,0:T(8,128)S(1)} %bitcast.11, f32[5,128]{1,0:T(8,128)S(1)} %bitcast.12), custom_call_target="tpu_custom_call" | custom-call | tf_op jit(solution)/shard_map/finish/pallas_call | solution.py:346
  (1 shorter events, 0.0 us)
Async XLA Ops:
  0.0 3.5 %copy-start.1 = (bf16[640,1024]{1,0:T(8,128)(2,1)S(1)}, bf16[640,1024]{1,0:T(8,128)(2,1)}, u32[]{:S(2)}) copy-start(bf16[640,1024]{1,0:T(8,128)(2,1)} %amp_ref.3) | copy-start | bytes 3932164
  0.0 3.5 %copy-start.2 = (f32[640]{0:T(1024)S(1)}, f32[640]{0:T(1024)}, u32[]{:S(2)}) copy-start(f32[640]{0:T(1024)} %param.8) | copy-start | bytes 7684
  3.4 80.0 %copy-start = (bf16[656,1024]{1,0:T(8,128)(2,1)}, bf16[656,1024]{1,0:T(8,128)(2,1)S(1)}, u32[]{:S(2)}) copy-start(bf16[656,1024]{1,0:T(8,128)(2,1)S(1)} %pick.1.own_any) | copy-start | bytes 4030468
  5.2 91.5 %all-to-all-start = ((bf16[512,5,2,128]{3,2,1,0:T(2,128)(2,1)}), bf16[512,5,2,128]{3,2,1,0:T(2,128)(2,1)}, u32[]{:S(2)}, u32[]{:S(2)}) async-start(bf16[512,5,2,128]{3,2,1,0:T(2,128)(2,1)} %bitcast.13), calls=%async_computation | async-start | bytes 2621440 | tf_op jit(solution)/shard_map/all_to_all | solution.py:382
  29.2 67.5 %copy-start.4 = (s32[4]{0:T(128)S(1)}, s32[4]{0:T(128)}, u32[]{:S(2)}) copy-start(s32[4]{0:T(128)} %size_ref.1) | copy-start | bytes 52
  29.2 45.0 %collective-permute-start = (bf16[656,1024]{1,0:T(8,128)(2,1)S(1)}, bf16[656,1024]{1,0:T(8,128)(2,1)S(1)}, u32[]{:S(2)}, u32[]{:S(2)}) collective-permute-start(bf16[656,1024]{1,0:T(8,128)(2,1)S(1)} %pick.1.own_any), channel_id=1, source_target_pairs={{0,3},{1,0},{2,1},{3,2},{4,7},{5,4},{6,5},{7,6},{8,11},{9,8},{10,9... | collective-permute-start | bytes 4030472 | tf_op jit(solution)/shard_map/ppermute | solution.py:378
  33.7 46.9 %collective-permute-start.2 = (bf16[656,1024]{1,0:T(8,128)(2,1)S(1)}, bf16[656,1024]{1,0:T(8,128)(2,1)S(1)}, u32[]{:S(2)}, u32[]{:S(2)}) collective-permute-start(bf16[656,1024]{1,0:T(8,128)(2,1)S(1)} %pick.1.own_any), channel_id=1, source_target_pairs={{0,1},{1,2},{2,3},{3,0},{4,5},{5,6},{6,7},{7,4},{8,9},{9,10},{10,1... | collective-permute-start | bytes 4030472 | tf_op jit(solution)/shard_map/ppermute | solution.py:378
  74.3 9.2 %copy-start.5 = (bf16[656,1024]{1,0:T(8,128)(2,1)}, bf16[656,1024]{1,0:T(8,128)(2,1)S(1)}, u32[]{:S(2)}) copy-start(bf16[656,1024]{1,0:T(8,128)(2,1)S(1)} %collective-permute-done.after_any) | copy-start | bytes 4030468
  75.3 31.1 %collective-permute-start.1 = (bf16[368,1024]{1,0:T(8,128)(2,1)}, bf16[368,1024]{1,0:T(8,128)(2,1)}, u32[]{:S(2)}, u32[]{:S(2)}) collective-permute-start(bf16[368,1024]{1,0:T(8,128)(2,1)} %slice.12), channel_id=1, source_target_pairs={{0,3},{1,0},{2,1},{3,2},{4,7},{5,4},{6,5},{7,6},{8,11},{9,8},{10,9... | collective-permute-start | bytes 2261000 | tf_op jit(solution)/shard_map/ppermute | solution.py:378
  80.6 6.1 %copy-start.6 = (bf16[656,1024]{1,0:T(8,128)(2,1)}, bf16[656,1024]{1,0:T(8,128)(2,1)S(1)}, u32[]{:S(2)}) copy-start(bf16[656,1024]{1,0:T(8,128)(2,1)S(1)} %collective-permute-done.2.before_any) | copy-start | bytes 4030468
  81.5 24.9 %collective-permute-start.3 = (bf16[272,1024]{1,0:T(8,128)(2,1)}, bf16[272,1024]{1,0:T(8,128)(2,1)S(1)}, u32[]{:S(2)}, u32[]{:S(2)}) collective-permute-start(bf16[272,1024]{1,0:T(8,128)(2,1)} %slice.13), channel_id=1, source_target_pairs={{0,1},{1,2},{2,3},{3,0},{4,5},{5,6},{6,7},{7,4},{8,9},{9,10},{10,1... | collective-permute-start | bytes 1671176 | tf_op jit(solution)/shard_map/ppermute | solution.py:378
  83.4 13.3 %collective-permute-start.4 = (bf16[16,1024]{1,0:T(8,128)(2,1)S(1)}, bf16[16,1024]{1,0:T(8,128)(2,1)S(1)}, u32[]{:S(2)}, u32[]{:S(2)}) collective-permute-start(bf16[16,1024]{1,0:T(8,128)(2,1)S(1)} %slice.14), channel_id=1, source_target_pairs={{0,2},{1,3},{2,0},{3,1},{4,6},{5,7},{6,4},{7,5},{8,10},{9,11},{10,... | collective-permute-start | bytes 98312 | tf_op jit(solution)/shard_map/ppermute | solution.py:378
  109.3 54.8 %copy-start.3 = (f32[640]{0:T(1024)S(1)}, f32[640]{0:T(1024)}, u32[]{:S(2)}) copy-start(f32[640]{0:T(1024)} %param.9) | copy-start | bytes 7684
